TPU v7x, 32 devices: a whole 2x2x4 slice. The times are simulated.
32 devices in a mesh: groups: 2 (over y), ctx: 4 (over z), dp: 4 (over x, core).
Axes of the slice: x: 2, y: 2, z: 4, core: 2. Of those that a mesh axis runs over, the one named last changes fastest.
Arguments:
- queries: bfloat16 [8, 512, 2048], P(('groups', 'dp'), 'ctx'), parts along dimension 0, may hold values from -10 to 10
- keys: bfloat16 [8, 512, 2048], P(('groups', 'dp'), 'ctx'), parts along dimension 0, may hold values from -10 to 10
- values: bfloat16 [8, 512, 2048], P(('groups', 'dp'), 'ctx'), parts along dimension 0, may hold values from -6 to 6
- grad_out: bfloat16 [8, 512, 2048], P(('groups', 'dp'), 'ctx'), parts along dimension 0, may hold values from -6 to 6
- rand_blocks: int32 [8, 8, 3], P(('groups', 'dp')), parts along dimension 0, may hold values from 0 to 7, as said below
- glob_blocks: int32 [8, 2], P(('groups', 'dp')), parts along dimension 0, may hold values from 0 to 7, as said below
Outputs:
- attn_out: bfloat16 [8, 512, 2048], P(('groups', 'dp'), 'ctx'), parts along dimension 0
- grad_queries: bfloat16 [8, 512, 2048], P(('groups', 'dp'), 'ctx'), parts along dimension 0
- grad_keys: bfloat16 [8, 512, 2048], P(('groups', 'dp'), 'ctx'), parts along dimension 0
- grad_values: bfloat16 [8, 512, 2048], P(('groups', 'dp'), 'ctx'), parts along dimension 0
There are 2 independent parts, one for each index of `groups`. A program takes and returns all parts, laid end to end along the dimension named above; each array names one. Nothing has to cross between parts.
Inputs may be any that keep to these rules, and one draw needn't show every extreme that they name: `rand_blocks`: block b lies on index b // 2 of ctx. The 3 random blocks of one query block lie on 3 different indices of ctx, none on the index that holds the query block. The query blocks of one index of ctx name at most 2 random blocks on any one other index, and exactly 2 on some index. `glob_blocks`: the 2 global blocks of a sequence are distinct.
All inputs are finite; a program needn't handle non-finite values.
Results may differ from a plain program's by a relative error of at most 0.013.
Values may be sent and summed in bfloat16 or wider, within the bound.
No kernel may reach another device: no remote copies, remote signals or barrier semaphores. Data moves between devices by JAX's collectives and lax.ppermute only.
A program may use at most 128 MiB of HBM per device.

v0:
```python
import jax
import jax.numpy as jnp
from jax import lax
from jax.sharding import PartitionSpec as P

HEADS = 16
BLOCK = 64


def extended_2(shard, sides, width):
    for axis, dim in sides:
        devices, length = (lax.axis_size(axis), shard.shape[dim])
        up = [(i, (i + 1) % devices) for i in range(devices)]
        down = [(j, i) for i, j in up]
        last = lax.slice_in_dim(shard, length - width, length, axis=dim)
        first = lax.slice_in_dim(shard, 0, width, axis=dim)
        before = lax.ppermute(last, axis, up)
        after = lax.ppermute(first, axis, down)
        shard = jnp.concatenate([before, shard, after], axis=dim)
    return shard


def broadcast(shard, axis, root):
    mine = lax.axis_index(axis) == root
    return lax.psum(jnp.where(mine, shard, jnp.zeros_like(shard)), axis)


def slot_layout(rand_all, ctx_size, local_blocks):
    slot_count = local_blocks * rand_all.shape[1]
    wanted = rand_all.reshape(ctx_size, slot_count)
    holders = wanted // local_blocks
    local_rows = wanted % local_blocks
    earlier = jnp.arange(slot_count)[:, None] > jnp.arange(slot_count)[None, :]
    same_holder = holders[:, :, None] == holders[:, None, :]
    slot_rank = jnp.sum(same_holder & earlier[None], axis=2)
    return (holders, local_rows, slot_rank)


def local(queries, keys, values, grad_out, rand_blocks, glob_blocks):
    ctx_size = lax.axis_size("ctx")
    device = lax.axis_index("ctx")
    tokens = queries.shape[1]
    feature_width = queries.shape[2]
    block_len = BLOCK
    head_count = HEADS
    head_dim = feature_width // head_count
    score_scale = head_dim ** (-0.5)
    local_blocks = tokens // block_len
    total_blocks = local_blocks * ctx_size
    rand_all = rand_blocks[0]
    global_ids = glob_blocks[0]
    rand_count = rand_all.shape[1]
    glob_count = global_ids.shape[0]
    slot_count = local_blocks * rand_count
    capacity = (slot_count + ctx_size - 2) // (ctx_size - 1)
    glob_len = glob_count * block_len
    win_len = 3 * block_len
    key_val = jnp.stack([keys[0], values[0]])
    own_kv = key_val.reshape(2, local_blocks, block_len, feature_width)
    extended = extended_2(key_val, (("ctx", 1),), block_len)
    ext_kv = extended.reshape(2, local_blocks + 2, block_len, feature_width)
    window_kv = jnp.concatenate(
        [
            ext_kv[:, 0:local_blocks],
            ext_kv[:, 1 : local_blocks + 1],
            ext_kv[:, 2 : local_blocks + 2],
        ],
        axis=2,
    )
    pieces = []
    for glob_slot in range(glob_count):
        root_device = global_ids[glob_slot] // local_blocks
        own_piece = lax.dynamic_index_in_dim(
            own_kv, global_ids[glob_slot] % local_blocks, 1, keepdims=False
        )
        pieces.append(broadcast(own_piece, "ctx", root_device))
    global_kv = jnp.concatenate(pieces, axis=1)
    holders, local_rows, slot_rank = slot_layout(rand_all, ctx_size, local_blocks)
    matched = (holders == device)[:, :, None] & (
        slot_rank[:, :, None] == jnp.arange(capacity)[None, None, :]
    )
    occupied = jnp.any(matched, axis=1).reshape(-1)
    source_row = jnp.sum(jnp.where(matched, local_rows[:, :, None], 0), axis=1).reshape(-1)
    outgoing = jnp.take(own_kv, source_row, axis=1)
    outgoing = jnp.where(occupied[None, :, None, None], outgoing, jnp.zeros_like(outgoing))
    arrived = lax.all_to_all(outgoing, "ctx", split_axis=1, concat_axis=1, tiled=True)
    my_holder = lax.dynamic_index_in_dim(holders, device, 0, keepdims=False)
    my_rank = lax.dynamic_index_in_dim(slot_rank, device, 0, keepdims=False)
    slot_target = my_holder * capacity + my_rank
    fetched = jnp.take(arrived, slot_target, axis=1)
    random_kv = fetched.reshape(2, local_blocks, rand_count * block_len, feature_width)
    first_block = device * local_blocks
    rows_here = first_block + jnp.arange(local_blocks, dtype=jnp.int32)
    window_ids = jnp.stack(
        [(rows_here - 1) % total_blocks, rows_here, (rows_here + 1) % total_blocks], axis=1
    )
    my_rand = lax.dynamic_slice_in_dim(rand_all, first_block, local_blocks, 0)
    window_ok = ~jnp.any(window_ids[:, :, None] == global_ids[None, None, :], axis=2)
    rand_ok = ~(
        jnp.any(my_rand[:, :, None] == global_ids[None, None, :], axis=2)
        | jnp.any(my_rand[:, :, None] == window_ids[:, None, :], axis=2)
    )
    block_ok = jnp.concatenate(
        [jnp.ones((local_blocks, glob_count), dtype=bool), window_ok, rand_ok], axis=1
    )
    valid = jnp.repeat(block_ok, block_len, axis=1)
    query4 = queries[0].reshape(local_blocks, block_len, head_count, head_dim)
    dout4 = grad_out[0].reshape(local_blocks, block_len, head_count, head_dim)
    glob_k = global_kv[0].reshape(glob_len, head_count, head_dim)
    glob_v = global_kv[1].reshape(glob_len, head_count, head_dim)
    win_k = window_kv[0].reshape(local_blocks, win_len, head_count, head_dim)
    win_v = window_kv[1].reshape(local_blocks, win_len, head_count, head_dim)
    rnd_k = random_kv[0].reshape(local_blocks, rand_count * block_len, head_count, head_dim)
    rnd_v = random_kv[1].reshape(local_blocks, rand_count * block_len, head_count, head_dim)
    f32 = jnp.float32
    scores = (
        jnp.concatenate(
            [
                jnp.einsum("aqhd,khd->ahqk", query4, glob_k, preferred_element_type=f32),
                jnp.einsum("aqhd,akhd->ahqk", query4, win_k, preferred_element_type=f32),
                jnp.einsum("aqhd,akhd->ahqk", query4, rnd_k, preferred_element_type=f32),
            ],
            axis=3,
        )
        * score_scale
    )
    scores = jnp.where(valid[:, None, None, :], scores, -jnp.inf)
    top = jnp.max(scores, axis=3, keepdims=True)
    expo = jnp.exp(scores - top)
    prob = expo / jnp.sum(expo, axis=3, keepdims=True)
    prob_b = prob.astype(jnp.bfloat16)
    prob_glob = prob_b[..., :glob_len]
    prob_win = prob_b[..., glob_len : glob_len + win_len]
    prob_rnd = prob_b[..., glob_len + win_len :]
    attended = (
        jnp.einsum("ahqk,khd->aqhd", prob_glob, glob_v, preferred_element_type=f32)
        + jnp.einsum("ahqk,akhd->aqhd", prob_win, win_v, preferred_element_type=f32)
        + jnp.einsum("ahqk,akhd->aqhd", prob_rnd, rnd_v, preferred_element_type=f32)
    )
    out4 = attended.astype(jnp.bfloat16)
    delta = jnp.sum(dout4.astype(f32) * out4.astype(f32), axis=3)
    dprob = jnp.concatenate(
        [
            jnp.einsum("aqhd,khd->ahqk", dout4, glob_v, preferred_element_type=f32),
            jnp.einsum("aqhd,akhd->ahqk", dout4, win_v, preferred_element_type=f32),
            jnp.einsum("aqhd,akhd->ahqk", dout4, rnd_v, preferred_element_type=f32),
        ],
        axis=3,
    )
    dscore = prob * (dprob - jnp.transpose(delta, (0, 2, 1))[..., None])
    dscore_b = dscore.astype(jnp.bfloat16)
    ds_glob = dscore_b[..., :glob_len]
    ds_win = dscore_b[..., glob_len : glob_len + win_len]
    ds_rnd = dscore_b[..., glob_len + win_len :]
    dquery = (
        jnp.einsum("ahqk,khd->aqhd", ds_glob, glob_k, preferred_element_type=f32)
        + jnp.einsum("ahqk,akhd->aqhd", ds_win, win_k, preferred_element_type=f32)
        + jnp.einsum("ahqk,akhd->aqhd", ds_rnd, rnd_k, preferred_element_type=f32)
    ) * score_scale
    glob_dk = (
        jnp.einsum("ahqk,aqhd->khd", ds_glob, query4, preferred_element_type=f32) * score_scale
    )
    glob_dv = jnp.einsum("ahqk,aqhd->khd", prob_glob, dout4, preferred_element_type=f32)
    glob_dk, glob_dv = lax.psum((glob_dk, glob_dv), "ctx")
    glob_grad = jnp.stack(
        [
            glob_dk.reshape(glob_count, block_len, feature_width),
            glob_dv.reshape(glob_count, block_len, feature_width),
        ]
    )
    glob_here = global_ids // local_blocks == device
    glob_row = global_ids % local_blocks
    glob_grad = jnp.where(glob_here[None, :, None, None], glob_grad, jnp.zeros_like(glob_grad))
    win_dk = jnp.einsum("ahqk,aqhd->akhd", ds_win, query4, preferred_element_type=f32) * score_scale
    win_dv = jnp.einsum("ahqk,aqhd->akhd", prob_win, dout4, preferred_element_type=f32)
    win_grad = jnp.stack([win_dk, win_dv]).reshape(2, local_blocks, 3, block_len, feature_width)
    ext_grad = (
        jnp.pad(win_grad[:, :, 0], ((0, 0), (0, 2), (0, 0), (0, 0)))
        + jnp.pad(win_grad[:, :, 1], ((0, 0), (1, 1), (0, 0), (0, 0)))
        + jnp.pad(win_grad[:, :, 2], ((0, 0), (2, 0), (0, 0), (0, 0)))
    )
    edges = jnp.concatenate([ext_grad[:, 0], ext_grad[:, local_blocks + 1]], axis=1)
    returned = extended_2(edges, (("ctx", 1),), block_len)
    local_grad = ext_grad[:, 1 : local_blocks + 1]
    local_grad = local_grad.at[:, glob_row].add(glob_grad)
    local_grad = local_grad.at[:, 0].add(returned[:, 0:block_len])
    local_grad = local_grad.at[:, local_blocks - 1].add(returned[:, 3 * block_len : 4 * block_len])
    rnd_dk = jnp.einsum("ahqk,aqhd->akhd", ds_rnd, query4, preferred_element_type=f32) * score_scale
    rnd_dv = jnp.einsum("ahqk,aqhd->akhd", prob_rnd, dout4, preferred_element_type=f32)
    slot_grad = jnp.stack(
        [
            rnd_dk.reshape(slot_count, block_len, feature_width),
            rnd_dv.reshape(slot_count, block_len, feature_width),
        ]
    )
    send_grad = (
        jnp.zeros((2, ctx_size * capacity, block_len, feature_width), f32)
        .at[:, slot_target]
        .set(slot_grad)
    )
    taken = lax.all_to_all(send_grad, "ctx", split_axis=1, concat_axis=1, tiled=True)
    contrib = taken
    contrib = jnp.where(occupied[None, :, None, None], contrib, jnp.zeros_like(contrib))
    local_grad = local_grad.at[:, source_row].add(contrib)
    attn_out = out4.reshape(1, tokens, feature_width)
    grad_queries = dquery.astype(jnp.bfloat16).reshape(1, tokens, feature_width)
    grad_keys = local_grad[0].astype(jnp.bfloat16).reshape(1, tokens, feature_width)
    grad_values = local_grad[1].astype(jnp.bfloat16).reshape(1, tokens, feature_width)
    return (attn_out, grad_queries, grad_keys, grad_values)


def solution(mesh):
    placed = (
        P(("groups", "dp"), "ctx", None),
        P(("groups", "dp"), "ctx", None),
        P(("groups", "dp"), "ctx", None),
        P(("groups", "dp"), "ctx", None),
        P(("groups", "dp"), None, None),
        P(("groups", "dp"), None),
    )
    return jax.shard_map(
        local,
        mesh=mesh,
        in_specs=placed,
        out_specs=(
            P(("groups", "dp"), "ctx", None),
            P(("groups", "dp"), "ctx", None),
            P(("groups", "dp"), "ctx", None),
            P(("groups", "dp"), "ctx", None),
        ),
        check_vma=False,
    )
```

profile of v0, /device:TPU:18, one launch (start us, length us, event | category | flops | bytes accessed | tf_op | source)
XLA Modules:
  0.0 596.5 jit_solution(12596927315824288741)
XLA Ops:
  11.8 2.8 gather_fusion
  14.5 4.7 select_bitcast_fusion.1
  19.2 5.2 all-to-all-start
  25.3 1.5 collective-permute-start
  37.3 134.8 %collective-permute-done = bf16[2,64,2048]{2,1,0:T(8,128)(2,1)} collective-permute-done((bf16[2,64,2048]{2,1,0:T(8,128)(2,1)}, bf16[2,64,2048]{2,1,0:T(8,128)(2,1)}, u32[]{:S(2)}, u32[]{:S(2)}) %collective-permute-start) | collective-permute-done | bytes 524320 | tf_op jit(solution)/shard_map/ppermute | solution.py:17
  172.1 1.4 pad_maximum_fusion.1
  176.0 2.5 convolution_bitcast_fusion.5
  178.5 2.5 convolution_bitcast_fusion.3
  184.1 2.3 fusion.94
  186.4 4.7 gather_fusion.1
  191.1 2.3 select_bitcast_fusion.2
  196.5 10.7 %fusion.93 = (f32[2,16,64]{2,1,0:T(8,128)S(1)}, f32[2,16,64,512]{3,2,1,0:T(8,128)S(1)}) fusion(f32[2,16,64,192]{3,2,1,0:T(8,128)S(1)} %convolution_bitcast_fusion.4, f32[2,16,64,192]{3,2,1,0:T(8,128)S(1)} %copy-done.14, pred[2,512]{1,0:T(4,128)(4,1)S(1)} %broadcast_in_dim.100, f32[2,16,64,128]{3,2,0,1:T(8,128)S(1)} %bitcast.232), kind=kOutput, calls=%fused_computation.172 | output fusion | flops 6291967 | bytes 8397824 | tf_op jit(solution)/shard_map/sub | solution.py:129
  208.2 2.9 convolution_bitcast_fusion
  214.8 1.3 multiply_reduce_fusion
  216.6 2.3 fusion.3
  218.9 1.3 multiply_bitcast_fusion
  220.2 3.5 copy.343
  223.7 4.6 stack_reshape.14
  228.3 5.4 copy.345
  233.7 4.5 stack_reshape.15
  238.3 3.3 maximum_bitcast_fusion
  241.5 3.1 copy.347
  244.7 4.3 broadcast.496.clone
  248.9 11.5 %scatter_fusion.1 = f32[2,8,64,2048]{3,2,1,0:T(8,128)} fusion(f32[2,8,64,2048]{3,2,1,0:T(8,128)} %broadcast.496.clone, s32[6]{0:T(128)S(1)} %fusion.72, f32[6,2,64,2048]{3,2,1,0:T(8,128)} %copy.347), kind=kCustom, calls=%fused_computation.3 | custom fusion | bytes 18874392 | tf_op jit(solution)/shard_map/scatter | solution.py:199
  260.5 7.7 %copy.348 = f32[2,8,64,2048]{3,2,0,1:T(8,128)} copy(f32[2,8,64,2048]{3,2,1,0:T(8,128)} %scatter_fusion.1) | data formatting | bytes 16777216 | tf_op jit(solution)/shard_map/scatter | solution.py:199
  268.2 5.6 all-to-all-start.1
  274.1 1.4 convolution_bitcast_fusion.6
  276.1 1.1 stack_reshape.13
  277.3 1.4 fusion.38
  280.4 1.9 multiply_bitcast_fusion.1
  282.3 3.5 copy.329
  285.8 4.5 stack.26
  290.3 1.9 convolution_bitcast_fusion.1
  292.2 3.5 copy.331
  295.7 4.8 stack.27
  300.7 1.7 copy-done.10
  304.1 1.5 add_bitcast_fusion
  305.5 1.5 collective-permute-start.3
  309.2 2.4 pad_add_fusion
  316.2 1.6 slice-done
  318.0 219.6 %all-reduce.8.cloned.1.call-done = (f32[1,2,64,2048]{3,2,1,0:T(8,128)}, f32[1,2,64,2048]{3,2,1,0:T(8,128)}) async-done(((f32[1,2,64,2048]{3,2,1,0:T(8,128)}, f32[1,2,64,2048]{3,2,1,0:T(8,128)}), (f32[1,2,64,2048]{3,2,1,0:T(8,128)}, f32[1,2,64,2048]{3,2,1,0:T(8,128)})) %all-reduce.8.cloned.1.call-update) | async-done | bytes 2097168 | tf_op jit(solution)/shard_map/psum | solution.py:164
  537.6 1.8 fusion.4
  539.5 1.5 copy.339
  540.9 2.9 scatter_fusion
  543.9 24.3 %collective-permute-done.2 = f32[2,64,2048]{2,1,0:T(8,128)} collective-permute-done((f32[2,64,2048]{2,1,0:T(8,128)}, f32[2,64,2048]{2,1,0:T(8,128)}, u32[]{:S(2)}, u32[]{:S(2)}) %collective-permute-start.2) | collective-permute-done | bytes 1048608 | tf_op jit(solution)/shard_map/ppermute | solution.py:17
  568.2 1.5 fusion.44
  570.0 8.4 %select_bitcast_fusion = f32[8,2,64,2048]{3,2,1,0:T(8,128)} fusion(f32[2,8,64,2048]{3,2,0,1:T(8,128)} %all-to-all-done.1, pred[8]{0:T(512)(128)(4,1)S(1)} %broadcast_in_dim.103), kind=kLoop, calls=%fused_computation.6 | loop fusion | flops 2097152 | bytes 16777224 | tf_op jit(solution)/shard_map/jit(_where)/select_n | solution.py:203
  578.3 9.9 %scatter_fusion.2 = f32[2,2,64,2048]{3,2,1,0:T(8,128)S(1)} fusion(f32[2,2,64,2048]{3,2,1,0:T(8,128)S(1)} %fusion.41, s32[8]{0:T(128)S(1)} %fusion.71, f32[8,2,64,2048]{3,2,1,0:T(8,128)} %select_bitcast_fusion), kind=kCustom, calls=%fused_computation.4 | custom fusion | flops 2097152 | bytes 25165856 | tf_op jit(solution)/shard_map/scatter-add | solution.py:204
  (146 shorter events, 37.2 us)
Async XLA Ops:
  19.2 167.2 %all-to-all-start = ((bf16[2,8,64,2048]{3,2,0,1:T(8,128)(2,1)}), bf16[2,8,64,2048]{3,2,0,1:T(8,128)(2,1)}, u32[]{:S(2)}, u32[]{:S(2)}) async-start(bf16[2,8,64,2048]{3,2,0,1:T(8,128)(2,1)} %select_bitcast_fusion.1), calls=%async_computation | async-start | bytes 8388608 | tf_op jit(solution)/shard_map/all_to_all | solution.py:86
  24.4 2.9 copy-start.20
  24.4 156.5 %all-reduce.10.cloned.1.call-start = ((), (), s32[]{:S(2)}) async-start(), calls=%async_computation.3 | async-start | bytes 2097152 | tf_op jit(solution)/shard_map/psum | solution.py:25
  25.3 9.7 %copy-start.19 = (s32[1,8,3]{1,0,2:T(1,128)S(1)}, s32[1,8,3]{1,0,2:T(1,128)}, u32[]{:S(2)}) copy-start(s32[1,8,3]{1,0,2:T(1,128)} %param.14) | copy-start | bytes 292
  25.3 10.6 %copy-start.17 = (bf16[1,128,2048]{2,1,0:T(8,128)(2,1)S(1)}, bf16[1,128,2048]{2,1,0:T(8,128)(2,1)}, u32[]{:S(2)}) copy-start(bf16[1,128,2048]{2,1,0:T(8,128)(2,1)} %param.10) | copy-start | bytes 1572868
  25.3 146.8 %collective-permute-start = (bf16[2,64,2048]{2,1,0:T(8,128)(2,1)}, bf16[2,64,2048]{2,1,0:T(8,128)(2,1)}, u32[]{:S(2)}, u32[]{:S(2)}) collective-permute-start(bf16[2,64,2048]{2,1,0:T(8,128)(2,1)} %get-tuple-element.56), channel_id=1, source_target_pairs={{0,4},{4,8},{8,12},{12,0},{1,5},{5,9},{9,13},{13,1},{2,6},{6,10},{... | collective-permute-start | bytes 1572872 | tf_op jit(solution)/shard_map/ppermute | solution.py:17
  26.8 145.3 %collective-permute-start.1 = (bf16[2,64,2048]{2,1,0:T(8,128)(2,1)S(1)}, bf16[2,64,2048]{2,1,0:T(8,128)(2,1)}, u32[]{:S(2)}, u32[]{:S(2)}) collective-permute-start(bf16[2,64,2048]{2,1,0:T(8,128)(2,1)S(1)} %get-tuple-element.57), channel_id=1, source_target_pairs={{4,0},{8,4},{12,8},{0,12},{5,1},{9,5},{13,9},{1,13},{6,2},{10,6},{... | collective-permute-start | bytes 1572872 | tf_op jit(solution)/shard_map/ppermute | solution.py:18
  34.0 3.0 copy-start.18
  175.6 2.9 copy-start.7
  176.0 2.5 copy-start.3
  183.8 2.6 copy-start.12
  194.1 1.2 copy-start.5
  194.1 2.2 copy-start.14
  194.1 2.4 copy-start.16
  207.6 7.2 %copy-start.2 = (bf16[2,16,64,512]{3,2,1,0:T(8,128)(2,1)}, bf16[2,16,64,512]{3,2,1,0:T(8,128)(2,1)S(1)}, u32[]{:S(2)}) copy-start(bf16[2,16,64,512]{3,2,1,0:T(8,128)(2,1)S(1)} %fusion.7) | copy-start | bytes 6291460
  212.6 1.4 copy-start.8
  214.8 1.8 copy-start.11
  218.9 1.3 copy-start
  268.2 301.8 %all-to-all-start.1 = ((f32[2,8,64,2048]{3,2,0,1:T(8,128)}), f32[2,8,64,2048]{3,2,0,1:T(8,128)}, u32[]{:S(2)}, u32[]{:S(2)}) async-start(f32[2,8,64,2048]{3,2,0,1:T(8,128)} %copy.348), calls=%async_computation.1 | async-start | bytes 16777216 | tf_op jit(solution)/shard_map/all_to_all | solution.py:201
  273.8 263.8 %all-reduce.8.cloned.1.call-start = ((), (), s32[]{:S(2)}) async-start(), calls=%async_computation.2 | async-start | bytes 4194304 | tf_op jit(solution)/shard_map/psum | solution.py:164
  295.7 4.8 copy-start.9
  300.5 1.9 copy-start.10
  304.1 3.7 copy-start.1
  305.5 264.1 %collective-permute-start.3 = (f32[2,64,2048]{2,1,0:T(8,128)}, f32[2,64,2048]{2,1,0:T(8,128)S(1)}, u32[]{:S(2)}, u32[]{:S(2)}) collective-permute-start(f32[2,64,2048]{2,1,0:T(8,128)} %get-tuple-element.36), channel_id=1, source_target_pairs={{4,0},{8,4},{12,8},{0,12},{5,1},{9,5},{13,9},{1,13},{6,2},{10,6},{... | collective-permute-start | bytes 3145736 | tf_op jit(solution)/shard_map/ppermute | solution.py:18
  307.0 1.4 copy-start.6
  307.0 261.2 %collective-permute-start.2 = (f32[2,64,2048]{2,1,0:T(8,128)}, f32[2,64,2048]{2,1,0:T(8,128)}, u32[]{:S(2)}, u32[]{:S(2)}) collective-permute-start(f32[2,64,2048]{2,1,0:T(8,128)} %get-tuple-element.37), channel_id=1, source_target_pairs={{0,4},{4,8},{8,12},{12,0},{1,5},{5,9},{9,13},{13,1},{2,6},{6,10},{... | collective-permute-start | bytes 3145736 | tf_op jit(solution)/shard_map/ppermute | solution.py:17
  309.2 2.4 copy-start.4
  311.6 1.0 copy-start.13
  312.4 1.1 copy-start.15
  316.2 1.6 slice-start
Sparse Core Ops, SparseCore 0:
  35.0 121.3 all-reduce.9
  300.6 236.9 all-reduce.7
where the time goes:
time: 601 us; the launch traced here: 597 us
  waiting for transfers between devices  379 us (63%)
  local copies, waits for them, and re-layouts  99.3 us (17%)
  other arithmetic  57.5 us (10%)
  matrix products  25.4 us (4%)
  between operations  20.2 us (3%)
  starting transfers between devices  15.4 us (3%)
    psum x1, waiting for transfers between devices, local(): glob_dk, glob_dv = lax.psum((glob_dk, glob_dv), 'ctx')  220 us
    ppermute x2, waiting for transfers between devices, extended_2(): before = lax.ppermute(last, axis, up)  159 us
    scatter x2, local copies, waits for them, and re-layouts, local(): send_grad = jnp.zeros((2, ctx_size * capacity, block_len, feature_width),...  19.2 us
    another operation x3, local copies, waits for them, and re-layouts, local(): jnp.stack([rnd_dk.reshape(slot_count, block_len, feature_width), rnd_dv.r...  12.2 us
  transfers between devices with their start and end apart: 8, of which 3 were waited for; matrix products, arithmetic and copies ran while one was open for 11% of the time, Pallas kernels for 0%

commit v1 on v0

v1 whole, which is shorter than its diff:
```python
import functools

import jax
import jax.numpy as jnp
from jax import lax
from jax.experimental import pallas as pl
from jax.experimental.pallas import tpu as pltpu
from jax.sharding import PartitionSpec as P

HEADS = 16
BLOCK = 64
QUERY_TILE = 512
ANY = pl.BlockSpec(memory_space=pl.ANY)


def pack_kernel(me_ref, *refs, ranks, width):
    arrays, outs, sems = refs[:4], refs[4 : 4 + ranks - 1], refs[-1]
    copies = []
    for shift in range(1, ranks):
        start = pl.multiple_of(lax.rem(me_ref[0] + shift, ranks) * width, 128)
        for i, array in enumerate(arrays):
            copies.append(
                pltpu.make_async_copy(
                    array.at[:, pl.ds(start, width)],
                    outs[shift - 1].at[i],
                    sems.at[shift - 1, i],
                )
            )
    for copy in copies:
        copy.start()
    for copy in copies:
        copy.wait()


def unpack_kernel(me_ref, *refs, ranks, width):
    pieces, outs, sems = refs[4 : 4 + ranks - 1], refs[4 + ranks - 1 : -1], refs[-1]
    copies = []
    for shift in range(1, ranks):
        start = pl.multiple_of(lax.rem(me_ref[0] + shift, ranks) * width, 128)
        for i, out in enumerate(outs):
            copies.append(
                pltpu.make_async_copy(
                    pieces[shift - 1].at[i],
                    out.at[:, pl.ds(start, width)],
                    sems.at[shift - 1, i],
                )
            )
    for copy in copies:
        copy.start()
    for copy in copies:
        copy.wait()


def attention_kernel(me_ref, bias_ref, *refs, ranks, tokens, scale):
    own, got = refs[:4], refs[4 : 4 + ranks - 1]
    own_outs, sent = refs[3 + ranks : 7 + ranks], refs[7 + ranks :]
    f32, bf16 = jnp.float32, jnp.bfloat16
    length = ranks * tokens
    tile = min(QUERY_TILE, length)

    def whole(i):
        return jnp.concatenate([own[i][...]] + [piece[i] for piece in got], axis=0)

    def dot(a, b):
        return jnp.dot(a, b, preferred_element_type=f32)

    def give(i, first, value):
        for r in range(value.shape[0] // tokens):
            rank, part = first // tokens + r, value[r * tokens : (r + 1) * tokens]
            if rank == 0:
                own_outs[i][...] = part
            else:
                sent[rank - 1][i] = part

    query, key, val, dout = (whole(i) for i in range(4))
    key_t, val_t = key.T, val.T
    dkey = dval = None
    for first in range(0, length, tile):
        q = query[first : first + tile]
        g = dout[first : first + tile]
        g_t = g.T
        scores = dot(key, q.T).reshape(-1, BLOCK, tile)
        bias = bias_ref[:, first : first + tile]
        scores = (scores + bias[:, None, :]).reshape(length, tile)
        top = jnp.max(scores, axis=0, keepdims=True)
        expo = jnp.exp((scores - top) * scale)
        prob = expo * (1.0 / jnp.sum(expo, axis=0, keepdims=True))
        prob_b = prob.astype(bf16)
        out_t = dot(val_t, prob_b).astype(bf16)
        delta = jnp.sum(g_t.astype(f32) * out_t.astype(f32), axis=0, keepdims=True)
        dscore = (prob * (dot(val, g_t) - delta)).astype(bf16)
        dquery_t = (dot(key_t, dscore) * scale).astype(bf16)
        give(0, first, out_t.T)
        give(1, first, dquery_t.T)
        dk, dv = dot(dscore, q), dot(prob_b, g)
        dkey = dk if dkey is None else dkey + dk
        dval = dv if dval is None else dval + dv
    give(2, 0, (dkey * scale).astype(bf16))
    give(3, 0, dval.astype(bf16))


def block_bias(rand_blocks, glob_blocks, me, ranks, local_blocks):
    total = ranks * local_blocks
    ids = jnp.arange(total, dtype=jnp.int32)
    order = (me - ids // local_blocks) % ranks * local_blocks + ids % local_blocks
    rand = jnp.take(rand_blocks, order, axis=0)
    gap = (order[:, None] - order[None, :]) % total
    near = (gap <= 1) | (gap == total - 1)
    glob = jnp.any(order[:, None] == glob_blocks[None, :], axis=1)
    picked = jnp.any(order[:, None, None] == rand[None, :, :], axis=2)
    allowed = near | glob[:, None] | picked
    bias = jnp.where(allowed, 0.0, -jnp.inf).astype(jnp.float32)
    return jnp.repeat(bias, BLOCK, axis=1)


def local(queries, keys, values, grad_out, rand_blocks, glob_blocks):
    ranks = lax.axis_size("ctx")
    me = lax.axis_index("ctx")
    tokens, features = queries.shape[1], queries.shape[2]
    head_dim = features // HEADS
    heads = HEADS // ranks
    width = heads * head_dim
    bf16 = jnp.bfloat16
    me_arr = jnp.reshape(me, (1,)).astype(jnp.int32)
    arrays = [queries[0], keys[0], values[0], grad_out[0]]
    piece = jax.ShapeDtypeStruct((4, tokens, width), bf16)
    full = jax.ShapeDtypeStruct((tokens, features), bf16)
    smem = pl.BlockSpec(memory_space=pltpu.SMEM)
    sems = pltpu.SemaphoreType.DMA((ranks - 1, 4))

    outgoing = pl.pallas_call(
        functools.partial(pack_kernel, ranks=ranks, width=width),
        out_shape=[piece] * (ranks - 1),
        in_specs=[smem] + [ANY] * 4,
        out_specs=[ANY] * (ranks - 1),
        scratch_shapes=[sems],
    )(me_arr, *arrays)
    got = [
        lax.ppermute(x, "ctx", [(j, (j + s) % ranks) for j in range(ranks)])
        for s, x in enumerate(outgoing, 1)
    ]
    bias = block_bias(rand_blocks[0], glob_blocks[0], me, ranks, tokens // BLOCK)
    mine = pl.BlockSpec((tokens, head_dim), lambda h, m: (0, m[0] * heads + h))
    block = pl.BlockSpec((4, tokens, head_dim), lambda h, m: (0, 0, h))
    results = pl.pallas_call(
        functools.partial(
            attention_kernel, ranks=ranks, tokens=tokens, scale=head_dim ** (-0.5)
        ),
        out_shape=[full] * 4 + [piece] * (ranks - 1),
        grid_spec=pltpu.PrefetchScalarGridSpec(
            num_scalar_prefetch=1,
            grid=(heads,),
            in_specs=[pl.BlockSpec(bias.shape, lambda h, m: (0, 0))]
            + [mine] * 4
            + [block] * (ranks - 1),
            out_specs=[mine] * 4 + [block] * (ranks - 1),
        ),
        compiler_params=pltpu.CompilerParams(vmem_limit_bytes=56 << 20),
    )(me_arr, bias, *arrays, *got)
    partial, sent = results[:4], results[4:]
    back = [
        lax.ppermute(x, "ctx", [(j, (j - s) % ranks) for j in range(ranks)])
        for s, x in enumerate(sent, 1)
    ]
    outs = pl.pallas_call(
        functools.partial(unpack_kernel, ranks=ranks, width=width),
        out_shape=[full] * 4,
        in_specs=[smem] + [ANY] * (4 + ranks - 1),
        out_specs=[ANY] * 4,
        scratch_shapes=[sems],
        input_output_aliases={1 + i: i for i in range(4)},
    )(me_arr, *partial, *back)
    return tuple(x[None] for x in outs)


def solution(mesh):
    wide = P(("groups", "dp"), "ctx", None)
    return jax.shard_map(
        local,
        mesh=mesh,
        in_specs=(wide,) * 4 + (P(("groups", "dp"), None, None), P(("groups", "dp"), None)),
        out_specs=(wide,) * 4,
        check_vma=False,
    )
```

time: 601 us -> 207 us (0.34)
  waiting for transfers between devices: 379 us -> 84 us
  Pallas kernels: 0 us -> 105 us
  local copies, waits for them, and re-layouts: 99.3 us -> 4.37 us
  other arithmetic: 57.5 us -> 0.37 us
  matrix products: 25.4 us -> 0 us
  between operations: 20.2 us -> 0.69 us
  starting transfers between devices: 15.4 us -> 9.01 us
    psum x2 -> x0, waiting for transfers between devices: 220 us -> none  [the longest x1 220 us: local(): glob_dk, glob_dv = lax.psum((glob_dk, glob_dv), 'ctx')]
    pallas_call x0 -> x3, Pallas kernels: none -> 105 us  [the longest x1 48.9 us: local(): pl.pallas_call(functools.partial(pack_kernel, ranks=ranks, width=width),...]
    ppermute x4 -> x6, waiting for transfers between devices: 159 us -> 84 us  [the longest x3 43.9 us: local(): lax.ppermute(x, 'ctx', [(j, (j - s) % ranks) for j in range(ranks)])]
    another operation x15 -> x0, local copies, waits for them, and re-layouts: 30.6 us -> none  [the longest x3 12.2 us: local(): jnp.stack([rnd_dk.reshape(slot_count, block_len, feature_width), rnd_dv.r...]
    dot_general x17 -> x0, matrix products: 23.1 us -> none  [the longest x1 2.93 us: local(): jnp.einsum('ahqk,aqhd->akhd', prob_rnd, dout4, preferred_element_type=f32)]
    scatter x2 -> x0, local copies, waits for them, and re-layouts: 19.2 us -> none  [local(): send_grad = jnp.zeros((2, ctx_size * capacity, block_len, feature_width),...]
    select_n x11 -> x3, other arithmetic: 18.8 us -> 0.17 us  [the longest x2 0.09 us: block_bias(): rand = jnp.take(rand_blocks, order, axis=0)]
    scatter-add x4 -> x0, other arithmetic: 14.6 us -> none  [the longest x1 9.92 us: local(): local_grad = local_grad.at[:, source_row].add(contrib)]
  transfers between devices with their start and end apart: 8 -> 6, of which waited for: 3 -> 5; matrix products, arithmetic and copies ran while one was open for 11% -> 1% of each run, Pallas kernels for 0% -> 0%
where the time goes in v1:
time: 207 us; the launch traced here: 204 us
  Pallas kernels  105 us (51%)
  waiting for transfers between devices  84 us (41%)
  starting transfers between devices  9.01 us (4%)
  local copies, waits for them, and re-layouts  4.37 us (2%)
    pallas_call x1, Pallas kernels, local(): pl.pallas_call(functools.partial(pack_kernel, ranks=ranks, width=width),...  48.9 us
    pallas_call x1, Pallas kernels, local(): pl.pallas_call(functools.partial(unpack_kernel, ranks=ranks, width=width)...  48.9 us
    ppermute x3, waiting for transfers between devices, local(): lax.ppermute(x, 'ctx', [(j, (j - s) % ranks) for j in range(ranks)])  43.9 us
    ppermute x3, waiting for transfers between devices, local(): lax.ppermute(x, 'ctx', [(j, (j + s) % ranks) for j in range(ranks)])  40.1 us
    pallas_call x1, Pallas kernels, local(): pl.pallas_call(functools.partial(attention_kernel, ranks=ranks, tokens=to...  7.6 us
    ppermute x3, starting transfers between devices, local(): lax.ppermute(x, 'ctx', [(j, (j - s) % ranks) for j in range(ranks)])  5.69 us
  transfers between devices with their start and end apart: 6, of which 5 were waited for; matrix products, arithmetic and copies ran while one was open for 1% of the time, Pallas kernels for 0%

profile of v1, /device:TPU:18, one launch (start us, length us, event | category | flops | bytes accessed | tf_op | source)
XLA Modules:
  0.0 203.8 jit_solution(4585628430699894358)
XLA Ops:
  0.6 48.9 %shard_map.93 = (bf16[4,128,512]{2,1,0:T(8,128)(2,1)}, bf16[4,128,512]{2,1,0:T(8,128)(2,1)}, bf16[4,128,512]{2,1,0:T(8,128)(2,1)}) custom-call(s32[1]{0:T(128)} %bitcast.me_ref, bf16[128,2048]{1,0:T(8,128)(2,1)} %bitcast.13, bf16[128,2048]{1,0:T(8,128)(2,1)} %bitcast.15, bf16[128,2048]{1,0:T(8,128)(2,1)} %bitcast.17, bf16[128,2048]{1,0:T(8,128)(2,1)} %bitcast.19), custom_call_target="tpu_custom_call" | custom-call | tf_op jit(solution)/shard_map/pallas_call | solution.py:131
  49.5 1.6 collective-permute-start
  51.1 0.3 collective-permute-start.1
  51.5 1.3 collective-permute-start.2
  52.9 0.0 copy-start.6
  52.9 0.7 copy-done.6
  53.5 0.1 copy.17
  53.6 0.6 gather_fusion
  54.2 0.1 broadcast_select_fusion
  54.2 0.1 copy.16
  54.3 0.0 copy-start.7
  54.4 0.6 copy-done.7
  55.0 0.1 compare_reduce_fusion.1
  55.1 0.1 compare_reduce_fusion
  55.2 0.1 or_select_fusion
  55.3 0.1 broadcast_in_dim.38
  55.3 0.7 reshape.203.bias_ref
  56.0 31.0 %collective-permute-done.refs_4_ = bf16[4,128,512]{2,1,0:T(8,128)(2,1)S(1)} collective-permute-done((bf16[4,128,512]{2,1,0:T(8,128)(2,1)}, bf16[4,128,512]{2,1,0:T(8,128)(2,1)S(1)}, u32[]{:S(2)}, u32[]{:S(2)}) %collective-permute-start) | collective-permute-done | bytes 524320 | tf_op jit(solution)/shard_map/ppermute | solution.py:139
  87.0 0.0 copy-start
  87.0 0.0 collective-permute-done.1.refs_5_
  87.1 0.0 copy-start.1
  87.1 9.0 %collective-permute-done.2.refs_6_ = bf16[4,128,512]{2,1,0:T(8,128)(2,1)S(1)} collective-permute-done((bf16[4,128,512]{2,1,0:T(8,128)(2,1)}, bf16[4,128,512]{2,1,0:T(8,128)(2,1)S(1)}, u32[]{:S(2)}, u32[]{:S(2)}) %collective-permute-start.2) | collective-permute-done | bytes 524320 | tf_op jit(solution)/shard_map/ppermute | solution.py:139
  96.1 0.0 copy-done
  96.1 0.0 copy-done.1
  96.1 0.0 copy-start.2
  96.1 0.8 copy-done.2
  96.9 7.6 %shard_map.94 = (bf16[128,2048]{1,0:T(8,128)(2,1)}, bf16[128,2048]{1,0:T(8,128)(2,1)}, bf16[128,2048]{1,0:T(8,128)(2,1)}, bf16[128,2048]{1,0:T(8,128)(2,1)}, bf1...) custom-call(s32[1]{0:T(128)} %bitcast.me_ref, f32[8,512]{1,0:T(8,128)} %reshape.203.bias_ref, ...), custom_call_target="tpu_custom_call" | custom-call | tf_op jit(solution)/shard_map/pallas_call | solution.py:145
  104.5 2.4 %collective-permute-start.3 = (bf16[4,128,512]{2,1,0:T(8,128)(2,1)}, bf16[4,128,512]{2,1,0:T(8,128)(2,1)S(1)}, u32[]{:S(2)}, u32[]{:S(2)}) collective-permute-start(bf16[4,128,512]{2,1,0:T(8,128)(2,1)} %get-tuple-element.25), channel_id=1, source_target_pairs={{0,12},{4,0},{8,4},{12,8},{1,13},{5,1},{9,5},{13,9},{2,14},{6,2},{... | collective-permute-start | bytes 1572872 | tf_op jit(solution)/shard_map/ppermute | solution.py:162
  106.9 3.3 %collective-permute-start.4 = (bf16[4,128,512]{2,1,0:T(8,128)(2,1)}, bf16[4,128,512]{2,1,0:T(8,128)(2,1)S(1)}, u32[]{:S(2)}, u32[]{:S(2)}) collective-permute-start(bf16[4,128,512]{2,1,0:T(8,128)(2,1)} %get-tuple-element.26), channel_id=1, source_target_pairs={{0,8},{4,12},{8,0},{12,4},{1,9},{5,13},{9,1},{13,5},{2,10},{6,14},... | collective-permute-start | bytes 1572872 | tf_op jit(solution)/shard_map/ppermute | solution.py:162
  110.2 0.0 collective-permute-start.5
  110.2 31.8 %collective-permute-done.3.refs_4_ = bf16[4,128,512]{2,1,0:T(8,128)(2,1)S(1)} collective-permute-done((bf16[4,128,512]{2,1,0:T(8,128)(2,1)}, bf16[4,128,512]{2,1,0:T(8,128)(2,1)S(1)}, u32[]{:S(2)}, u32[]{:S(2)}) %collective-permute-start.3) | collective-permute-done | bytes 524320 | tf_op jit(solution)/shard_map/ppermute | solution.py:162
  142.0 0.0 copy-start.3
  142.0 10.3 %collective-permute-done.4.refs_5_ = bf16[4,128,512]{2,1,0:T(8,128)(2,1)S(1)} collective-permute-done((bf16[4,128,512]{2,1,0:T(8,128)(2,1)}, bf16[4,128,512]{2,1,0:T(8,128)(2,1)S(1)}, u32[]{:S(2)}, u32[]{:S(2)}) %collective-permute-start.4) | collective-permute-done | bytes 524320 | tf_op jit(solution)/shard_map/ppermute | solution.py:162
  152.3 0.0 copy-start.4
  152.3 1.8 collective-permute-done.5.refs_6_
  154.1 0.0 copy-start.5
  154.1 0.0 copy-done.3
  154.1 0.0 copy-done.4
  154.1 0.8 copy-done.5
  154.9 48.9 %shard_map.95 = (bf16[128,2048]{1,0:T(8,128)(2,1)}, bf16[128,2048]{1,0:T(8,128)(2,1)}, bf16[128,2048]{1,0:T(8,128)(2,1)}, bf16[128,2048]{1,0:T(8,128)(2,1)}) custom-call(s32[1]{0:T(128)} %bitcast.me_ref, bf16[128,2048]{1,0:T(8,128)(2,1)} %get-tuple-element.21.refs_0_, ...), custom_call_target="tpu_custom_call", output_to_operand_aliasing={{0}: (1, {}), {1}: (2, {}), {2}: (3, {}), {3}: (4, {})} | custom-call | tf_op jit(solution)/shard_map/pallas_call | solution.py:165
  (4 shorter events, 0.1 us)
Async XLA Ops:
  49.5 37.5 %collective-permute-start = (bf16[4,128,512]{2,1,0:T(8,128)(2,1)}, bf16[4,128,512]{2,1,0:T(8,128)(2,1)S(1)}, u32[]{:S(2)}, u32[]{:S(2)}) collective-permute-start(bf16[4,128,512]{2,1,0:T(8,128)(2,1)} %get-tuple-element.18), channel_id=1, source_target_pairs={{0,4},{4,8},{8,12},{12,0},{1,5},{5,9},{9,13},{13,1},{2,6},{6,10},{... | collective-permute-start | bytes 1572872 | tf_op jit(solution)/shard_map/ppermute | solution.py:139
  51.1 35.9 %collective-permute-start.1 = (bf16[4,128,512]{2,1,0:T(8,128)(2,1)}, bf16[4,128,512]{2,1,0:T(8,128)(2,1)S(1)}, u32[]{:S(2)}, u32[]{:S(2)}) collective-permute-start(bf16[4,128,512]{2,1,0:T(8,128)(2,1)} %get-tuple-element.19), channel_id=1, source_target_pairs={{0,8},{4,12},{8,0},{12,4},{1,9},{5,13},{9,1},{13,5},{2,10},{6,14},... | collective-permute-start | bytes 1572872 | tf_op jit(solution)/shard_map/ppermute | solution.py:139
  51.5 44.6 %collective-permute-start.2 = (bf16[4,128,512]{2,1,0:T(8,128)(2,1)}, bf16[4,128,512]{2,1,0:T(8,128)(2,1)S(1)}, u32[]{:S(2)}, u32[]{:S(2)}) collective-permute-start(bf16[4,128,512]{2,1,0:T(8,128)(2,1)} %get-tuple-element.20), channel_id=1, source_target_pairs={{0,12},{4,0},{8,4},{12,8},{1,13},{5,1},{9,5},{13,9},{2,14},{6,2},{... | collective-permute-start | bytes 1572872 | tf_op jit(solution)/shard_map/ppermute | solution.py:139
  52.9 0.7 copy-start.6
  54.3 0.7 copy-start.7
  87.0 9.1 %copy-start = (bf16[4,128,512]{2,1,0:T(8,128)(2,1)}, bf16[4,128,512]{2,1,0:T(8,128)(2,1)S(1)}, u32[]{:S(2)}) copy-start(bf16[4,128,512]{2,1,0:T(8,128)(2,1)S(1)} %collective-permute-done.refs_4_) | copy-start | bytes 1572868
  87.1 9.1 %copy-start.1 = (bf16[4,128,512]{2,1,0:T(8,128)(2,1)}, bf16[4,128,512]{2,1,0:T(8,128)(2,1)S(1)}, u32[]{:S(2)}) copy-start(bf16[4,128,512]{2,1,0:T(8,128)(2,1)S(1)} %collective-permute-done.1.refs_5_) | copy-start | bytes 1572868
  96.1 0.8 copy-start.2
  104.5 37.5 %collective-permute-start.3 = (bf16[4,128,512]{2,1,0:T(8,128)(2,1)}, bf16[4,128,512]{2,1,0:T(8,128)(2,1)S(1)}, u32[]{:S(2)}, u32[]{:S(2)}) collective-permute-start(bf16[4,128,512]{2,1,0:T(8,128)(2,1)} %get-tuple-element.25), channel_id=1, source_target_pairs={{0,12},{4,0},{8,4},{12,8},{1,13},{5,1},{9,5},{13,9},{2,14},{6,2},{... | collective-permute-start | bytes 1572872 | tf_op jit(solution)/shard_map/ppermute | solution.py:162
  106.9 45.4 %collective-permute-start.4 = (bf16[4,128,512]{2,1,0:T(8,128)(2,1)}, bf16[4,128,512]{2,1,0:T(8,128)(2,1)S(1)}, u32[]{:S(2)}, u32[]{:S(2)}) collective-permute-start(bf16[4,128,512]{2,1,0:T(8,128)(2,1)} %get-tuple-element.26), channel_id=1, source_target_pairs={{0,8},{4,12},{8,0},{12,4},{1,9},{5,13},{9,1},{13,5},{2,10},{6,14},... | collective-permute-start | bytes 1572872 | tf_op jit(solution)/shard_map/ppermute | solution.py:162
  110.2 43.9 %collective-permute-start.5 = (bf16[4,128,512]{2,1,0:T(8,128)(2,1)}, bf16[4,128,512]{2,1,0:T(8,128)(2,1)S(1)}, u32[]{:S(2)}, u32[]{:S(2)}) collective-permute-start(bf16[4,128,512]{2,1,0:T(8,128)(2,1)} %get-tuple-element.27), channel_id=1, source_target_pairs={{0,4},{4,8},{8,12},{12,0},{1,5},{5,9},{9,13},{13,1},{2,6},{6,10},{... | collective-permute-start | bytes 1572872 | tf_op jit(solution)/shard_map/ppermute | solution.py:162
  142.0 12.1 %copy-start.3 = (bf16[4,128,512]{2,1,0:T(8,128)(2,1)}, bf16[4,128,512]{2,1,0:T(8,128)(2,1)S(1)}, u32[]{:S(2)}) copy-start(bf16[4,128,512]{2,1,0:T(8,128)(2,1)S(1)} %collective-permute-done.3.refs_4_) | copy-start | bytes 1572868
  152.3 1.8 copy-start.4
  154.1 0.8 copy-start.5

commit v2 on v1

v2 whole, which is shorter than its diff:
```python
import functools
import math

import jax
import jax.numpy as jnp
from jax import lax
from jax.experimental import pallas as pl
from jax.experimental.pallas import tpu as pltpu
from jax.sharding import PartitionSpec as P

HEADS = 16
BLOCK = 64
QUERY_TILE = 512
CHUNKS = 2
ANY = pl.BlockSpec(memory_space=pl.ANY)
SMEM = pl.BlockSpec(memory_space=pltpu.SMEM)
PARAMS = pltpu.CompilerParams(vmem_limit_bytes=56 << 20)


def pack_kernel(me_ref, *refs, ranks, chunks):
    arrays, outs = refs[:4], refs[4:]
    width = outs[0].shape[2]
    for chunk in range(chunks):
        for shift in range(1, ranks):
            dest = lax.rem(me_ref[0] + shift, ranks)
            start = pl.multiple_of((dest * chunks + chunk) * width, 128)
            out = outs[chunk * (ranks - 1) + shift - 1]
            for i, array in enumerate(arrays):
                out[i] = array[:, pl.ds(start, width)]


def unpack_kernel(me_ref, *refs, ranks):
    pieces, outs = refs[4 : 3 + ranks], refs[3 + ranks :]
    for shift in range(1, ranks):

        @pl.when(pl.program_id(0) == shift - 1)
        def _():
            for i, out in enumerate(outs):
                out[...] = pieces[shift - 1][i]


def attention_kernel(me_ref, bias_ref, *refs, ranks, tokens, scale):
    own, got = refs[:4], refs[4 : 3 + ranks]
    own_outs, sent = refs[-3 - ranks : 1 - ranks], refs[1 - ranks :]
    f32, bf16 = jnp.float32, jnp.bfloat16
    length = ranks * tokens
    tile = min(QUERY_TILE, length)

    def whole(i):
        return jnp.concatenate([own[i][...]] + [piece[i] for piece in got], axis=0)

    def dot(a, b):
        return jnp.dot(a, b, preferred_element_type=f32)

    def give(i, first, value):
        for r in range(value.shape[0] // tokens):
            rank, part = first // tokens + r, value[r * tokens : (r + 1) * tokens]
            if rank == 0:
                own_outs[i][...] = part
            else:
                sent[rank - 1][i] = part

    query, key, val, dout = (whole(i) for i in range(4))
    key_t, val_t = key.T, val.T
    dkey = dval = None
    for first in range(0, length, tile):
        q = query[first : first + tile]
        g = dout[first : first + tile]
        g_t = g.T
        scores = dot(key, q.T).reshape(-1, BLOCK, tile)
        bias = bias_ref[:, first : first + tile]
        scores = (scores + bias[:, None, :]).reshape(length, tile)
        top = jnp.max(scores, axis=0, keepdims=True)
        expo = jnp.exp((scores - top) * scale)
        prob = expo * (1.0 / jnp.sum(expo, axis=0, keepdims=True))
        prob_b = prob.astype(bf16)
        out_t = dot(val_t, prob_b).astype(bf16)
        delta = jnp.sum(g_t.astype(f32) * out_t.astype(f32), axis=0, keepdims=True)
        dscore = (prob * (dot(val, g_t) - delta)).astype(bf16)
        dquery_t = (dot(key_t, dscore) * scale).astype(bf16)
        give(0, first, out_t.T)
        give(1, first, dquery_t.T)
        dk, dv = dot(dscore, q), dot(prob_b, g)
        dkey = dk if dkey is None else dkey + dk
        dval = dv if dval is None else dval + dv
    give(2, 0, (dkey * scale).astype(bf16))
    give(3, 0, dval.astype(bf16))


def block_bias(rand_blocks, glob_blocks, me, ranks, local_blocks):
    total = ranks * local_blocks
    ids = jnp.arange(total, dtype=jnp.int32)
    order = (me - ids // local_blocks) % ranks * local_blocks + ids % local_blocks
    rand = jnp.take(rand_blocks, order, axis=0)
    gap = (order[:, None] - order[None, :]) % total
    near = (gap <= 1) | (gap == total - 1)
    glob = jnp.any(order[:, None] == glob_blocks[None, :], axis=1)
    picked = jnp.any(order[:, None, None] == rand[None, :, :], axis=2)
    allowed = near | glob[:, None] | picked
    bias = jnp.where(allowed, 0.0, -jnp.inf).astype(jnp.float32)
    return jnp.repeat(bias, BLOCK, axis=1)


def local(queries, keys, values, grad_out, rand_blocks, glob_blocks):
    ranks = lax.axis_size("ctx")
    me = lax.axis_index("ctx")
    tokens, features = queries.shape[1], queries.shape[2]
    head_dim = features // HEADS
    chunks = math.gcd(HEADS // ranks, CHUNKS)
    heads = HEADS // ranks // chunks
    width = heads * head_dim
    me_arr = jnp.reshape(me, (1,)).astype(jnp.int32)
    arrays = [queries[0], keys[0], values[0], grad_out[0]]
    piece = jax.ShapeDtypeStruct((4, tokens, width), jnp.bfloat16)
    full = jax.ShapeDtypeStruct((tokens, features), jnp.bfloat16)
    block = pl.BlockSpec((4, tokens, head_dim), lambda h, m: (0, 0, h))

    def attend(chunk, got, partial):
        first = chunk * heads
        mine = pl.BlockSpec(
            (tokens, head_dim), lambda h, m: (0, m[0] * (heads * chunks) + first + h)
        )
        results = pl.pallas_call(
            functools.partial(
                attention_kernel, ranks=ranks, tokens=tokens, scale=head_dim ** (-0.5)
            ),
            out_shape=[full] * 4 + [piece] * (ranks - 1),
            grid_spec=pltpu.PrefetchScalarGridSpec(
                num_scalar_prefetch=1,
                grid=(heads,),
                in_specs=[pl.BlockSpec(bias.shape, lambda h, m: (0, 0))]
                + [mine] * 4
                + [block] * (ranks - 1)
                + [ANY] * len(partial),
                out_specs=[mine] * 4 + [block] * (ranks - 1),
            ),
            input_output_aliases={5 + ranks + i: i for i in range(len(partial))},
            compiler_params=PARAMS,
        )(me_arr, bias, *arrays, *got, *partial)
        return results[:4], results[4:]

    def unpack(chunk, back, partial):
        whole = pl.BlockSpec((4, tokens, width), lambda s, m: (0, 0, 0))
        there = pl.BlockSpec(
            (tokens, width), lambda s, m: (0, lax.rem(m[0] + s + 1, ranks) * chunks + chunk)
        )
        return pl.pallas_call(
            functools.partial(unpack_kernel, ranks=ranks),
            out_shape=[full] * 4,
            grid_spec=pltpu.PrefetchScalarGridSpec(
                num_scalar_prefetch=1,
                grid=(ranks - 1,),
                in_specs=[ANY] * 4 + [whole] * (ranks - 1),
                out_specs=[there] * 4,
            ),
            input_output_aliases={1 + i: i for i in range(4)},
            compiler_params=PARAMS,
        )(me_arr, *partial, *back)

    outgoing = pl.pallas_call(
        functools.partial(pack_kernel, ranks=ranks, chunks=chunks),
        out_shape=[piece] * (chunks * (ranks - 1)),
        in_specs=[SMEM] + [pl.BlockSpec(memory_space=pltpu.VMEM)] * 4,
        compiler_params=PARAMS,
    )(me_arr, *arrays)
    got = [
        lax.ppermute(x, "ctx", [(j, (j + i % (ranks - 1) + 1) % ranks) for j in range(ranks)])
        for i, x in enumerate(outgoing)
    ]
    bias = block_bias(rand_blocks[0], glob_blocks[0], me, ranks, tokens // BLOCK)
    partial, back = [], []
    for chunk in range(chunks):
        partial, sent = attend(
            chunk, got[chunk * (ranks - 1) : (chunk + 1) * (ranks - 1)], partial
        )
        back.append(
            [
                lax.ppermute(x, "ctx", [(j, (j - s) % ranks) for j in range(ranks)])
                for s, x in enumerate(sent, 1)
            ]
        )
    for chunk in range(chunks):
        partial = unpack(chunk, back[chunk], partial)
    return tuple(x[None] for x in partial)


def solution(mesh):
    wide = P(("groups", "dp"), "ctx", None)
    return jax.shard_map(
        local,
        mesh=mesh,
        in_specs=(wide,) * 4 + (P(("groups", "dp"), None, None), P(("groups", "dp"), None)),
        out_specs=(wide,) * 4,
        check_vma=False,
    )
```

time: 207 us -> 109 us (0.53); the launches traced: 204 us -> 108 us
  Pallas kernels: 105 us -> 17.3 us
  waiting for transfers between devices: 84 us -> 64.6 us
  starting transfers between devices: 9.01 us -> 18.8 us
    pallas_call x3 -> x5, Pallas kernels: 105 us -> 17.3 us  [the longest x2 9.36 us: attend(): pl.pallas_call(functools.partial(attention_kernel, ranks=ranks, tokens=to...]
    ppermute x3 -> x6, waiting for transfers between devices: 43.9 us -> 31.2 us  [local(): lax.ppermute(x, 'ctx', [(j, (j - s) % ranks) for j in range(ranks)])]
    ppermute x3 -> x6, waiting for transfers between devices: 40.1 us -> 33.4 us  [local(): lax.ppermute(x, 'ctx', [(j, (j + i % (ranks - 1) + 1) % ranks) for j in r...]
    ppermute x3 -> x6, starting transfers between devices: 5.69 us -> 11.4 us  [local(): lax.ppermute(x, 'ctx', [(j, (j - s) % ranks) for j in range(ranks)])]
    ppermute x3 -> x6, starting transfers between devices: 3.31 us -> 7.43 us  [local(): lax.ppermute(x, 'ctx', [(j, (j + i % (ranks - 1) + 1) % ranks) for j in r...]
    unnamed x16 -> x28, local copies, waits for them, and re-layouts: 2.9 us -> 4.94 us
  transfers between devices with their start and end apart: 6 -> 12, of which waited for: 5 -> 5; matrix products, arithmetic and copies ran while one was open for 1% -> 2% of each run, Pallas kernels for 0% -> 11%
where the time goes in v2:
time: 109 us; the launch traced here: 108 us
  waiting for transfers between devices  64.6 us (59%)
  starting transfers between devices  18.8 us (17%)
  Pallas kernels  17.3 us (16%)
  local copies, waits for them, and re-layouts  6.41 us (6%)
    ppermute x6, waiting for transfers between devices, local(): lax.ppermute(x, 'ctx', [(j, (j + i % (ranks - 1) + 1) % ranks) for j in r...  33.4 us
    ppermute x6, waiting for transfers between devices, local(): lax.ppermute(x, 'ctx', [(j, (j - s) % ranks) for j in range(ranks)])  31.2 us
    ppermute x6, starting transfers between devices, local(): lax.ppermute(x, 'ctx', [(j, (j - s) % ranks) for j in range(ranks)])  11.4 us
    pallas_call x2, Pallas kernels, attend(): pl.pallas_call(functools.partial(attention_kernel, ranks=ranks, tokens=to...  9.36 us
    ppermute x6, starting transfers between devices, local(): lax.ppermute(x, 'ctx', [(j, (j + i % (ranks - 1) + 1) % ranks) for j in r...  7.43 us
    pallas_call x2, Pallas kernels, unpack(): pl.pallas_call(functools.partial(unpack_kernel, ranks=ranks), out_shape=[...  5.1 us
    unnamed x28, local copies, waits for them, and re-layouts  4.94 us
    pallas_call x1, Pallas kernels, local(): pl.pallas_call(functools.partial(pack_kernel, ranks=ranks, chunks=chunks)...  2.88 us
  transfers between devices with their start and end apart: 12, of which 5 were waited for; matrix products, arithmetic and copies ran while one was open for 2% of the time, Pallas kernels for 11%

profile of v2, /device:TPU:18, one launch (start us, length us, event | category | flops | bytes accessed | tf_op | source)
XLA Modules:
  0.0 108.3 jit_solution(9603442408557634373)
XLA Ops:
  0.6 2.9 %shard_map.93 = (bf16[4,128,256]{2,1,0:T(8,128)(2,1)}, bf16[4,128,256]{2,1,0:T(8,128)(2,1)}, bf16[4,128,256]{2,1,0:T(8,128)(2,1)}, bf16[4,128,256]{2,1,0:T(8,128...) custom-call(s32[1]{0:T(128)} %bitcast.me_ref, bf16[128,2048]{1,0:T(8,128)(2,1)} %bitcast.13, ...), custom_call_target="tpu_custom_call" | custom-call | tf_op jit(solution)/shard_map/pallas_call | solution.py:160
  3.5 1.6 %collective-permute-start = (bf16[4,128,256]{2,1,0:T(8,128)(2,1)}, bf16[4,128,256]{2,1,0:T(8,128)(2,1)S(1)}, u32[]{:S(2)}, u32[]{:S(2)}) collective-permute-start(bf16[4,128,256]{2,1,0:T(8,128)(2,1)} %get-tuple-element.32), channel_id=1, source_target_pairs={{0,4},{4,8},{8,12},{12,0},{1,5},{5,9},{9,13},{13,1},{2,6},{6,10},{... | collective-permute-start | bytes 786440 | tf_op jit(solution)/shard_map/ppermute | solution.py:167
  5.1 0.3 collective-permute-start.1
  5.4 1.6 %collective-permute-start.3 = (bf16[4,128,256]{2,1,0:T(8,128)(2,1)}, bf16[4,128,256]{2,1,0:T(8,128)(2,1)S(1)}, u32[]{:S(2)}, u32[]{:S(2)}) collective-permute-start(bf16[4,128,256]{2,1,0:T(8,128)(2,1)} %get-tuple-element.35), channel_id=1, source_target_pairs={{0,4},{4,8},{8,12},{12,0},{1,5},{5,9},{9,13},{13,1},{2,6},{6,10},{... | collective-permute-start | bytes 786440 | tf_op jit(solution)/shard_map/ppermute | solution.py:167
  7.0 1.2 %collective-permute-start.4 = (bf16[4,128,256]{2,1,0:T(8,128)(2,1)}, bf16[4,128,256]{2,1,0:T(8,128)(2,1)S(1)}, u32[]{:S(2)}, u32[]{:S(2)}) collective-permute-start(bf16[4,128,256]{2,1,0:T(8,128)(2,1)} %get-tuple-element.36), channel_id=1, source_target_pairs={{0,8},{4,12},{8,0},{12,4},{1,9},{5,13},{9,1},{13,5},{2,10},{6,14},... | collective-permute-start | bytes 786440 | tf_op jit(solution)/shard_map/ppermute | solution.py:167
  8.2 2.7 %collective-permute-start.5 = (bf16[4,128,256]{2,1,0:T(8,128)(2,1)}, bf16[4,128,256]{2,1,0:T(8,128)(2,1)S(1)}, u32[]{:S(2)}, u32[]{:S(2)}) collective-permute-start(bf16[4,128,256]{2,1,0:T(8,128)(2,1)} %get-tuple-element.37), channel_id=1, source_target_pairs={{0,12},{4,0},{8,4},{12,8},{1,13},{5,1},{9,5},{13,9},{2,14},{6,2},{... | collective-permute-start | bytes 786440 | tf_op jit(solution)/shard_map/ppermute | solution.py:167
  11.0 0.0 copy-start.12
  11.0 0.7 copy-done.12
  11.7 0.1 copy.25
  11.7 0.6 gather_fusion
  12.3 0.1 broadcast_select_fusion
  12.4 0.1 copy.24
  12.5 0.1 compare_reduce_fusion
  12.6 0.7 copy-done.13
  13.2 0.1 compare_reduce_fusion.1
  13.3 33.4 %collective-permute-done.3.refs_4_ = bf16[4,128,256]{2,1,0:T(8,128)(2,1)S(1)} collective-permute-done((bf16[4,128,256]{2,1,0:T(8,128)(2,1)}, bf16[4,128,256]{2,1,0:T(8,128)(2,1)S(1)}, u32[]{:S(2)}, u32[]{:S(2)}) %collective-permute-start.3) | collective-permute-done | bytes 262176 | tf_op jit(solution)/shard_map/ppermute | solution.py:167
  46.7 0.0 collective-permute-start.2
  46.7 0.1 or_select_fusion
  46.8 0.1 broadcast_in_dim.38
  46.8 0.7 reshape.203.bias_ref
  47.5 0.0 collective-permute-done.4.refs_5_
  47.5 0.0 collective-permute-done.5.refs_6_
  47.5 0.7 copy-done.7
  48.2 0.7 copy-done.8
  48.9 4.7 %shard_map.94 = (bf16[128,2048]{1,0:T(8,128)(2,1)}, bf16[128,2048]{1,0:T(8,128)(2,1)}, bf16[128,2048]{1,0:T(8,128)(2,1)}, bf16[128,2048]{1,0:T(8,128)(2,1)}, bf1...) custom-call(s32[1]{0:T(128)} %bitcast.me_ref, f32[8,512]{1,0:T(8,128)} %reshape.203.bias_ref, ...), custom_call_target="tpu_custom_call" | custom-call | tf_op jit(solution)/shard_map/pallas_call | solution.py:123
  53.6 3.3 %collective-permute-start.6 = (bf16[4,128,256]{2,1,0:T(8,128)(2,1)}, bf16[4,128,256]{2,1,0:T(8,128)(2,1)S(1)}, u32[]{:S(2)}, u32[]{:S(2)}) collective-permute-start(bf16[4,128,256]{2,1,0:T(8,128)(2,1)} %get-tuple-element.46), channel_id=1, source_target_pairs={{0,12},{4,0},{8,4},{12,8},{1,13},{5,1},{9,5},{13,9},{2,14},{6,2},{... | collective-permute-start | bytes 786440 | tf_op jit(solution)/shard_map/ppermute | solution.py:178
  56.9 4.2 %collective-permute-start.7 = (bf16[4,128,256]{2,1,0:T(8,128)(2,1)}, bf16[4,128,256]{2,1,0:T(8,128)(2,1)S(1)}, u32[]{:S(2)}, u32[]{:S(2)}) collective-permute-start(bf16[4,128,256]{2,1,0:T(8,128)(2,1)} %get-tuple-element.47), channel_id=1, source_target_pairs={{0,8},{4,12},{8,0},{12,4},{1,9},{5,13},{9,1},{13,5},{2,10},{6,14},... | collective-permute-start | bytes 786440 | tf_op jit(solution)/shard_map/ppermute | solution.py:178
  61.1 0.0 collective-permute-done.refs_4_
  61.1 0.0 collective-permute-start.8
  61.1 0.0 collective-permute-done.1.refs_5_
  61.1 0.0 collective-permute-done.2.refs_6_
  61.1 0.7 copy-done
  61.8 0.1 copy-done.1
  61.9 0.1 copy-done.4
  62.0 4.7 %shard_map.95 = (bf16[128,2048]{1,0:T(8,128)(2,1)}, bf16[128,2048]{1,0:T(8,128)(2,1)}, bf16[128,2048]{1,0:T(8,128)(2,1)}, bf16[128,2048]{1,0:T(8,128)(2,1)}, bf1...) custom-call(s32[1]{0:T(128)} %bitcast.me_ref, ...), custom_call_target="tpu_custom_call", output_to_operand_aliasing={{0}: (9, {}), {1}: (10, {}), {2}: (11, {}), {3}: (12, {})} | custom-call | tf_op jit(solution)/shard_map/pallas_call | solution.py:123
  66.7 2.0 %collective-permute-start.9 = (bf16[4,128,256]{2,1,0:T(8,128)(2,1)}, bf16[4,128,256]{2,1,0:T(8,128)(2,1)S(1)}, u32[]{:S(2)}, u32[]{:S(2)}) collective-permute-start(bf16[4,128,256]{2,1,0:T(8,128)(2,1)} %get-tuple-element.53), channel_id=1, source_target_pairs={{0,12},{4,0},{8,4},{12,8},{1,13},{5,1},{9,5},{13,9},{2,14},{6,2},{... | collective-permute-start | bytes 786440 | tf_op jit(solution)/shard_map/ppermute | solution.py:178
  68.7 1.9 %collective-permute-start.10 = (bf16[4,128,256]{2,1,0:T(8,128)(2,1)}, bf16[4,128,256]{2,1,0:T(8,128)(2,1)S(1)}, u32[]{:S(2)}, u32[]{:S(2)}) collective-permute-start(bf16[4,128,256]{2,1,0:T(8,128)(2,1)} %get-tuple-element.54), channel_id=1, source_target_pairs={{0,8},{4,12},{8,0},{12,4},{1,9},{5,13},{9,1},{13,5},{2,10},{6,14},... | collective-permute-start | bytes 786440 | tf_op jit(solution)/shard_map/ppermute | solution.py:178
  70.5 0.0 collective-permute-done.6.refs_4_
  70.5 0.0 collective-permute-start.11
  70.5 11.3 %collective-permute-done.7.refs_5_ = bf16[4,128,256]{2,1,0:T(8,128)(2,1)S(1)} collective-permute-done((bf16[4,128,256]{2,1,0:T(8,128)(2,1)}, bf16[4,128,256]{2,1,0:T(8,128)(2,1)S(1)}, u32[]{:S(2)}, u32[]{:S(2)}) %collective-permute-start.7) | collective-permute-done | bytes 262176 | tf_op jit(solution)/shard_map/ppermute | solution.py:178
  81.9 12.9 %collective-permute-done.8.refs_6_ = bf16[4,128,256]{2,1,0:T(8,128)(2,1)S(1)} collective-permute-done((bf16[4,128,256]{2,1,0:T(8,128)(2,1)}, bf16[4,128,256]{2,1,0:T(8,128)(2,1)S(1)}, u32[]{:S(2)}, u32[]{:S(2)}) %collective-permute-start.8) | collective-permute-done | bytes 262176 | tf_op jit(solution)/shard_map/ppermute | solution.py:178
  94.8 0.7 copy-done.6
  95.5 2.5 %shard_map.96 = (bf16[128,2048]{1,0:T(8,128)(2,1)}, bf16[128,2048]{1,0:T(8,128)(2,1)}, bf16[128,2048]{1,0:T(8,128)(2,1)}, bf16[128,2048]{1,0:T(8,128)(2,1)}) custom-call(s32[1]{0:T(128)} %bitcast.me_ref, bf16[128,2048]{1,0:T(8,128)(2,1)} %get-tuple-element.42.refs_0_, ...), custom_call_target="tpu_custom_call", output_to_operand_aliasing={{0}: (1, {}), {1}: (2, {}), {2}: (3, {}), {3}: (4, {})} | custom-call | tf_op jit(solution)/shard_map/pallas_call | solution.py:147
  98.0 0.0 collective-permute-done.9.refs_4_
  98.0 3.3 %collective-permute-done.10.refs_5_ = bf16[4,128,256]{2,1,0:T(8,128)(2,1)S(1)} collective-permute-done((bf16[4,128,256]{2,1,0:T(8,128)(2,1)}, bf16[4,128,256]{2,1,0:T(8,128)(2,1)S(1)}, u32[]{:S(2)}, u32[]{:S(2)}) %collective-permute-start.10) | collective-permute-done | bytes 262176 | tf_op jit(solution)/shard_map/ppermute | solution.py:178
  101.3 3.7 %collective-permute-done.11.refs_6_ = bf16[4,128,256]{2,1,0:T(8,128)(2,1)S(1)} collective-permute-done((bf16[4,128,256]{2,1,0:T(8,128)(2,1)}, bf16[4,128,256]{2,1,0:T(8,128)(2,1)S(1)}, u32[]{:S(2)}, u32[]{:S(2)}) %collective-permute-start.11) | collective-permute-done | bytes 262176 | tf_op jit(solution)/shard_map/ppermute | solution.py:178
  105.0 0.7 copy-done.11
  105.7 2.6 %shard_map.97 = (bf16[128,2048]{1,0:T(8,128)(2,1)}, bf16[128,2048]{1,0:T(8,128)(2,1)}, bf16[128,2048]{1,0:T(8,128)(2,1)}, bf16[128,2048]{1,0:T(8,128)(2,1)}) custom-call(s32[1]{0:T(128)} %bitcast.me_ref, bf16[128,2048]{1,0:T(8,128)(2,1)} %get-tuple-element.49.refs_0_, ...), custom_call_target="tpu_custom_call", output_to_operand_aliasing={{0}: (1, {}), {1}: (2, {}), {2}: (3, {}), {3}: (4, {})} | custom-call | tf_op jit(solution)/shard_map/pallas_call | solution.py:147
  (22 shorter events, 0.1 us)
Async XLA Ops:
  3.5 57.6 %collective-permute-start = (bf16[4,128,256]{2,1,0:T(8,128)(2,1)}, bf16[4,128,256]{2,1,0:T(8,128)(2,1)S(1)}, u32[]{:S(2)}, u32[]{:S(2)}) collective-permute-start(bf16[4,128,256]{2,1,0:T(8,128)(2,1)} %get-tuple-element.32), channel_id=1, source_target_pairs={{0,4},{4,8},{8,12},{12,0},{1,5},{5,9},{9,13},{13,1},{2,6},{6,10},{... | collective-permute-start | bytes 786440 | tf_op jit(solution)/shard_map/ppermute | solution.py:167
  5.1 56.0 %collective-permute-start.1 = (bf16[4,128,256]{2,1,0:T(8,128)(2,1)}, bf16[4,128,256]{2,1,0:T(8,128)(2,1)S(1)}, u32[]{:S(2)}, u32[]{:S(2)}) collective-permute-start(bf16[4,128,256]{2,1,0:T(8,128)(2,1)} %get-tuple-element.33), channel_id=1, source_target_pairs={{0,8},{4,12},{8,0},{12,4},{1,9},{5,13},{9,1},{13,5},{2,10},{6,14},... | collective-permute-start | bytes 786440 | tf_op jit(solution)/shard_map/ppermute | solution.py:167
  5.4 41.2 %collective-permute-start.3 = (bf16[4,128,256]{2,1,0:T(8,128)(2,1)}, bf16[4,128,256]{2,1,0:T(8,128)(2,1)S(1)}, u32[]{:S(2)}, u32[]{:S(2)}) collective-permute-start(bf16[4,128,256]{2,1,0:T(8,128)(2,1)} %get-tuple-element.35), channel_id=1, source_target_pairs={{0,4},{4,8},{8,12},{12,0},{1,5},{5,9},{9,13},{13,1},{2,6},{6,10},{... | collective-permute-start | bytes 786440 | tf_op jit(solution)/shard_map/ppermute | solution.py:167
  7.0 40.5 %collective-permute-start.4 = (bf16[4,128,256]{2,1,0:T(8,128)(2,1)}, bf16[4,128,256]{2,1,0:T(8,128)(2,1)S(1)}, u32[]{:S(2)}, u32[]{:S(2)}) collective-permute-start(bf16[4,128,256]{2,1,0:T(8,128)(2,1)} %get-tuple-element.36), channel_id=1, source_target_pairs={{0,8},{4,12},{8,0},{12,4},{1,9},{5,13},{9,1},{13,5},{2,10},{6,14},... | collective-permute-start | bytes 786440 | tf_op jit(solution)/shard_map/ppermute | solution.py:167
  8.2 39.3 %collective-permute-start.5 = (bf16[4,128,256]{2,1,0:T(8,128)(2,1)}, bf16[4,128,256]{2,1,0:T(8,128)(2,1)S(1)}, u32[]{:S(2)}, u32[]{:S(2)}) collective-permute-start(bf16[4,128,256]{2,1,0:T(8,128)(2,1)} %get-tuple-element.37), channel_id=1, source_target_pairs={{0,12},{4,0},{8,4},{12,8},{1,13},{5,1},{9,5},{13,9},{2,14},{6,2},{... | collective-permute-start | bytes 786440 | tf_op jit(solution)/shard_map/ppermute | solution.py:167
  11.0 0.7 copy-start.12
  12.5 0.7 copy-start.13
  46.7 0.9 copy-start.5
  46.7 14.5 %collective-permute-start.2 = (bf16[4,128,256]{2,1,0:T(8,128)(2,1)}, bf16[4,128,256]{2,1,0:T(8,128)(2,1)S(1)}, u32[]{:S(2)}, u32[]{:S(2)}) collective-permute-start(bf16[4,128,256]{2,1,0:T(8,128)(2,1)} %get-tuple-element.34), channel_id=1, source_target_pairs={{0,12},{4,0},{8,4},{12,8},{1,13},{5,1},{9,5},{13,9},{2,14},{6,2},{... | collective-permute-start | bytes 786440 | tf_op jit(solution)/shard_map/ppermute | solution.py:167
  47.5 0.7 copy-start.7
  48.2 0.7 copy-start.8
  53.6 16.9 %collective-permute-start.6 = (bf16[4,128,256]{2,1,0:T(8,128)(2,1)}, bf16[4,128,256]{2,1,0:T(8,128)(2,1)S(1)}, u32[]{:S(2)}, u32[]{:S(2)}) collective-permute-start(bf16[4,128,256]{2,1,0:T(8,128)(2,1)} %get-tuple-element.46), channel_id=1, source_target_pairs={{0,12},{4,0},{8,4},{12,8},{1,13},{5,1},{9,5},{13,9},{2,14},{6,2},{... | collective-permute-start | bytes 786440 | tf_op jit(solution)/shard_map/ppermute | solution.py:178
  56.9 24.9 %collective-permute-start.7 = (bf16[4,128,256]{2,1,0:T(8,128)(2,1)}, bf16[4,128,256]{2,1,0:T(8,128)(2,1)S(1)}, u32[]{:S(2)}, u32[]{:S(2)}) collective-permute-start(bf16[4,128,256]{2,1,0:T(8,128)(2,1)} %get-tuple-element.47), channel_id=1, source_target_pairs={{0,8},{4,12},{8,0},{12,4},{1,9},{5,13},{9,1},{13,5},{2,10},{6,14},... | collective-permute-start | bytes 786440 | tf_op jit(solution)/shard_map/ppermute | solution.py:178
  61.1 0.7 copy-start
  61.1 33.7 %collective-permute-start.8 = (bf16[4,128,256]{2,1,0:T(8,128)(2,1)}, bf16[4,128,256]{2,1,0:T(8,128)(2,1)S(1)}, u32[]{:S(2)}, u32[]{:S(2)}) collective-permute-start(bf16[4,128,256]{2,1,0:T(8,128)(2,1)} %get-tuple-element.48), channel_id=1, source_target_pairs={{0,4},{4,8},{8,12},{12,0},{1,5},{5,9},{9,13},{13,1},{2,6},{6,10},{... | collective-permute-start | bytes 786440 | tf_op jit(solution)/shard_map/ppermute | solution.py:178
  61.1 0.8 copy-start.1
  61.1 0.8 copy-start.4
  66.7 31.4 %collective-permute-start.9 = (bf16[4,128,256]{2,1,0:T(8,128)(2,1)}, bf16[4,128,256]{2,1,0:T(8,128)(2,1)S(1)}, u32[]{:S(2)}, u32[]{:S(2)}) collective-permute-start(bf16[4,128,256]{2,1,0:T(8,128)(2,1)} %get-tuple-element.53), channel_id=1, source_target_pairs={{0,12},{4,0},{8,4},{12,8},{1,13},{5,1},{9,5},{13,9},{2,14},{6,2},{... | collective-permute-start | bytes 786440 | tf_op jit(solution)/shard_map/ppermute | solution.py:178
  68.7 32.6 %collective-permute-start.10 = (bf16[4,128,256]{2,1,0:T(8,128)(2,1)}, bf16[4,128,256]{2,1,0:T(8,128)(2,1)S(1)}, u32[]{:S(2)}, u32[]{:S(2)}) collective-permute-start(bf16[4,128,256]{2,1,0:T(8,128)(2,1)} %get-tuple-element.54), channel_id=1, source_target_pairs={{0,8},{4,12},{8,0},{12,4},{1,9},{5,13},{9,1},{13,5},{2,10},{6,14},... | collective-permute-start | bytes 786440 | tf_op jit(solution)/shard_map/ppermute | solution.py:178
  70.5 24.2 %copy-start.2 = (bf16[4,128,256]{2,1,0:T(8,128)(2,1)}, bf16[4,128,256]{2,1,0:T(8,128)(2,1)S(1)}, u32[]{:S(2)}) copy-start(bf16[4,128,256]{2,1,0:T(8,128)(2,1)S(1)} %collective-permute-done.6.refs_4_) | copy-start | bytes 786436
  70.5 34.5 %collective-permute-start.11 = (bf16[4,128,256]{2,1,0:T(8,128)(2,1)}, bf16[4,128,256]{2,1,0:T(8,128)(2,1)S(1)}, u32[]{:S(2)}, u32[]{:S(2)}) collective-permute-start(bf16[4,128,256]{2,1,0:T(8,128)(2,1)} %get-tuple-element.55), channel_id=1, source_target_pairs={{0,4},{4,8},{8,12},{12,0},{1,5},{5,9},{9,13},{13,1},{2,6},{6,10},{... | collective-permute-start | bytes 786440 | tf_op jit(solution)/shard_map/ppermute | solution.py:178
  81.9 12.9 %copy-start.3 = (bf16[4,128,256]{2,1,0:T(8,128)(2,1)}, bf16[4,128,256]{2,1,0:T(8,128)(2,1)S(1)}, u32[]{:S(2)}) copy-start(bf16[4,128,256]{2,1,0:T(8,128)(2,1)S(1)} %collective-permute-done.7.refs_5_) | copy-start | bytes 786436
  94.8 0.7 copy-start.6
  98.0 7.0 %copy-start.9 = (bf16[4,128,256]{2,1,0:T(8,128)(2,1)}, bf16[4,128,256]{2,1,0:T(8,128)(2,1)S(1)}, u32[]{:S(2)}) copy-start(bf16[4,128,256]{2,1,0:T(8,128)(2,1)S(1)} %collective-permute-done.9.refs_4_) | copy-start | bytes 786436
  101.3 3.7 %copy-start.10 = (bf16[4,128,256]{2,1,0:T(8,128)(2,1)}, bf16[4,128,256]{2,1,0:T(8,128)(2,1)S(1)}, u32[]{:S(2)}) copy-start(bf16[4,128,256]{2,1,0:T(8,128)(2,1)S(1)} %collective-permute-done.10.refs_5_) | copy-start | bytes 786436
  105.0 0.7 copy-start.11

commit v3 on v1

v3 whole, which is shorter than its diff:
```python
import functools

import jax
import jax.numpy as jnp
from jax import lax
from jax.experimental import pallas as pl
from jax.experimental.pallas import tpu as pltpu
from jax.sharding import PartitionSpec as P

HEADS = 16
BLOCK = 64
QUERY_TILE = 512
ANY = pl.BlockSpec(memory_space=pl.ANY)
SMEM = pl.BlockSpec(memory_space=pltpu.SMEM)
VMEM = pl.BlockSpec(memory_space=pltpu.VMEM)
PARAMS = pltpu.CompilerParams(vmem_limit_bytes=48 << 20)


def pack_kernel(me_ref, *refs, ranks, wanted):
    arrays, outs, sems = refs[:4], refs[4:-1], refs[-1]
    features, width = arrays[0].shape[1], outs[0].shape[2]
    copies = []
    for n, (head, step) in enumerate(wanted):
        dest = me_ref[0] ^ step
        start = pl.multiple_of(dest * (features // ranks) + head * width, 128)
        for i, array in enumerate(arrays):
            copies.append(
                pltpu.make_async_copy(
                    array.at[:, pl.ds(start, width)], outs[n].at[i], sems.at[n, i]
                )
            )
    for copy in copies:
        copy.start()
    for copy in copies:
        copy.wait()


def unpack_kernel(me_ref, *refs, ranks, heads):
    pieces, outs, buffers, sems = refs[: ranks * heads], refs[ranks * heads : -2], refs[-2], refs[-1]
    features, width = outs[0].shape[1], pieces[0].shape[2]
    copies = []
    for i, out in enumerate(outs):
        for head in range(heads):
            for step in range(ranks):
                dest = me_ref[0] ^ step
                start = pl.multiple_of(dest * (features // ranks) + head * width, 128)
                buffers[i, :, pl.ds(start, width)] = pieces[head * ranks + step][i]
        copies.append(pltpu.make_async_copy(buffers.at[i], out, sems.at[i]))
        copies[-1].start()
    for copy in copies:
        copy.wait()


def attention_kernel(bias_ref, *refs, ranks, tokens, scale):
    got, sent = refs[:ranks], refs[ranks:]
    f32, bf16 = jnp.float32, jnp.bfloat16
    length = ranks * tokens
    tile = min(QUERY_TILE, length)

    def whole(i):
        return jnp.concatenate([piece[i] for piece in got], axis=0)

    def dot(a, b):
        return jnp.dot(a, b, preferred_element_type=f32)

    def give(i, first, value):
        for r in range(value.shape[0] // tokens):
            sent[first // tokens + r][i] = value[r * tokens : (r + 1) * tokens]

    query, key, val, dout = (whole(i) for i in range(4))
    key_t, val_t = key.T, val.T
    dkey = dval = None
    for first in range(0, length, tile):
        q = query[first : first + tile]
        g = dout[first : first + tile]
        g_t = g.T
        scores = dot(key, q.T).reshape(-1, BLOCK, tile)
        bias = bias_ref[:, first : first + tile]
        scores = (scores + bias[:, None, :]).reshape(length, tile)
        top = jnp.max(scores, axis=0, keepdims=True)
        expo = jnp.exp((scores - top) * scale)
        prob = expo * (1.0 / jnp.sum(expo, axis=0, keepdims=True))
        prob_b = prob.astype(bf16)
        out_t = dot(val_t, prob_b).astype(bf16)
        delta = jnp.sum(g_t.astype(f32) * out_t.astype(f32), axis=0, keepdims=True)
        dscore = (prob * (dot(val, g_t) - delta)).astype(bf16)
        dquery_t = (dot(key_t, dscore) * scale).astype(bf16)
        give(0, first, out_t.T)
        give(1, first, dquery_t.T)
        dk, dv = dot(dscore, q), dot(prob_b, g)
        dkey = dk if dkey is None else dkey + dk
        dval = dv if dval is None else dval + dv
    give(2, 0, (dkey * scale).astype(bf16))
    give(3, 0, dval.astype(bf16))


def block_bias(rand_blocks, glob_blocks, me, ranks, local_blocks):
    total = ranks * local_blocks
    ids = jnp.arange(total, dtype=jnp.int32)
    order = (me ^ ids // local_blocks) * local_blocks + ids % local_blocks
    rand = jnp.take(rand_blocks, order, axis=0)
    gap = (order[:, None] - order[None, :]) % total
    near = (gap <= 1) | (gap == total - 1)
    glob = jnp.any(order[:, None] == glob_blocks[None, :], axis=1)
    picked = jnp.any(order[:, None, None] == rand[None, :, :], axis=2)
    allowed = near | glob[:, None] | picked
    bias = jnp.where(allowed, 0.0, -jnp.inf).astype(jnp.float32)
    return jnp.repeat(bias, BLOCK, axis=1)


def local(queries, keys, values, grad_out, rand_blocks, glob_blocks):
    ranks = lax.axis_size("ctx")
    me = lax.axis_index("ctx")
    tokens, features = queries.shape[1], queries.shape[2]
    head_dim = features // HEADS
    heads = HEADS // ranks
    me_arr = jnp.reshape(me, (1,)).astype(jnp.int32)
    arrays = [
        pltpu.with_memory_space_constraint(x[0], pltpu.HBM)
        for x in (queries, keys, values, grad_out)
    ]
    piece = pltpu.VMEM((4, tokens, head_dim), jnp.bfloat16)
    full = jax.ShapeDtypeStruct((tokens, features), jnp.bfloat16)

    def on_chip(xs):
        return [pltpu.with_memory_space_constraint(x, pltpu.VMEM) for x in xs]

    def pack(wanted):
        pieces = pl.pallas_call(
            functools.partial(pack_kernel, ranks=ranks, wanted=wanted),
            out_shape=[piece] * len(wanted),
            in_specs=[SMEM] + [ANY] * 4,
            out_specs=[VMEM] * len(wanted),
            scratch_shapes=[pltpu.SemaphoreType.DMA((len(wanted), 4))],
            compiler_params=PARAMS,
        )(me_arr, *arrays)
        return dict(zip(wanted, pieces))

    def permute(x, step):
        return lax.ppermute(x, "ctx", [(j, j ^ step) for j in range(ranks)])

    def attend(got):
        return pl.pallas_call(
            functools.partial(
                attention_kernel, ranks=ranks, tokens=tokens, scale=head_dim ** (-0.5)
            ),
            out_shape=[piece] * ranks,
            in_specs=[VMEM] * (1 + ranks),
            out_specs=[VMEM] * ranks,
            compiler_params=PARAMS,
        )(bias, *on_chip(got))

    slots = [(head, step) for head in range(heads) for step in range(ranks)]
    early = [(0, step) for step in range(1, ranks)]
    pieces = pack(early)
    pieces.update(pack([slot for slot in slots if slot not in early]))
    got = {
        slot: permute(pieces[slot], slot[1]) if slot[1] else pieces[slot] for slot in slots
    }
    bias = block_bias(rand_blocks[0], glob_blocks[0], me, ranks, tokens // BLOCK)
    back = []
    for head in range(heads):
        sent = attend([got[head, step] for step in range(ranks)])
        back += [permute(x, step) if step else x for step, x in enumerate(sent)]
    outs = pl.pallas_call(
        functools.partial(unpack_kernel, ranks=ranks, heads=heads),
        out_shape=[full] * 4,
        in_specs=[SMEM] + [VMEM] * len(back),
        out_specs=[ANY] * 4,
        scratch_shapes=[
            pltpu.VMEM((4, tokens, features), jnp.bfloat16),
            pltpu.SemaphoreType.DMA((4,)),
        ],
        compiler_params=PARAMS,
    )(me_arr, *on_chip(back))
    return tuple(x[None] for x in outs)


def solution(mesh):
    wide = P(("groups", "dp"), "ctx", None)
    return jax.shard_map(
        local,
        mesh=mesh,
        in_specs=(wide,) * 4 + (P(("groups", "dp"), None, None), P(("groups", "dp"), None)),
        out_specs=(wide,) * 4,
        check_vma=False,
    )
```

time: 207 us -> 98.2 us (0.47)
  Pallas kernels: 105 us -> 9.82 us
  waiting for transfers between devices: 84 us -> 44.2 us
  starting transfers between devices: 9.01 us -> 39.5 us
  local copies, waits for them, and re-layouts: 4.37 us -> 2.18 us
    pallas_call x3 -> x7, Pallas kernels: 105 us -> 9.82 us  [the longest x4 5.41 us: attend(): pl.pallas_call(functools.partial(attention_kernel, ranks=ranks, tokens=to...]
    ppermute x6 -> x24, waiting for transfers between devices: 84 us -> 44.2 us  [permute(): return lax.ppermute(x, 'ctx', [(j, j ^ step) for j in range(ranks)])]
    ppermute x6 -> x24, starting transfers between devices: 9.01 us -> 39.5 us  [permute(): return lax.ppermute(x, 'ctx', [(j, j ^ step) for j in range(ranks)])]
  transfers between devices with their start and end apart: 6 -> 24, of which waited for: 5 -> 14; matrix products, arithmetic and copies ran while one was open for 1% -> 1% of each run, Pallas kernels for 0% -> 8%
where the time goes in v3:
time: 98.2 us; the launch traced here: 96.8 us
  waiting for transfers between devices  44.2 us (45%)
  starting transfers between devices  39.5 us (40%)
  Pallas kernels  9.82 us (10%)
  local copies, waits for them, and re-layouts  2.18 us (2%)
    ppermute x24, waiting for transfers between devices, permute(): return lax.ppermute(x, 'ctx', [(j, j ^ step) for j in range(ranks)])  44.2 us
    ppermute x24, starting transfers between devices, permute(): return lax.ppermute(x, 'ctx', [(j, j ^ step) for j in range(ranks)])  39.5 us
    pallas_call x4, Pallas kernels, attend(): pl.pallas_call(functools.partial(attention_kernel, ranks=ranks, tokens=to...  5.41 us
    pallas_call x2, Pallas kernels, pack(): pl.pallas_call(functools.partial(pack_kernel, ranks=ranks, wanted=wanted)...  2.92 us
  transfers between devices with their start and end apart: 24, of which 14 were waited for; matrix products, arithmetic and copies ran while one was open for 1% of the time, Pallas kernels for 8%

profile of v3, /device:TPU:18, one launch (start us, length us, event | category | flops | bytes accessed | tf_op | source)
XLA Modules:
  0.0 96.8 jit_solution(10991824347538604745)
XLA Ops:
  0.6 1.1 %shard_map.94 = (bf16[4,128,128]{2,1,0:T(8,128)(2,1)S(1)}, bf16[4,128,128]{2,1,0:T(8,128)(2,1)S(1)}, bf16[4,128,128]{2,1,0:T(8,128)(2,1)S(1)}) custom-call(s32[1]{0:T(128)} %bitcast.me_ref, bf16[128,2048]{1,0:T(8,128)(2,1)} %bitcast.13, bf16[128,2048]{1,0:T(8,128)(2,1)} %bitcast.15, bf16[128,2048]{1,0:T(8,128)(2,1)} %bitcast.17, bf16[128,2048]{1,0:T(8,128)(2,1)} %bitcast.19), custom_call_target="tpu_custom_call" | custom-call | tf_op jit(solution)/shard_map/pallas_call | solution.py:129
  1.7 1.6 %collective-permute-start = (bf16[4,128,128]{2,1,0:T(8,128)(2,1)S(1)}, bf16[4,128,128]{2,1,0:T(8,128)(2,1)S(1)}, u32[]{:S(2)}, u32[]{:S(2)}) collective-permute-start(bf16[4,128,128]{2,1,0:T(8,128)(2,1)S(1)} %get-tuple-element.41), channel_id=1, source_target_pairs={{0,4},{4,0},{8,12},{12,8},{1,5},{5,1},{9,13},{13,9},{2,6},{6,2},{1... | collective-permute-start | bytes 393224 | tf_op jit(solution)/shard_map/ppermute | solution.py:140
  3.3 0.3 collective-permute-start.1
  3.7 1.6 %collective-permute-start.2 = (bf16[4,128,128]{2,1,0:T(8,128)(2,1)S(1)}, bf16[4,128,128]{2,1,0:T(8,128)(2,1)S(1)}, u32[]{:S(2)}, u32[]{:S(2)}) collective-permute-start(bf16[4,128,128]{2,1,0:T(8,128)(2,1)S(1)} %get-tuple-element.43), channel_id=1, source_target_pairs={{0,12},{4,8},{8,4},{12,0},{1,13},{5,9},{9,5},{13,1},{2,14},{6,10},... | collective-permute-start | bytes 393224 | tf_op jit(solution)/shard_map/ppermute | solution.py:140
  5.2 1.9 %shard_map.93 = (bf16[4,128,128]{2,1,0:T(8,128)(2,1)S(1)}, bf16[4,128,128]{2,1,0:T(8,128)(2,1)S(1)}, bf16[4,128,128]{2,1,0:T(8,128)(2,1)S(1)}, bf16[4,128,128]{2...) custom-call(s32[1]{0:T(128)} %bitcast.me_ref, ...), custom_call_target="tpu_custom_call" | custom-call | tf_op jit(solution)/shard_map/pallas_call | solution.py:129
  7.1 2.5 %collective-permute-start.6 = (bf16[4,128,128]{2,1,0:T(8,128)(2,1)S(1)}, bf16[4,128,128]{2,1,0:T(8,128)(2,1)S(1)}, u32[]{:S(2)}, u32[]{:S(2)}) collective-permute-start(bf16[4,128,128]{2,1,0:T(8,128)(2,1)S(1)} %get-tuple-element.49), channel_id=1, source_target_pairs={{0,4},{4,0},{8,12},{12,8},{1,5},{5,1},{9,13},{13,9},{2,6},{6,2},{1... | collective-permute-start | bytes 393224 | tf_op jit(solution)/shard_map/ppermute | solution.py:140
  9.7 0.0 copy-start
  9.7 0.7 copy-done
  10.4 0.1 copy.13
  10.5 0.6 gather_fusion
  11.0 0.1 broadcast_select_fusion
  11.1 0.7 copy-done.1
  11.8 0.1 compare_reduce_fusion.1
  11.8 0.1 copy.12
  11.9 0.1 compare_reduce_fusion
  12.0 1.6 %collective-permute-start.8 = (bf16[4,128,128]{2,1,0:T(8,128)(2,1)S(1)}, bf16[4,128,128]{2,1,0:T(8,128)(2,1)S(1)}, u32[]{:S(2)}, u32[]{:S(2)}) collective-permute-start(bf16[4,128,128]{2,1,0:T(8,128)(2,1)S(1)} %get-tuple-element.51), channel_id=1, source_target_pairs={{0,12},{4,8},{8,4},{12,0},{1,13},{5,9},{9,5},{13,1},{2,14},{6,10},... | collective-permute-start | bytes 393224 | tf_op jit(solution)/shard_map/ppermute | solution.py:140
  13.6 3.7 %collective-permute-start.12 = (bf16[4,128,128]{2,1,0:T(8,128)(2,1)S(1)}, bf16[4,128,128]{2,1,0:T(8,128)(2,1)S(1)}, u32[]{:S(2)}, u32[]{:S(2)}) collective-permute-start(bf16[4,128,128]{2,1,0:T(8,128)(2,1)S(1)} %get-tuple-element.57), channel_id=1, source_target_pairs={{0,4},{4,0},{8,12},{12,8},{1,5},{5,1},{9,13},{13,9},{2,6},{6,2},{1... | collective-permute-start | bytes 393224 | tf_op jit(solution)/shard_map/ppermute | solution.py:140
  17.3 6.9 %collective-permute-done.2.refs_3_ = bf16[4,128,128]{2,1,0:T(8,128)(2,1)S(1)} collective-permute-done((bf16[4,128,128]{2,1,0:T(8,128)(2,1)S(1)}, bf16[4,128,128]{2,1,0:T(8,128)(2,1)S(1)}, u32[]{:S(2)}, u32[]{:S(2)}) %collective-permute-start.2) | collective-permute-done | bytes 131104 | tf_op jit(solution)/shard_map/ppermute | solution.py:140
  24.2 0.1 or_select_fusion
  24.3 0.1 broadcast_in_dim.38
  24.4 0.1 reshape.148.bias_ref
  24.5 1.4 %shard_map.95 = (bf16[4,128,128]{2,1,0:T(8,128)(2,1)S(1)}, bf16[4,128,128]{2,1,0:T(8,128)(2,1)S(1)}, bf16[4,128,128]{2,1,0:T(8,128)(2,1)S(1)}, bf16[4,128,128]{2,1,0:T(8,128)(2,1)S(1)}) custom-call(f32[8,512]{1,0:T(8,128)S(1)} %reshape.148.bias_ref, bf16[4,128,128]{2,1,0:T(8,128)(2,1)S(1)} %get-tuple-element.40.refs_0_, ...), custom_call_target="tpu_custom_call" | custom-call | tf_op jit(solution)/shard_map/pallas_call | solution.py:143
  25.8 2.3 %collective-permute-done.7.refs_2_ = bf16[4,128,128]{2,1,0:T(8,128)(2,1)S(1)} collective-permute-done((bf16[4,128,128]{2,1,0:T(8,128)(2,1)S(1)}, bf16[4,128,128]{2,1,0:T(8,128)(2,1)S(1)}, u32[]{:S(2)}, u32[]{:S(2)}) %collective-permute-start.7) | collective-permute-done | bytes 131104 | tf_op jit(solution)/shard_map/ppermute | solution.py:140
  28.1 5.3 %collective-permute-start.18 = (bf16[4,128,128]{2,1,0:T(8,128)(2,1)S(1)}, bf16[4,128,128]{2,1,0:T(8,128)(2,1)S(1)}, u32[]{:S(2)}, u32[]{:S(2)}) collective-permute-start(bf16[4,128,128]{2,1,0:T(8,128)(2,1)S(1)} %get-tuple-element.65), channel_id=1, source_target_pairs={{0,4},{4,0},{8,12},{12,8},{1,5},{5,1},{9,13},{13,9},{2,6},{6,2},{1... | collective-permute-start | bytes 393224 | tf_op jit(solution)/shard_map/ppermute | solution.py:140
  33.4 1.3 %collective-permute-done.8.refs_3_ = bf16[4,128,128]{2,1,0:T(8,128)(2,1)S(1)} collective-permute-done((bf16[4,128,128]{2,1,0:T(8,128)(2,1)S(1)}, bf16[4,128,128]{2,1,0:T(8,128)(2,1)S(1)}, u32[]{:S(2)}, u32[]{:S(2)}) %collective-permute-start.8) | collective-permute-done | bytes 131104 | tf_op jit(solution)/shard_map/ppermute | solution.py:140
  34.8 0.6 collective-permute-start.20
  35.4 4.0 %collective-permute-done.13.refs_2_ = bf16[4,128,128]{2,1,0:T(8,128)(2,1)S(1)} collective-permute-done((bf16[4,128,128]{2,1,0:T(8,128)(2,1)S(1)}, bf16[4,128,128]{2,1,0:T(8,128)(2,1)S(1)}, u32[]{:S(2)}, u32[]{:S(2)}) %collective-permute-start.13) | collective-permute-done | bytes 131104 | tf_op jit(solution)/shard_map/ppermute | solution.py:140
  39.4 5.2 %collective-permute-start.3 = (bf16[4,128,128]{2,1,0:T(8,128)(2,1)S(1)}, bf16[4,128,128]{2,1,0:T(8,128)(2,1)S(1)}, u32[]{:S(2)}, u32[]{:S(2)}) collective-permute-start(bf16[4,128,128]{2,1,0:T(8,128)(2,1)S(1)} %get-tuple-element.45), channel_id=1, source_target_pairs={{0,4},{4,0},{8,12},{12,8},{1,5},{5,1},{9,13},{13,9},{2,6},{6,2},{1... | collective-permute-start | bytes 393224 | tf_op jit(solution)/shard_map/ppermute | solution.py:140
  44.7 1.3 %collective-permute-done.14.refs_3_ = bf16[4,128,128]{2,1,0:T(8,128)(2,1)S(1)} collective-permute-done((bf16[4,128,128]{2,1,0:T(8,128)(2,1)S(1)}, bf16[4,128,128]{2,1,0:T(8,128)(2,1)S(1)}, u32[]{:S(2)}, u32[]{:S(2)}) %collective-permute-start.14) | collective-permute-done | bytes 131104 | tf_op jit(solution)/shard_map/ppermute | solution.py:140
  46.0 1.4 %shard_map.96 = (bf16[4,128,128]{2,1,0:T(8,128)(2,1)S(1)}, bf16[4,128,128]{2,1,0:T(8,128)(2,1)S(1)}, bf16[4,128,128]{2,1,0:T(8,128)(2,1)S(1)}, bf16[4,128,128]{2,1,0:T(8,128)(2,1)S(1)}) custom-call(f32[8,512]{1,0:T(8,128)S(1)} %reshape.148.bias_ref, bf16[4,128,128]{2,1,0:T(8,128)(2,1)S(1)} %get-tuple-element.48.refs_0_, ...), custom_call_target="tpu_custom_call" | custom-call | tf_op jit(solution)/shard_map/pallas_call | solution.py:143
  47.4 1.4 %shard_map.97 = (bf16[4,128,128]{2,1,0:T(8,128)(2,1)S(1)}, bf16[4,128,128]{2,1,0:T(8,128)(2,1)S(1)}, bf16[4,128,128]{2,1,0:T(8,128)(2,1)S(1)}, bf16[4,128,128]{2,1,0:T(8,128)(2,1)S(1)}) custom-call(f32[8,512]{1,0:T(8,128)S(1)} %reshape.148.bias_ref, bf16[4,128,128]{2,1,0:T(8,128)(2,1)S(1)} %get-tuple-element.56.refs_0_, ...), custom_call_target="tpu_custom_call" | custom-call | tf_op jit(solution)/shard_map/pallas_call | solution.py:143
  48.7 0.7 collective-permute-start.5
  49.4 4.8 %collective-permute-start.9 = (bf16[4,128,128]{2,1,0:T(8,128)(2,1)S(1)}, bf16[4,128,128]{2,1,0:T(8,128)(2,1)S(1)}, u32[]{:S(2)}, u32[]{:S(2)}) collective-permute-start(bf16[4,128,128]{2,1,0:T(8,128)(2,1)S(1)} %get-tuple-element.53), channel_id=1, source_target_pairs={{0,4},{4,0},{8,12},{12,8},{1,5},{5,1},{9,13},{13,9},{2,6},{6,2},{1... | collective-permute-start | bytes 393224 | tf_op jit(solution)/shard_map/ppermute | solution.py:140
  54.3 3.2 %collective-permute-done.20.refs_3_ = bf16[4,128,128]{2,1,0:T(8,128)(2,1)S(1)} collective-permute-done((bf16[4,128,128]{2,1,0:T(8,128)(2,1)S(1)}, bf16[4,128,128]{2,1,0:T(8,128)(2,1)S(1)}, u32[]{:S(2)}, u32[]{:S(2)}) %collective-permute-start.20) | collective-permute-done | bytes 131104 | tf_op jit(solution)/shard_map/ppermute | solution.py:140
  57.4 1.8 %collective-permute-start.11 = (bf16[4,128,128]{2,1,0:T(8,128)(2,1)S(1)}, bf16[4,128,128]{2,1,0:T(8,128)(2,1)S(1)}, u32[]{:S(2)}, u32[]{:S(2)}) collective-permute-start(bf16[4,128,128]{2,1,0:T(8,128)(2,1)S(1)} %get-tuple-element.55), channel_id=1, source_target_pairs={{0,12},{4,8},{8,4},{12,0},{1,13},{5,9},{9,5},{13,1},{2,14},{6,10},... | collective-permute-start | bytes 393224 | tf_op jit(solution)/shard_map/ppermute | solution.py:140
  59.3 1.7 %collective-permute-done.4.refs_2_ = bf16[4,128,128]{2,1,0:T(8,128)(2,1)S(1)} collective-permute-done((bf16[4,128,128]{2,1,0:T(8,128)(2,1)S(1)}, bf16[4,128,128]{2,1,0:T(8,128)(2,1)S(1)}, u32[]{:S(2)}, u32[]{:S(2)}) %collective-permute-start.4) | collective-permute-done | bytes 131104 | tf_op jit(solution)/shard_map/ppermute | solution.py:140
  61.0 4.7 %collective-permute-start.15 = (bf16[4,128,128]{2,1,0:T(8,128)(2,1)S(1)}, bf16[4,128,128]{2,1,0:T(8,128)(2,1)S(1)}, u32[]{:S(2)}, u32[]{:S(2)}) collective-permute-start(bf16[4,128,128]{2,1,0:T(8,128)(2,1)S(1)} %get-tuple-element.61), channel_id=1, source_target_pairs={{0,4},{4,0},{8,12},{12,8},{1,5},{5,1},{9,13},{13,9},{2,6},{6,2},{1... | collective-permute-start | bytes 393224 | tf_op jit(solution)/shard_map/ppermute | solution.py:140
  65.7 1.4 %shard_map.98 = (bf16[4,128,128]{2,1,0:T(8,128)(2,1)S(1)}, bf16[4,128,128]{2,1,0:T(8,128)(2,1)S(1)}, bf16[4,128,128]{2,1,0:T(8,128)(2,1)S(1)}, bf16[4,128,128]{2,1,0:T(8,128)(2,1)S(1)}) custom-call(f32[8,512]{1,0:T(8,128)S(1)} %reshape.148.bias_ref, bf16[4,128,128]{2,1,0:T(8,128)(2,1)S(1)} %get-tuple-element.64.refs_0_, ...), custom_call_target="tpu_custom_call" | custom-call | tf_op jit(solution)/shard_map/pallas_call | solution.py:143
  67.1 4.2 %collective-permute-done.5.refs_3_ = bf16[4,128,128]{2,1,0:T(8,128)(2,1)S(1)} collective-permute-done((bf16[4,128,128]{2,1,0:T(8,128)(2,1)S(1)}, bf16[4,128,128]{2,1,0:T(8,128)(2,1)S(1)}, u32[]{:S(2)}, u32[]{:S(2)}) %collective-permute-start.5) | collective-permute-done | bytes 131104 | tf_op jit(solution)/shard_map/ppermute | solution.py:140
  71.3 0.9 collective-permute-done.10.refs_6_
  72.2 3.5 %collective-permute-start.21 = (bf16[4,128,128]{2,1,0:T(8,128)(2,1)S(1)}, bf16[4,128,128]{2,1,0:T(8,128)(2,1)S(1)}, u32[]{:S(2)}, u32[]{:S(2)}) collective-permute-start(bf16[4,128,128]{2,1,0:T(8,128)(2,1)S(1)} %get-tuple-element.69), channel_id=1, source_target_pairs={{0,4},{4,0},{8,12},{12,8},{1,5},{5,1},{9,13},{13,9},{2,6},{6,2},{1... | collective-permute-start | bytes 393224 | tf_op jit(solution)/shard_map/ppermute | solution.py:140
  75.7 5.6 %collective-permute-done.11.refs_7_ = bf16[4,128,128]{2,1,0:T(8,128)(2,1)S(1)} collective-permute-done((bf16[4,128,128]{2,1,0:T(8,128)(2,1)S(1)}, bf16[4,128,128]{2,1,0:T(8,128)(2,1)S(1)}, u32[]{:S(2)}, u32[]{:S(2)}) %collective-permute-start.11) | collective-permute-done | bytes 131104 | tf_op jit(solution)/shard_map/ppermute | solution.py:140
  81.3 1.4 %collective-permute-start.23 = (bf16[4,128,128]{2,1,0:T(8,128)(2,1)S(1)}, bf16[4,128,128]{2,1,0:T(8,128)(2,1)S(1)}, u32[]{:S(2)}, u32[]{:S(2)}) collective-permute-start(bf16[4,128,128]{2,1,0:T(8,128)(2,1)S(1)} %get-tuple-element.71), channel_id=1, source_target_pairs={{0,12},{4,8},{8,4},{12,0},{1,13},{5,9},{9,5},{13,1},{2,14},{6,10},... | collective-permute-start | bytes 393224 | tf_op jit(solution)/shard_map/ppermute | solution.py:140
  82.7 0.8 collective-permute-done.16.refs_10_
  83.5 7.5 %collective-permute-done.17.refs_11_ = bf16[4,128,128]{2,1,0:T(8,128)(2,1)S(1)} collective-permute-done((bf16[4,128,128]{2,1,0:T(8,128)(2,1)S(1)}, bf16[4,128,128]{2,1,0:T(8,128)(2,1)S(1)}, u32[]{:S(2)}, u32[]{:S(2)}) %collective-permute-start.17) | collective-permute-done | bytes 131104 | tf_op jit(solution)/shard_map/ppermute | solution.py:140
  90.9 0.9 collective-permute-done.22.refs_14_
  91.9 3.5 %collective-permute-done.23.refs_15_ = bf16[4,128,128]{2,1,0:T(8,128)(2,1)S(1)} collective-permute-done((bf16[4,128,128]{2,1,0:T(8,128)(2,1)S(1)}, bf16[4,128,128]{2,1,0:T(8,128)(2,1)S(1)}, u32[]{:S(2)}, u32[]{:S(2)}) %collective-permute-start.23) | collective-permute-done | bytes 131104 | tf_op jit(solution)/shard_map/ppermute | solution.py:140
  95.3 1.5 %shard_map.99 = (bf16[128,2048]{1,0:T(8,128)(2,1)}, bf16[128,2048]{1,0:T(8,128)(2,1)}, bf16[128,2048]{1,0:T(8,128)(2,1)}, bf16[128,2048]{1,0:T(8,128)(2,1)}) custom-call(s32[1]{0:T(128)} %bitcast.me_ref, bf16[4,128,128]{2,1,0:T(8,128)(2,1)S(1)} %get-tuple-element.44.refs_0_, bf16[4,128,128]{2,1,0:T(8,128)(2,1)S(1)} %collective-permute-done.3.refs_1_, ...), custom_call_target="tpu_custom_call" | custom-call | tf_op jit(solution)/shard_map/pallas_call | solution.py:165
  (24 shorter events, 0.1 us)
Async XLA Ops:
  1.7 10.3 %collective-permute-start = (bf16[4,128,128]{2,1,0:T(8,128)(2,1)S(1)}, bf16[4,128,128]{2,1,0:T(8,128)(2,1)S(1)}, u32[]{:S(2)}, u32[]{:S(2)}) collective-permute-start(bf16[4,128,128]{2,1,0:T(8,128)(2,1)S(1)} %get-tuple-element.41), channel_id=1, source_target_pairs={{0,4},{4,0},{8,12},{12,8},{1,5},{5,1},{9,13},{13,9},{2,6},{6,2},{1... | collective-permute-start | bytes 393224 | tf_op jit(solution)/shard_map/ppermute | solution.py:140
  3.3 10.2 %collective-permute-start.1 = (bf16[4,128,128]{2,1,0:T(8,128)(2,1)S(1)}, bf16[4,128,128]{2,1,0:T(8,128)(2,1)S(1)}, u32[]{:S(2)}, u32[]{:S(2)}) collective-permute-start(bf16[4,128,128]{2,1,0:T(8,128)(2,1)S(1)} %get-tuple-element.42), channel_id=1, source_target_pairs={{0,8},{4,12},{8,0},{12,4},{1,9},{5,13},{9,1},{13,5},{2,10},{6,14},... | collective-permute-start | bytes 393224 | tf_op jit(solution)/shard_map/ppermute | solution.py:140
  3.7 20.5 %collective-permute-start.2 = (bf16[4,128,128]{2,1,0:T(8,128)(2,1)S(1)}, bf16[4,128,128]{2,1,0:T(8,128)(2,1)S(1)}, u32[]{:S(2)}, u32[]{:S(2)}) collective-permute-start(bf16[4,128,128]{2,1,0:T(8,128)(2,1)S(1)} %get-tuple-element.43), channel_id=1, source_target_pairs={{0,12},{4,8},{8,4},{12,0},{1,13},{5,9},{9,5},{13,1},{2,14},{6,10},... | collective-permute-start | bytes 393224 | tf_op jit(solution)/shard_map/ppermute | solution.py:140
  7.1 17.1 %collective-permute-start.6 = (bf16[4,128,128]{2,1,0:T(8,128)(2,1)S(1)}, bf16[4,128,128]{2,1,0:T(8,128)(2,1)S(1)}, u32[]{:S(2)}, u32[]{:S(2)}) collective-permute-start(bf16[4,128,128]{2,1,0:T(8,128)(2,1)S(1)} %get-tuple-element.49), channel_id=1, source_target_pairs={{0,4},{4,0},{8,12},{12,8},{1,5},{5,1},{9,13},{13,9},{2,6},{6,2},{1... | collective-permute-start | bytes 393224 | tf_op jit(solution)/shard_map/ppermute | solution.py:140
  9.7 18.4 %collective-permute-start.7 = (bf16[4,128,128]{2,1,0:T(8,128)(2,1)S(1)}, bf16[4,128,128]{2,1,0:T(8,128)(2,1)S(1)}, u32[]{:S(2)}, u32[]{:S(2)}) collective-permute-start(bf16[4,128,128]{2,1,0:T(8,128)(2,1)S(1)} %get-tuple-element.50), channel_id=1, source_target_pairs={{0,8},{4,12},{8,0},{12,4},{1,9},{5,13},{9,1},{13,5},{2,10},{6,14},... | collective-permute-start | bytes 393224 | tf_op jit(solution)/shard_map/ppermute | solution.py:140
  9.7 0.7 copy-start
  11.1 0.7 copy-start.1
  12.0 22.8 %collective-permute-start.8 = (bf16[4,128,128]{2,1,0:T(8,128)(2,1)S(1)}, bf16[4,128,128]{2,1,0:T(8,128)(2,1)S(1)}, u32[]{:S(2)}, u32[]{:S(2)}) collective-permute-start(bf16[4,128,128]{2,1,0:T(8,128)(2,1)S(1)} %get-tuple-element.51), channel_id=1, source_target_pairs={{0,12},{4,8},{8,4},{12,0},{1,13},{5,9},{9,5},{13,1},{2,14},{6,10},... | collective-permute-start | bytes 393224 | tf_op jit(solution)/shard_map/ppermute | solution.py:140
  13.6 21.2 %collective-permute-start.12 = (bf16[4,128,128]{2,1,0:T(8,128)(2,1)S(1)}, bf16[4,128,128]{2,1,0:T(8,128)(2,1)S(1)}, u32[]{:S(2)}, u32[]{:S(2)}) collective-permute-start(bf16[4,128,128]{2,1,0:T(8,128)(2,1)S(1)} %get-tuple-element.57), channel_id=1, source_target_pairs={{0,4},{4,0},{8,12},{12,8},{1,5},{5,1},{9,13},{13,9},{2,6},{6,2},{1... | collective-permute-start | bytes 393224 | tf_op jit(solution)/shard_map/ppermute | solution.py:140
  24.2 15.2 %collective-permute-start.13 = (bf16[4,128,128]{2,1,0:T(8,128)(2,1)S(1)}, bf16[4,128,128]{2,1,0:T(8,128)(2,1)S(1)}, u32[]{:S(2)}, u32[]{:S(2)}) collective-permute-start(bf16[4,128,128]{2,1,0:T(8,128)(2,1)S(1)} %get-tuple-element.58), channel_id=1, source_target_pairs={{0,8},{4,12},{8,0},{12,4},{1,9},{5,13},{9,1},{13,5},{2,10},{6,14},... | collective-permute-start | bytes 393224 | tf_op jit(solution)/shard_map/ppermute | solution.py:140
  24.2 21.8 %collective-permute-start.14 = (bf16[4,128,128]{2,1,0:T(8,128)(2,1)S(1)}, bf16[4,128,128]{2,1,0:T(8,128)(2,1)S(1)}, u32[]{:S(2)}, u32[]{:S(2)}) collective-permute-start(bf16[4,128,128]{2,1,0:T(8,128)(2,1)S(1)} %get-tuple-element.59), channel_id=1, source_target_pairs={{0,12},{4,8},{8,4},{12,0},{1,13},{5,9},{9,5},{13,1},{2,14},{6,10},... | collective-permute-start | bytes 393224 | tf_op jit(solution)/shard_map/ppermute | solution.py:140
  28.1 20.6 %collective-permute-start.18 = (bf16[4,128,128]{2,1,0:T(8,128)(2,1)S(1)}, bf16[4,128,128]{2,1,0:T(8,128)(2,1)S(1)}, u32[]{:S(2)}, u32[]{:S(2)}) collective-permute-start(bf16[4,128,128]{2,1,0:T(8,128)(2,1)S(1)} %get-tuple-element.65), channel_id=1, source_target_pairs={{0,4},{4,0},{8,12},{12,8},{1,5},{5,1},{9,13},{13,9},{2,6},{6,2},{1... | collective-permute-start | bytes 393224 | tf_op jit(solution)/shard_map/ppermute | solution.py:140
  34.8 14.7 %collective-permute-start.19 = (bf16[4,128,128]{2,1,0:T(8,128)(2,1)S(1)}, bf16[4,128,128]{2,1,0:T(8,128)(2,1)S(1)}, u32[]{:S(2)}, u32[]{:S(2)}) collective-permute-start(bf16[4,128,128]{2,1,0:T(8,128)(2,1)S(1)} %get-tuple-element.66), channel_id=1, source_target_pairs={{0,8},{4,12},{8,0},{12,4},{1,9},{5,13},{9,1},{13,5},{2,10},{6,14},... | collective-permute-start | bytes 393224 | tf_op jit(solution)/shard_map/ppermute | solution.py:140
  34.8 22.7 %collective-permute-start.20 = (bf16[4,128,128]{2,1,0:T(8,128)(2,1)S(1)}, bf16[4,128,128]{2,1,0:T(8,128)(2,1)S(1)}, u32[]{:S(2)}, u32[]{:S(2)}) collective-permute-start(bf16[4,128,128]{2,1,0:T(8,128)(2,1)S(1)} %get-tuple-element.67), channel_id=1, source_target_pairs={{0,12},{4,8},{8,4},{12,0},{1,13},{5,9},{9,5},{13,1},{2,14},{6,10},... | collective-permute-start | bytes 393224 | tf_op jit(solution)/shard_map/ppermute | solution.py:140
  39.4 18.0 %collective-permute-start.3 = (bf16[4,128,128]{2,1,0:T(8,128)(2,1)S(1)}, bf16[4,128,128]{2,1,0:T(8,128)(2,1)S(1)}, u32[]{:S(2)}, u32[]{:S(2)}) collective-permute-start(bf16[4,128,128]{2,1,0:T(8,128)(2,1)S(1)} %get-tuple-element.45), channel_id=1, source_target_pairs={{0,4},{4,0},{8,12},{12,8},{1,5},{5,1},{9,13},{13,9},{2,6},{6,2},{1... | collective-permute-start | bytes 393224 | tf_op jit(solution)/shard_map/ppermute | solution.py:140
  46.0 15.0 %collective-permute-start.4 = (bf16[4,128,128]{2,1,0:T(8,128)(2,1)S(1)}, bf16[4,128,128]{2,1,0:T(8,128)(2,1)S(1)}, u32[]{:S(2)}, u32[]{:S(2)}) collective-permute-start(bf16[4,128,128]{2,1,0:T(8,128)(2,1)S(1)} %get-tuple-element.46), channel_id=1, source_target_pairs={{0,8},{4,12},{8,0},{12,4},{1,9},{5,13},{9,1},{13,5},{2,10},{6,14},... | collective-permute-start | bytes 393224 | tf_op jit(solution)/shard_map/ppermute | solution.py:140
  48.7 22.6 %collective-permute-start.5 = (bf16[4,128,128]{2,1,0:T(8,128)(2,1)S(1)}, bf16[4,128,128]{2,1,0:T(8,128)(2,1)S(1)}, u32[]{:S(2)}, u32[]{:S(2)}) collective-permute-start(bf16[4,128,128]{2,1,0:T(8,128)(2,1)S(1)} %get-tuple-element.47), channel_id=1, source_target_pairs={{0,12},{4,8},{8,4},{12,0},{1,13},{5,9},{9,5},{13,1},{2,14},{6,10},... | collective-permute-start | bytes 393224 | tf_op jit(solution)/shard_map/ppermute | solution.py:140
  49.4 21.9 %collective-permute-start.9 = (bf16[4,128,128]{2,1,0:T(8,128)(2,1)S(1)}, bf16[4,128,128]{2,1,0:T(8,128)(2,1)S(1)}, u32[]{:S(2)}, u32[]{:S(2)}) collective-permute-start(bf16[4,128,128]{2,1,0:T(8,128)(2,1)S(1)} %get-tuple-element.53), channel_id=1, source_target_pairs={{0,4},{4,0},{8,12},{12,8},{1,5},{5,1},{9,13},{13,9},{2,6},{6,2},{1... | collective-permute-start | bytes 393224 | tf_op jit(solution)/shard_map/ppermute | solution.py:140
  57.4 14.8 %collective-permute-start.10 = (bf16[4,128,128]{2,1,0:T(8,128)(2,1)S(1)}, bf16[4,128,128]{2,1,0:T(8,128)(2,1)S(1)}, u32[]{:S(2)}, u32[]{:S(2)}) collective-permute-start(bf16[4,128,128]{2,1,0:T(8,128)(2,1)S(1)} %get-tuple-element.54), channel_id=1, source_target_pairs={{0,8},{4,12},{8,0},{12,4},{1,9},{5,13},{9,1},{13,5},{2,10},{6,14},... | collective-permute-start | bytes 393224 | tf_op jit(solution)/shard_map/ppermute | solution.py:140
  57.4 23.9 %collective-permute-start.11 = (bf16[4,128,128]{2,1,0:T(8,128)(2,1)S(1)}, bf16[4,128,128]{2,1,0:T(8,128)(2,1)S(1)}, u32[]{:S(2)}, u32[]{:S(2)}) collective-permute-start(bf16[4,128,128]{2,1,0:T(8,128)(2,1)S(1)} %get-tuple-element.55), channel_id=1, source_target_pairs={{0,12},{4,8},{8,4},{12,0},{1,13},{5,9},{9,5},{13,1},{2,14},{6,10},... | collective-permute-start | bytes 393224 | tf_op jit(solution)/shard_map/ppermute | solution.py:140
  61.0 20.3 %collective-permute-start.15 = (bf16[4,128,128]{2,1,0:T(8,128)(2,1)S(1)}, bf16[4,128,128]{2,1,0:T(8,128)(2,1)S(1)}, u32[]{:S(2)}, u32[]{:S(2)}) collective-permute-start(bf16[4,128,128]{2,1,0:T(8,128)(2,1)S(1)} %get-tuple-element.61), channel_id=1, source_target_pairs={{0,4},{4,0},{8,12},{12,8},{1,5},{5,1},{9,13},{13,9},{2,6},{6,2},{1... | collective-permute-start | bytes 393224 | tf_op jit(solution)/shard_map/ppermute | solution.py:140
  71.3 12.2 %collective-permute-start.16 = (bf16[4,128,128]{2,1,0:T(8,128)(2,1)S(1)}, bf16[4,128,128]{2,1,0:T(8,128)(2,1)S(1)}, u32[]{:S(2)}, u32[]{:S(2)}) collective-permute-start(bf16[4,128,128]{2,1,0:T(8,128)(2,1)S(1)} %get-tuple-element.62), channel_id=1, source_target_pairs={{0,8},{4,12},{8,0},{12,4},{1,9},{5,13},{9,1},{13,5},{2,10},{6,14},... | collective-permute-start | bytes 393224 | tf_op jit(solution)/shard_map/ppermute | solution.py:140
  71.3 19.7 %collective-permute-start.17 = (bf16[4,128,128]{2,1,0:T(8,128)(2,1)S(1)}, bf16[4,128,128]{2,1,0:T(8,128)(2,1)S(1)}, u32[]{:S(2)}, u32[]{:S(2)}) collective-permute-start(bf16[4,128,128]{2,1,0:T(8,128)(2,1)S(1)} %get-tuple-element.63), channel_id=1, source_target_pairs={{0,12},{4,8},{8,4},{12,0},{1,13},{5,9},{9,5},{13,1},{2,14},{6,10},... | collective-permute-start | bytes 393224 | tf_op jit(solution)/shard_map/ppermute | solution.py:140
  72.2 18.7 %collective-permute-start.21 = (bf16[4,128,128]{2,1,0:T(8,128)(2,1)S(1)}, bf16[4,128,128]{2,1,0:T(8,128)(2,1)S(1)}, u32[]{:S(2)}, u32[]{:S(2)}) collective-permute-start(bf16[4,128,128]{2,1,0:T(8,128)(2,1)S(1)} %get-tuple-element.69), channel_id=1, source_target_pairs={{0,4},{4,0},{8,12},{12,8},{1,5},{5,1},{9,13},{13,9},{2,6},{6,2},{1... | collective-permute-start | bytes 393224 | tf_op jit(solution)/shard_map/ppermute | solution.py:140
  81.3 10.6 %collective-permute-start.22 = (bf16[4,128,128]{2,1,0:T(8,128)(2,1)S(1)}, bf16[4,128,128]{2,1,0:T(8,128)(2,1)S(1)}, u32[]{:S(2)}, u32[]{:S(2)}) collective-permute-start(bf16[4,128,128]{2,1,0:T(8,128)(2,1)S(1)} %get-tuple-element.70), channel_id=1, source_target_pairs={{0,8},{4,12},{8,0},{12,4},{1,9},{5,13},{9,1},{13,5},{2,10},{6,14},... | collective-permute-start | bytes 393224 | tf_op jit(solution)/shard_map/ppermute | solution.py:140
  81.3 14.0 %collective-permute-start.23 = (bf16[4,128,128]{2,1,0:T(8,128)(2,1)S(1)}, bf16[4,128,128]{2,1,0:T(8,128)(2,1)S(1)}, u32[]{:S(2)}, u32[]{:S(2)}) collective-permute-start(bf16[4,128,128]{2,1,0:T(8,128)(2,1)S(1)} %get-tuple-element.71), channel_id=1, source_target_pairs={{0,12},{4,8},{8,4},{12,0},{1,13},{5,9},{9,5},{13,1},{2,14},{6,10},... | collective-permute-start | bytes 393224 | tf_op jit(solution)/shard_map/ppermute | solution.py:140

commit v4 on v3

--- a/solution.py
+++ b/solution.py
@@ -150,8 +150,9 @@
             compiler_params=PARAMS,
         )(bias, *on_chip(got))
 
-    slots = [(head, step) for head in range(heads) for step in range(ranks)]
-    early = [(0, step) for step in range(1, ranks)]
+    steps = [*range(ranks - 1, -1, -1)]
+    slots = [(head, step) for head in range(heads) for step in steps]
+    early = [(0, step) for step in steps if step > 1]
     pieces = pack(early)
     pieces.update(pack([slot for slot in slots if slot not in early]))
     got = {
@@ -161,7 +162,8 @@
     back = []
     for head in range(heads):
         sent = attend([got[head, step] for step in range(ranks)])
-        back += [permute(x, step) if step else x for step, x in enumerate(sent)]
+        moved = {step: permute(sent[step], step) if step else sent[step] for step in steps}
+        back += [moved[step] for step in range(ranks)]
     outs = pl.pallas_call(
         functools.partial(unpack_kernel, ranks=ranks, heads=heads),
         out_shape=[full] * 4,

time: 98.2 us -> 97.1 us (0.989)
  starting transfers between devices: 39.5 us -> 36.4 us
  waiting for transfers between devices: 44.2 us -> 47 us
    ppermute x24, starting transfers between devices: 39.5 us -> 36.4 us  [permute(): return lax.ppermute(x, 'ctx', [(j, j ^ step) for j in range(ranks)])]
    ppermute x24, waiting for transfers between devices: 44.2 us -> 47 us  [permute(): return lax.ppermute(x, 'ctx', [(j, j ^ step) for j in range(ranks)])]
  transfers between devices with their start and end apart: 24 -> 24, of which waited for: 14 -> 13; matrix products, arithmetic and copies ran while one was open for 1% -> 1% of each run, Pallas kernels for 8% -> 8%
where the time goes in v4:
time: 97.1 us; the launch traced here: 96.5 us
  waiting for transfers between devices  47 us (48%)
  starting transfers between devices  36.4 us (37%)
  Pallas kernels  9.8 us (10%)
  local copies, waits for them, and re-layouts  2.18 us (2%)
    ppermute x24, waiting for transfers between devices, permute(): return lax.ppermute(x, 'ctx', [(j, j ^ step) for j in range(ranks)])  47 us
    ppermute x24, starting transfers between devices, permute(): return lax.ppermute(x, 'ctx', [(j, j ^ step) for j in range(ranks)])  36.4 us
    pallas_call x4, Pallas kernels, attend(): pl.pallas_call(functools.partial(attention_kernel, ranks=ranks, tokens=to...  5.41 us
    pallas_call x2, Pallas kernels, pack(): pl.pallas_call(functools.partial(pack_kernel, ranks=ranks, wanted=wanted)...  2.9 us
  transfers between devices with their start and end apart: 24, of which 13 were waited for; matrix products, arithmetic and copies ran while one was open for 1% of the time, Pallas kernels for 8%

profile of v4, /device:TPU:18, one launch (start us, length us, event | category | flops | bytes accessed | tf_op | source)
XLA Modules:
  0.0 96.5 jit_solution(1086765006659729029)
XLA Ops:
  0.6 1.0 shard_map.94
  1.6 0.4 collective-permute-start.1
  2.0 2.7 %collective-permute-start.2 = (bf16[4,128,128]{2,1,0:T(8,128)(2,1)S(1)}, bf16[4,128,128]{2,1,0:T(8,128)(2,1)S(1)}, u32[]{:S(2)}, u32[]{:S(2)}) collective-permute-start(bf16[4,128,128]{2,1,0:T(8,128)(2,1)S(1)} %get-tuple-element.43), channel_id=1, source_target_pairs={{0,12},{4,8},{8,4},{12,0},{1,13},{5,9},{9,5},{13,1},{2,14},{6,10},... | collective-permute-start | bytes 393224 | tf_op jit(solution)/shard_map/ppermute | solution.py:140
  4.7 1.9 %shard_map.93 = (bf16[4,128,128]{2,1,0:T(8,128)(2,1)S(1)}, bf16[4,128,128]{2,1,0:T(8,128)(2,1)S(1)}, bf16[4,128,128]{2,1,0:T(8,128)(2,1)S(1)}, bf16[4,128,128]{2...) custom-call(s32[1]{0:T(128)} %bitcast.me_ref, ...), custom_call_target="tpu_custom_call" | custom-call | tf_op jit(solution)/shard_map/pallas_call | solution.py:129
  6.7 1.4 %collective-permute-start = (bf16[4,128,128]{2,1,0:T(8,128)(2,1)S(1)}, bf16[4,128,128]{2,1,0:T(8,128)(2,1)S(1)}, u32[]{:S(2)}, u32[]{:S(2)}) collective-permute-start(bf16[4,128,128]{2,1,0:T(8,128)(2,1)S(1)} %get-tuple-element.41), channel_id=1, source_target_pairs={{0,4},{4,0},{8,12},{12,8},{1,5},{5,1},{9,13},{13,9},{2,6},{6,2},{1... | collective-permute-start | bytes 393224 | tf_op jit(solution)/shard_map/ppermute | solution.py:140
  8.1 0.7 collective-permute-start.6
  8.7 1.2 %collective-permute-start.7 = (bf16[4,128,128]{2,1,0:T(8,128)(2,1)S(1)}, bf16[4,128,128]{2,1,0:T(8,128)(2,1)S(1)}, u32[]{:S(2)}, u32[]{:S(2)}) collective-permute-start(bf16[4,128,128]{2,1,0:T(8,128)(2,1)S(1)} %get-tuple-element.50), channel_id=1, source_target_pairs={{0,8},{4,12},{8,0},{12,4},{1,9},{5,13},{9,1},{13,5},{2,10},{6,14},... | collective-permute-start | bytes 393224 | tf_op jit(solution)/shard_map/ppermute | solution.py:140
  10.0 0.0 copy-start
  10.0 0.7 copy-done
  10.7 0.1 copy.13
  10.8 0.6 gather_fusion
  11.3 0.1 broadcast_select_fusion
  11.4 0.7 copy-done.1
  12.1 0.1 compare_reduce_fusion.1
  12.2 0.1 copy.12
  12.2 0.1 compare_reduce_fusion
  12.3 1.6 %collective-permute-start.8 = (bf16[4,128,128]{2,1,0:T(8,128)(2,1)S(1)}, bf16[4,128,128]{2,1,0:T(8,128)(2,1)S(1)}, u32[]{:S(2)}, u32[]{:S(2)}) collective-permute-start(bf16[4,128,128]{2,1,0:T(8,128)(2,1)S(1)} %get-tuple-element.51), channel_id=1, source_target_pairs={{0,12},{4,8},{8,4},{12,0},{1,13},{5,9},{9,5},{13,1},{2,14},{6,10},... | collective-permute-start | bytes 393224 | tf_op jit(solution)/shard_map/ppermute | solution.py:140
  13.9 3.6 %collective-permute-done.2.refs_3_ = bf16[4,128,128]{2,1,0:T(8,128)(2,1)S(1)} collective-permute-done((bf16[4,128,128]{2,1,0:T(8,128)(2,1)S(1)}, bf16[4,128,128]{2,1,0:T(8,128)(2,1)S(1)}, u32[]{:S(2)}, u32[]{:S(2)}) %collective-permute-start.2) | collective-permute-done | bytes 131104 | tf_op jit(solution)/shard_map/ppermute | solution.py:140
  17.5 5.7 %collective-permute-start.13 = (bf16[4,128,128]{2,1,0:T(8,128)(2,1)S(1)}, bf16[4,128,128]{2,1,0:T(8,128)(2,1)S(1)}, u32[]{:S(2)}, u32[]{:S(2)}) collective-permute-start(bf16[4,128,128]{2,1,0:T(8,128)(2,1)S(1)} %get-tuple-element.58), channel_id=1, source_target_pairs={{0,8},{4,12},{8,0},{12,4},{1,9},{5,13},{9,1},{13,5},{2,10},{6,14},... | collective-permute-start | bytes 393224 | tf_op jit(solution)/shard_map/ppermute | solution.py:140
  23.3 0.1 or_select_fusion
  23.3 0.1 broadcast_in_dim.38
  23.4 0.1 reshape.148.bias_ref
  23.5 1.4 %shard_map.95 = (bf16[4,128,128]{2,1,0:T(8,128)(2,1)S(1)}, bf16[4,128,128]{2,1,0:T(8,128)(2,1)S(1)}, bf16[4,128,128]{2,1,0:T(8,128)(2,1)S(1)}, bf16[4,128,128]{2,1,0:T(8,128)(2,1)S(1)}) custom-call(f32[8,512]{1,0:T(8,128)S(1)} %reshape.148.bias_ref, bf16[4,128,128]{2,1,0:T(8,128)(2,1)S(1)} %get-tuple-element.40.refs_0_, ...), custom_call_target="tpu_custom_call" | custom-call | tf_op jit(solution)/shard_map/pallas_call | solution.py:143
  24.9 5.7 %collective-permute-start.18 = (bf16[4,128,128]{2,1,0:T(8,128)(2,1)S(1)}, bf16[4,128,128]{2,1,0:T(8,128)(2,1)S(1)}, u32[]{:S(2)}, u32[]{:S(2)}) collective-permute-start(bf16[4,128,128]{2,1,0:T(8,128)(2,1)S(1)} %get-tuple-element.65), channel_id=1, source_target_pairs={{0,4},{4,0},{8,12},{12,8},{1,5},{5,1},{9,13},{13,9},{2,6},{6,2},{1... | collective-permute-start | bytes 393224 | tf_op jit(solution)/shard_map/ppermute | solution.py:140
  30.5 2.7 %collective-permute-done.8.refs_3_ = bf16[4,128,128]{2,1,0:T(8,128)(2,1)S(1)} collective-permute-done((bf16[4,128,128]{2,1,0:T(8,128)(2,1)S(1)}, bf16[4,128,128]{2,1,0:T(8,128)(2,1)S(1)}, u32[]{:S(2)}, u32[]{:S(2)}) %collective-permute-start.8) | collective-permute-done | bytes 131104 | tf_op jit(solution)/shard_map/ppermute | solution.py:140
  33.3 0.5 collective-permute-start.20
  33.8 0.2 collective-permute-done.13.refs_2_
  34.0 3.7 %collective-permute-start.3 = (bf16[4,128,128]{2,1,0:T(8,128)(2,1)S(1)}, bf16[4,128,128]{2,1,0:T(8,128)(2,1)S(1)}, u32[]{:S(2)}, u32[]{:S(2)}) collective-permute-start(bf16[4,128,128]{2,1,0:T(8,128)(2,1)S(1)} %get-tuple-element.45), channel_id=1, source_target_pairs={{0,4},{4,0},{8,12},{12,8},{1,5},{5,1},{9,13},{13,9},{2,6},{6,2},{1... | collective-permute-start | bytes 393224 | tf_op jit(solution)/shard_map/ppermute | solution.py:140
  37.7 6.9 %collective-permute-done.14.refs_3_ = bf16[4,128,128]{2,1,0:T(8,128)(2,1)S(1)} collective-permute-done((bf16[4,128,128]{2,1,0:T(8,128)(2,1)S(1)}, bf16[4,128,128]{2,1,0:T(8,128)(2,1)S(1)}, u32[]{:S(2)}, u32[]{:S(2)}) %collective-permute-start.14) | collective-permute-done | bytes 131104 | tf_op jit(solution)/shard_map/ppermute | solution.py:140
  44.6 1.4 %shard_map.96 = (bf16[4,128,128]{2,1,0:T(8,128)(2,1)S(1)}, bf16[4,128,128]{2,1,0:T(8,128)(2,1)S(1)}, bf16[4,128,128]{2,1,0:T(8,128)(2,1)S(1)}, bf16[4,128,128]{2,1,0:T(8,128)(2,1)S(1)}) custom-call(f32[8,512]{1,0:T(8,128)S(1)} %reshape.148.bias_ref, bf16[4,128,128]{2,1,0:T(8,128)(2,1)S(1)} %get-tuple-element.48.refs_0_, ...), custom_call_target="tpu_custom_call" | custom-call | tf_op jit(solution)/shard_map/pallas_call | solution.py:143
  45.9 1.4 %shard_map.97 = (bf16[4,128,128]{2,1,0:T(8,128)(2,1)S(1)}, bf16[4,128,128]{2,1,0:T(8,128)(2,1)S(1)}, bf16[4,128,128]{2,1,0:T(8,128)(2,1)S(1)}, bf16[4,128,128]{2,1,0:T(8,128)(2,1)S(1)}) custom-call(f32[8,512]{1,0:T(8,128)S(1)} %reshape.148.bias_ref, bf16[4,128,128]{2,1,0:T(8,128)(2,1)S(1)} %get-tuple-element.56.refs_0_, ...), custom_call_target="tpu_custom_call" | custom-call | tf_op jit(solution)/shard_map/pallas_call | solution.py:143
  47.3 0.5 collective-permute-start.5
  47.8 4.0 %collective-permute-start.9 = (bf16[4,128,128]{2,1,0:T(8,128)(2,1)S(1)}, bf16[4,128,128]{2,1,0:T(8,128)(2,1)S(1)}, u32[]{:S(2)}, u32[]{:S(2)}) collective-permute-start(bf16[4,128,128]{2,1,0:T(8,128)(2,1)S(1)} %get-tuple-element.53), channel_id=1, source_target_pairs={{0,4},{4,0},{8,12},{12,8},{1,5},{5,1},{9,13},{13,9},{2,6},{6,2},{1... | collective-permute-start | bytes 393224 | tf_op jit(solution)/shard_map/ppermute | solution.py:140
  51.8 4.1 %collective-permute-done.20.refs_3_ = bf16[4,128,128]{2,1,0:T(8,128)(2,1)S(1)} collective-permute-done((bf16[4,128,128]{2,1,0:T(8,128)(2,1)S(1)}, bf16[4,128,128]{2,1,0:T(8,128)(2,1)S(1)}, u32[]{:S(2)}, u32[]{:S(2)}) %collective-permute-start.20) | collective-permute-done | bytes 131104 | tf_op jit(solution)/shard_map/ppermute | solution.py:140
  55.8 0.7 collective-permute-done.4.refs_2_
  56.5 3.7 %collective-permute-start.15 = (bf16[4,128,128]{2,1,0:T(8,128)(2,1)S(1)}, bf16[4,128,128]{2,1,0:T(8,128)(2,1)S(1)}, u32[]{:S(2)}, u32[]{:S(2)}) collective-permute-start(bf16[4,128,128]{2,1,0:T(8,128)(2,1)S(1)} %get-tuple-element.61), channel_id=1, source_target_pairs={{0,4},{4,0},{8,12},{12,8},{1,5},{5,1},{9,13},{13,9},{2,6},{6,2},{1... | collective-permute-start | bytes 393224 | tf_op jit(solution)/shard_map/ppermute | solution.py:140
  60.2 1.4 %shard_map.98 = (bf16[4,128,128]{2,1,0:T(8,128)(2,1)S(1)}, bf16[4,128,128]{2,1,0:T(8,128)(2,1)S(1)}, bf16[4,128,128]{2,1,0:T(8,128)(2,1)S(1)}, bf16[4,128,128]{2,1,0:T(8,128)(2,1)S(1)}) custom-call(f32[8,512]{1,0:T(8,128)S(1)} %reshape.148.bias_ref, bf16[4,128,128]{2,1,0:T(8,128)(2,1)S(1)} %get-tuple-element.64.refs_0_, ...), custom_call_target="tpu_custom_call" | custom-call | tf_op jit(solution)/shard_map/pallas_call | solution.py:143
  61.6 5.5 %collective-permute-done.5.refs_3_ = bf16[4,128,128]{2,1,0:T(8,128)(2,1)S(1)} collective-permute-done((bf16[4,128,128]{2,1,0:T(8,128)(2,1)S(1)}, bf16[4,128,128]{2,1,0:T(8,128)(2,1)S(1)}, u32[]{:S(2)}, u32[]{:S(2)}) %collective-permute-start.5) | collective-permute-done | bytes 131104 | tf_op jit(solution)/shard_map/ppermute | solution.py:140
  67.1 0.5 collective-permute-start.17
  67.5 0.2 collective-permute-done.10.refs_6_
  67.7 3.7 %collective-permute-start.21 = (bf16[4,128,128]{2,1,0:T(8,128)(2,1)S(1)}, bf16[4,128,128]{2,1,0:T(8,128)(2,1)S(1)}, u32[]{:S(2)}, u32[]{:S(2)}) collective-permute-start(bf16[4,128,128]{2,1,0:T(8,128)(2,1)S(1)} %get-tuple-element.69), channel_id=1, source_target_pairs={{0,4},{4,0},{8,12},{12,8},{1,5},{5,1},{9,13},{13,9},{2,6},{6,2},{1... | collective-permute-start | bytes 393224 | tf_op jit(solution)/shard_map/ppermute | solution.py:140
  71.4 6.8 %collective-permute-done.11.refs_7_ = bf16[4,128,128]{2,1,0:T(8,128)(2,1)S(1)} collective-permute-done((bf16[4,128,128]{2,1,0:T(8,128)(2,1)S(1)}, bf16[4,128,128]{2,1,0:T(8,128)(2,1)S(1)}, u32[]{:S(2)}, u32[]{:S(2)}) %collective-permute-start.11) | collective-permute-done | bytes 131104 | tf_op jit(solution)/shard_map/ppermute | solution.py:140
  78.3 0.5 collective-permute-start.23
  78.8 0.2 collective-permute-done.16.refs_10_
  79.0 10.5 %collective-permute-done.17.refs_11_ = bf16[4,128,128]{2,1,0:T(8,128)(2,1)S(1)} collective-permute-done((bf16[4,128,128]{2,1,0:T(8,128)(2,1)S(1)}, bf16[4,128,128]{2,1,0:T(8,128)(2,1)S(1)}, u32[]{:S(2)}, u32[]{:S(2)}) %collective-permute-start.17) | collective-permute-done | bytes 131104 | tf_op jit(solution)/shard_map/ppermute | solution.py:140
  89.5 0.8 collective-permute-done.22.refs_14_
  90.3 4.7 %collective-permute-done.23.refs_15_ = bf16[4,128,128]{2,1,0:T(8,128)(2,1)S(1)} collective-permute-done((bf16[4,128,128]{2,1,0:T(8,128)(2,1)S(1)}, bf16[4,128,128]{2,1,0:T(8,128)(2,1)S(1)}, u32[]{:S(2)}, u32[]{:S(2)}) %collective-permute-start.23) | collective-permute-done | bytes 131104 | tf_op jit(solution)/shard_map/ppermute | solution.py:140
  95.0 1.5 %shard_map.99 = (bf16[128,2048]{1,0:T(8,128)(2,1)}, bf16[128,2048]{1,0:T(8,128)(2,1)}, bf16[128,2048]{1,0:T(8,128)(2,1)}, bf16[128,2048]{1,0:T(8,128)(2,1)}) custom-call(s32[1]{0:T(128)} %bitcast.me_ref, bf16[4,128,128]{2,1,0:T(8,128)(2,1)S(1)} %get-tuple-element.44.refs_0_, bf16[4,128,128]{2,1,0:T(8,128)(2,1)S(1)} %collective-permute-done.3.refs_1_, ...), custom_call_target="tpu_custom_call" | custom-call | tf_op jit(solution)/shard_map/pallas_call | solution.py:167
  (24 shorter events, 0.1 us)
Async XLA Ops:
  1.6 10.7 %collective-permute-start.1 = (bf16[4,128,128]{2,1,0:T(8,128)(2,1)S(1)}, bf16[4,128,128]{2,1,0:T(8,128)(2,1)S(1)}, u32[]{:S(2)}, u32[]{:S(2)}) collective-permute-start(bf16[4,128,128]{2,1,0:T(8,128)(2,1)S(1)} %get-tuple-element.42), channel_id=1, source_target_pairs={{0,8},{4,12},{8,0},{12,4},{1,9},{5,13},{9,1},{13,5},{2,10},{6,14},... | collective-permute-start | bytes 393224 | tf_op jit(solution)/shard_map/ppermute | solution.py:140
  2.0 15.5 %collective-permute-start.2 = (bf16[4,128,128]{2,1,0:T(8,128)(2,1)S(1)}, bf16[4,128,128]{2,1,0:T(8,128)(2,1)S(1)}, u32[]{:S(2)}, u32[]{:S(2)}) collective-permute-start(bf16[4,128,128]{2,1,0:T(8,128)(2,1)S(1)} %get-tuple-element.43), channel_id=1, source_target_pairs={{0,12},{4,8},{8,4},{12,0},{1,13},{5,9},{9,5},{13,1},{2,14},{6,10},... | collective-permute-start | bytes 393224 | tf_op jit(solution)/shard_map/ppermute | solution.py:140
  6.7 10.9 %collective-permute-start = (bf16[4,128,128]{2,1,0:T(8,128)(2,1)S(1)}, bf16[4,128,128]{2,1,0:T(8,128)(2,1)S(1)}, u32[]{:S(2)}, u32[]{:S(2)}) collective-permute-start(bf16[4,128,128]{2,1,0:T(8,128)(2,1)S(1)} %get-tuple-element.41), channel_id=1, source_target_pairs={{0,4},{4,0},{8,12},{12,8},{1,5},{5,1},{9,13},{13,9},{2,6},{6,2},{1... | collective-permute-start | bytes 393224 | tf_op jit(solution)/shard_map/ppermute | solution.py:140
  8.1 15.2 %collective-permute-start.6 = (bf16[4,128,128]{2,1,0:T(8,128)(2,1)S(1)}, bf16[4,128,128]{2,1,0:T(8,128)(2,1)S(1)}, u32[]{:S(2)}, u32[]{:S(2)}) collective-permute-start(bf16[4,128,128]{2,1,0:T(8,128)(2,1)S(1)} %get-tuple-element.49), channel_id=1, source_target_pairs={{0,4},{4,0},{8,12},{12,8},{1,5},{5,1},{9,13},{13,9},{2,6},{6,2},{1... | collective-permute-start | bytes 393224 | tf_op jit(solution)/shard_map/ppermute | solution.py:140
  8.7 16.1 %collective-permute-start.7 = (bf16[4,128,128]{2,1,0:T(8,128)(2,1)S(1)}, bf16[4,128,128]{2,1,0:T(8,128)(2,1)S(1)}, u32[]{:S(2)}, u32[]{:S(2)}) collective-permute-start(bf16[4,128,128]{2,1,0:T(8,128)(2,1)S(1)} %get-tuple-element.50), channel_id=1, source_target_pairs={{0,8},{4,12},{8,0},{12,4},{1,9},{5,13},{9,1},{13,5},{2,10},{6,14},... | collective-permute-start | bytes 393224 | tf_op jit(solution)/shard_map/ppermute | solution.py:140
  10.0 0.7 copy-start
  11.4 0.7 copy-start.1
  12.3 21.0 %collective-permute-start.8 = (bf16[4,128,128]{2,1,0:T(8,128)(2,1)S(1)}, bf16[4,128,128]{2,1,0:T(8,128)(2,1)S(1)}, u32[]{:S(2)}, u32[]{:S(2)}) collective-permute-start(bf16[4,128,128]{2,1,0:T(8,128)(2,1)S(1)} %get-tuple-element.51), channel_id=1, source_target_pairs={{0,12},{4,8},{8,4},{12,0},{1,13},{5,9},{9,5},{13,1},{2,14},{6,10},... | collective-permute-start | bytes 393224 | tf_op jit(solution)/shard_map/ppermute | solution.py:140
  17.5 15.8 %collective-permute-start.12 = (bf16[4,128,128]{2,1,0:T(8,128)(2,1)S(1)}, bf16[4,128,128]{2,1,0:T(8,128)(2,1)S(1)}, u32[]{:S(2)}, u32[]{:S(2)}) collective-permute-start(bf16[4,128,128]{2,1,0:T(8,128)(2,1)S(1)} %get-tuple-element.57), channel_id=1, source_target_pairs={{0,4},{4,0},{8,12},{12,8},{1,5},{5,1},{9,13},{13,9},{2,6},{6,2},{1... | collective-permute-start | bytes 393224 | tf_op jit(solution)/shard_map/ppermute | solution.py:140
  17.5 16.5 %collective-permute-start.13 = (bf16[4,128,128]{2,1,0:T(8,128)(2,1)S(1)}, bf16[4,128,128]{2,1,0:T(8,128)(2,1)S(1)}, u32[]{:S(2)}, u32[]{:S(2)}) collective-permute-start(bf16[4,128,128]{2,1,0:T(8,128)(2,1)S(1)} %get-tuple-element.58), channel_id=1, source_target_pairs={{0,8},{4,12},{8,0},{12,4},{1,9},{5,13},{9,1},{13,5},{2,10},{6,14},... | collective-permute-start | bytes 393224 | tf_op jit(solution)/shard_map/ppermute | solution.py:140
  23.3 21.3 %collective-permute-start.14 = (bf16[4,128,128]{2,1,0:T(8,128)(2,1)S(1)}, bf16[4,128,128]{2,1,0:T(8,128)(2,1)S(1)}, u32[]{:S(2)}, u32[]{:S(2)}) collective-permute-start(bf16[4,128,128]{2,1,0:T(8,128)(2,1)S(1)} %get-tuple-element.59), channel_id=1, source_target_pairs={{0,12},{4,8},{8,4},{12,0},{1,13},{5,9},{9,5},{13,1},{2,14},{6,10},... | collective-permute-start | bytes 393224 | tf_op jit(solution)/shard_map/ppermute | solution.py:140
  24.9 22.4 %collective-permute-start.18 = (bf16[4,128,128]{2,1,0:T(8,128)(2,1)S(1)}, bf16[4,128,128]{2,1,0:T(8,128)(2,1)S(1)}, u32[]{:S(2)}, u32[]{:S(2)}) collective-permute-start(bf16[4,128,128]{2,1,0:T(8,128)(2,1)S(1)} %get-tuple-element.65), channel_id=1, source_target_pairs={{0,4},{4,0},{8,12},{12,8},{1,5},{5,1},{9,13},{13,9},{2,6},{6,2},{1... | collective-permute-start | bytes 393224 | tf_op jit(solution)/shard_map/ppermute | solution.py:140
  33.3 14.5 %collective-permute-start.19 = (bf16[4,128,128]{2,1,0:T(8,128)(2,1)S(1)}, bf16[4,128,128]{2,1,0:T(8,128)(2,1)S(1)}, u32[]{:S(2)}, u32[]{:S(2)}) collective-permute-start(bf16[4,128,128]{2,1,0:T(8,128)(2,1)S(1)} %get-tuple-element.66), channel_id=1, source_target_pairs={{0,8},{4,12},{8,0},{12,4},{1,9},{5,13},{9,1},{13,5},{2,10},{6,14},... | collective-permute-start | bytes 393224 | tf_op jit(solution)/shard_map/ppermute | solution.py:140
  33.3 22.5 %collective-permute-start.20 = (bf16[4,128,128]{2,1,0:T(8,128)(2,1)S(1)}, bf16[4,128,128]{2,1,0:T(8,128)(2,1)S(1)}, u32[]{:S(2)}, u32[]{:S(2)}) collective-permute-start(bf16[4,128,128]{2,1,0:T(8,128)(2,1)S(1)} %get-tuple-element.67), channel_id=1, source_target_pairs={{0,12},{4,8},{8,4},{12,0},{1,13},{5,9},{9,5},{13,1},{2,14},{6,10},... | collective-permute-start | bytes 393224 | tf_op jit(solution)/shard_map/ppermute | solution.py:140
  34.0 21.8 %collective-permute-start.3 = (bf16[4,128,128]{2,1,0:T(8,128)(2,1)S(1)}, bf16[4,128,128]{2,1,0:T(8,128)(2,1)S(1)}, u32[]{:S(2)}, u32[]{:S(2)}) collective-permute-start(bf16[4,128,128]{2,1,0:T(8,128)(2,1)S(1)} %get-tuple-element.45), channel_id=1, source_target_pairs={{0,4},{4,0},{8,12},{12,8},{1,5},{5,1},{9,13},{13,9},{2,6},{6,2},{1... | collective-permute-start | bytes 393224 | tf_op jit(solution)/shard_map/ppermute | solution.py:140
  44.6 11.9 %collective-permute-start.4 = (bf16[4,128,128]{2,1,0:T(8,128)(2,1)S(1)}, bf16[4,128,128]{2,1,0:T(8,128)(2,1)S(1)}, u32[]{:S(2)}, u32[]{:S(2)}) collective-permute-start(bf16[4,128,128]{2,1,0:T(8,128)(2,1)S(1)} %get-tuple-element.46), channel_id=1, source_target_pairs={{0,8},{4,12},{8,0},{12,4},{1,9},{5,13},{9,1},{13,5},{2,10},{6,14},... | collective-permute-start | bytes 393224 | tf_op jit(solution)/shard_map/ppermute | solution.py:140
  47.3 19.7 %collective-permute-start.5 = (bf16[4,128,128]{2,1,0:T(8,128)(2,1)S(1)}, bf16[4,128,128]{2,1,0:T(8,128)(2,1)S(1)}, u32[]{:S(2)}, u32[]{:S(2)}) collective-permute-start(bf16[4,128,128]{2,1,0:T(8,128)(2,1)S(1)} %get-tuple-element.47), channel_id=1, source_target_pairs={{0,12},{4,8},{8,4},{12,0},{1,13},{5,9},{9,5},{13,1},{2,14},{6,10},... | collective-permute-start | bytes 393224 | tf_op jit(solution)/shard_map/ppermute | solution.py:140
  47.8 19.3 %collective-permute-start.9 = (bf16[4,128,128]{2,1,0:T(8,128)(2,1)S(1)}, bf16[4,128,128]{2,1,0:T(8,128)(2,1)S(1)}, u32[]{:S(2)}, u32[]{:S(2)}) collective-permute-start(bf16[4,128,128]{2,1,0:T(8,128)(2,1)S(1)} %get-tuple-element.53), channel_id=1, source_target_pairs={{0,4},{4,0},{8,12},{12,8},{1,5},{5,1},{9,13},{13,9},{2,6},{6,2},{1... | collective-permute-start | bytes 393224 | tf_op jit(solution)/shard_map/ppermute | solution.py:140
  55.8 11.9 %collective-permute-start.10 = (bf16[4,128,128]{2,1,0:T(8,128)(2,1)S(1)}, bf16[4,128,128]{2,1,0:T(8,128)(2,1)S(1)}, u32[]{:S(2)}, u32[]{:S(2)}) collective-permute-start(bf16[4,128,128]{2,1,0:T(8,128)(2,1)S(1)} %get-tuple-element.54), channel_id=1, source_target_pairs={{0,8},{4,12},{8,0},{12,4},{1,9},{5,13},{9,1},{13,5},{2,10},{6,14},... | collective-permute-start | bytes 393224 | tf_op jit(solution)/shard_map/ppermute | solution.py:140
  55.8 22.5 %collective-permute-start.11 = (bf16[4,128,128]{2,1,0:T(8,128)(2,1)S(1)}, bf16[4,128,128]{2,1,0:T(8,128)(2,1)S(1)}, u32[]{:S(2)}, u32[]{:S(2)}) collective-permute-start(bf16[4,128,128]{2,1,0:T(8,128)(2,1)S(1)} %get-tuple-element.55), channel_id=1, source_target_pairs={{0,12},{4,8},{8,4},{12,0},{1,13},{5,9},{9,5},{13,1},{2,14},{6,10},... | collective-permute-start | bytes 393224 | tf_op jit(solution)/shard_map/ppermute | solution.py:140
  56.5 21.8 %collective-permute-start.15 = (bf16[4,128,128]{2,1,0:T(8,128)(2,1)S(1)}, bf16[4,128,128]{2,1,0:T(8,128)(2,1)S(1)}, u32[]{:S(2)}, u32[]{:S(2)}) collective-permute-start(bf16[4,128,128]{2,1,0:T(8,128)(2,1)S(1)} %get-tuple-element.61), channel_id=1, source_target_pairs={{0,4},{4,0},{8,12},{12,8},{1,5},{5,1},{9,13},{13,9},{2,6},{6,2},{1... | collective-permute-start | bytes 393224 | tf_op jit(solution)/shard_map/ppermute | solution.py:140
  67.1 11.9 %collective-permute-start.16 = (bf16[4,128,128]{2,1,0:T(8,128)(2,1)S(1)}, bf16[4,128,128]{2,1,0:T(8,128)(2,1)S(1)}, u32[]{:S(2)}, u32[]{:S(2)}) collective-permute-start(bf16[4,128,128]{2,1,0:T(8,128)(2,1)S(1)} %get-tuple-element.62), channel_id=1, source_target_pairs={{0,8},{4,12},{8,0},{12,4},{1,9},{5,13},{9,1},{13,5},{2,10},{6,14},... | collective-permute-start | bytes 393224 | tf_op jit(solution)/shard_map/ppermute | solution.py:140
  67.1 22.5 %collective-permute-start.17 = (bf16[4,128,128]{2,1,0:T(8,128)(2,1)S(1)}, bf16[4,128,128]{2,1,0:T(8,128)(2,1)S(1)}, u32[]{:S(2)}, u32[]{:S(2)}) collective-permute-start(bf16[4,128,128]{2,1,0:T(8,128)(2,1)S(1)} %get-tuple-element.63), channel_id=1, source_target_pairs={{0,12},{4,8},{8,4},{12,0},{1,13},{5,9},{9,5},{13,1},{2,14},{6,10},... | collective-permute-start | bytes 393224 | tf_op jit(solution)/shard_map/ppermute | solution.py:140
  67.7 21.8 %collective-permute-start.21 = (bf16[4,128,128]{2,1,0:T(8,128)(2,1)S(1)}, bf16[4,128,128]{2,1,0:T(8,128)(2,1)S(1)}, u32[]{:S(2)}, u32[]{:S(2)}) collective-permute-start(bf16[4,128,128]{2,1,0:T(8,128)(2,1)S(1)} %get-tuple-element.69), channel_id=1, source_target_pairs={{0,4},{4,0},{8,12},{12,8},{1,5},{5,1},{9,13},{13,9},{2,6},{6,2},{1... | collective-permute-start | bytes 393224 | tf_op jit(solution)/shard_map/ppermute | solution.py:140
  78.3 12.0 %collective-permute-start.22 = (bf16[4,128,128]{2,1,0:T(8,128)(2,1)S(1)}, bf16[4,128,128]{2,1,0:T(8,128)(2,1)S(1)}, u32[]{:S(2)}, u32[]{:S(2)}) collective-permute-start(bf16[4,128,128]{2,1,0:T(8,128)(2,1)S(1)} %get-tuple-element.70), channel_id=1, source_target_pairs={{0,8},{4,12},{8,0},{12,4},{1,9},{5,13},{9,1},{13,5},{2,10},{6,14},... | collective-permute-start | bytes 393224 | tf_op jit(solution)/shard_map/ppermute | solution.py:140
  78.3 16.8 %collective-permute-start.23 = (bf16[4,128,128]{2,1,0:T(8,128)(2,1)S(1)}, bf16[4,128,128]{2,1,0:T(8,128)(2,1)S(1)}, u32[]{:S(2)}, u32[]{:S(2)}) collective-permute-start(bf16[4,128,128]{2,1,0:T(8,128)(2,1)S(1)} %get-tuple-element.71), channel_id=1, source_target_pairs={{0,12},{4,8},{8,4},{12,0},{1,13},{5,9},{9,5},{13,1},{2,14},{6,10},... | collective-permute-start | bytes 393224 | tf_op jit(solution)/shard_map/ppermute | solution.py:140

commit v5 on v4

--- a/solution.py
+++ b/solution.py
@@ -35,24 +35,42 @@
         copy.wait()
 
 
-def unpack_kernel(me_ref, *refs, ranks, heads):
-    pieces, outs, buffers, sems = refs[: ranks * heads], refs[ranks * heads : -2], refs[-2], refs[-1]
+def rows_kernel(me_ref, *refs, ranks, wanted):
+    pieces, outs, buffers, sems = refs[: len(wanted)], refs[len(wanted) : -2], refs[-2], refs[-1]
     features, width = outs[0].shape[1], pieces[0].shape[2]
     copies = []
     for i, out in enumerate(outs):
-        for head in range(heads):
-            for step in range(ranks):
-                dest = me_ref[0] ^ step
-                start = pl.multiple_of(dest * (features // ranks) + head * width, 128)
-                buffers[i, :, pl.ds(start, width)] = pieces[head * ranks + step][i]
+        for n, (head, step) in enumerate(wanted):
+            dest = me_ref[0] ^ step
+            start = pl.multiple_of(dest * (features // ranks) + head * width, 128)
+            buffers[i, :, pl.ds(start, width)] = pieces[n][i]
         copies.append(pltpu.make_async_copy(buffers.at[i], out, sems.at[i]))
         copies[-1].start()
     for copy in copies:
         copy.wait()
 
 
-def attention_kernel(bias_ref, *refs, ranks, tokens, scale):
-    got, sent = refs[:ranks], refs[ranks:]
+def columns_kernel(me_ref, *refs, ranks, wanted):
+    pieces, outs, sems = refs[: len(wanted)], refs[-5:-1], refs[-1]
+    features, width = outs[0].shape[1], pieces[0].shape[2]
+    copies = []
+    for n, (head, step) in enumerate(wanted):
+        dest = me_ref[0] ^ step
+        start = pl.multiple_of(dest * (features // ranks) + head * width, 128)
+        for i, out in enumerate(outs):
+            copies.append(
+                pltpu.make_async_copy(
+                    pieces[n].at[i], out.at[:, pl.ds(start, width)], sems.at[n, i]
+                )
+            )
+    for copy in copies:
+        copy.start()
+    for copy in copies:
+        copy.wait()
+
+
+def attention_kernel(bias_ref, *refs, ranks, tokens, scale, order):
+    got, sent = [refs[order.index(step)] for step in range(ranks)], refs[ranks:]
     f32, bf16 = jnp.float32, jnp.bfloat16
     length = ranks * tokens
     tile = min(QUERY_TILE, length)
@@ -139,10 +157,10 @@
     def permute(x, step):
         return lax.ppermute(x, "ctx", [(j, j ^ step) for j in range(ranks)])
 
-    def attend(got):
+    def attend(got, order):
         return pl.pallas_call(
             functools.partial(
-                attention_kernel, ranks=ranks, tokens=tokens, scale=head_dim ** (-0.5)
+                attention_kernel, ranks=ranks, tokens=tokens, scale=head_dim ** (-0.5), order=order
             ),
             out_shape=[piece] * ranks,
             in_specs=[VMEM] * (1 + ranks),
@@ -151,6 +169,8 @@
         )(bias, *on_chip(got))
 
     steps = [*range(ranks - 1, -1, -1)]
+    orders = [[0, 1, *range(ranks - 1, 1, -1)]] + [[*range(2, ranks), 1, 0]] * (heads - 1)
+    order_out = [*range(2, ranks), 1, 0]
     slots = [(head, step) for head in range(heads) for step in steps]
     early = [(0, step) for step in steps if step > 1]
     pieces = pack(early)
@@ -161,20 +181,31 @@
     bias = block_bias(rand_blocks[0], glob_blocks[0], me, ranks, tokens // BLOCK)
     back = []
     for head in range(heads):
-        sent = attend([got[head, step] for step in range(ranks)])
+        sent = attend([got[head, step] for step in orders[head]], orders[head])
         moved = {step: permute(sent[step], step) if step else sent[step] for step in steps}
-        back += [moved[step] for step in range(ranks)]
-    outs = pl.pallas_call(
-        functools.partial(unpack_kernel, ranks=ranks, heads=heads),
-        out_shape=[full] * 4,
-        in_specs=[SMEM] + [VMEM] * len(back),
-        out_specs=[ANY] * 4,
-        scratch_shapes=[
-            pltpu.VMEM((4, tokens, features), jnp.bfloat16),
-            pltpu.SemaphoreType.DMA((4,)),
-        ],
-        compiler_params=PARAMS,
-    )(me_arr, *on_chip(back))
+        back += [moved[step] for step in order_out]
+
+    def unpack(kernel, wanted, scratch, outs):
+        return pl.pallas_call(
+            functools.partial(kernel, ranks=ranks, wanted=wanted),
+            out_shape=[full] * 4,
+            in_specs=[SMEM] + [VMEM] * len(wanted) + [ANY] * len(outs),
+            out_specs=[ANY] * 4,
+            scratch_shapes=scratch,
+            input_output_aliases={1 + len(wanted) + i: i for i in range(len(outs))},
+            compiler_params=PARAMS,
+        )(me_arr, *on_chip([back[h * ranks + order_out.index(s)] for h, s in wanted]), *outs)
+
+    rows = [
+        pltpu.VMEM((4, tokens, features), jnp.bfloat16),
+        pltpu.SemaphoreType.DMA((4,)),
+    ]
+    done = [(head, step) for head in range(heads) for step in order_out]
+    last = [slot for slot in done if slot[0] == heads - 1 and slot[1]]
+    outs = []
+    if len(last) < len(done):
+        outs = unpack(rows_kernel, [slot for slot in done if slot not in last], rows, outs)
+    outs = unpack(columns_kernel, last, [pltpu.SemaphoreType.DMA((len(last), 4))], outs)
     return tuple(x[None] for x in outs)
 
 

time: 97.1 us -> 95.8 us (0.987)
  waiting for transfers between devices: 47 us -> 33 us
  starting transfers between devices: 36.4 us -> 48 us
    ppermute x24, waiting for transfers between devices: 47 us -> 33 us  [permute(): return lax.ppermute(x, 'ctx', [(j, j ^ step) for j in range(ranks)])]
    ppermute x24, starting transfers between devices: 36.4 us -> 48 us  [permute(): return lax.ppermute(x, 'ctx', [(j, j ^ step) for j in range(ranks)])]
    pallas_call x1 -> x2, Pallas kernels: 1.49 us -> 2.3 us  [unpack(): pl.pallas_call(functools.partial(kernel, ranks=ranks, wanted=wanted), out...]
  transfers between devices with their start and end apart: 24 -> 24, of which waited for: 13 -> 13; matrix products, arithmetic and copies ran while one was open for 1% -> 1% of each run, Pallas kernels for 8% -> 9%
where the time goes in v5:
time: 95.8 us; the launch traced here: 94.9 us
  starting transfers between devices  48 us (50%)
  waiting for transfers between devices  33 us (34%)
  Pallas kernels  10.6 us (11%)
  local copies, waits for them, and re-layouts  2.18 us (2%)
    ppermute x24, starting transfers between devices, permute(): return lax.ppermute(x, 'ctx', [(j, j ^ step) for j in range(ranks)])  48 us
    ppermute x24, waiting for transfers between devices, permute(): return lax.ppermute(x, 'ctx', [(j, j ^ step) for j in range(ranks)])  33 us
    pallas_call x4, Pallas kernels, attend(): pl.pallas_call(functools.partial(attention_kernel, ranks=ranks, tokens=to...  5.41 us
    pallas_call x2, Pallas kernels, pack(): pl.pallas_call(functools.partial(pack_kernel, ranks=ranks, wanted=wanted)...  2.9 us
    pallas_call x2, Pallas kernels, unpack(): pl.pallas_call(functools.partial(kernel, ranks=ranks, wanted=wanted), out...  2.3 us
  transfers between devices with their start and end apart: 24, of which 13 were waited for; matrix products, arithmetic and copies ran while one was open for 1% of the time, Pallas kernels for 9%

profile of v5, /device:TPU:18, one launch (start us, length us, event | category | flops | bytes accessed | tf_op | source)
XLA Modules:
  0.0 94.9 jit_solution(12611857902192841768)
XLA Ops:
  0.6 1.0 %shard_map.95 = (bf16[4,128,128]{2,1,0:T(8,128)(2,1)S(1)}, bf16[4,128,128]{2,1,0:T(8,128)(2,1)S(1)}) custom-call(s32[1]{0:T(128)} %bitcast.me_ref, bf16[128,2048]{1,0:T(8,128)(2,1)} %bitcast.13, bf16[128,2048]{1,0:T(8,128)(2,1)} %bitcast.15, bf16[128,2048]{1,0:T(8,128)(2,1)} %bitcast.17, bf16[128,2048]{1,0:T(8,128)(2,1)} %bitcast.19), custom_call_target="tpu_custom_call" | custom-call | tf_op jit(solution)/shard_map/pallas_call | solution.py:147
  1.6 0.5 collective-permute-start.7
  2.1 3.5 %collective-permute-start.8 = (bf16[4,128,128]{2,1,0:T(8,128)(2,1)S(1)}, bf16[4,128,128]{2,1,0:T(8,128)(2,1)S(1)}, u32[]{:S(2)}, u32[]{:S(2)}) collective-permute-start(bf16[4,128,128]{2,1,0:T(8,128)(2,1)S(1)} %get-tuple-element.54), channel_id=1, source_target_pairs={{0,8},{4,12},{8,0},{12,4},{1,9},{5,13},{9,1},{13,5},{2,10},{6,14},... | collective-permute-start | bytes 393224 | tf_op jit(solution)/shard_map/ppermute | solution.py:158
  5.6 1.9 %shard_map.93 = (bf16[4,128,128]{2,1,0:T(8,128)(2,1)S(1)}, bf16[4,128,128]{2,1,0:T(8,128)(2,1)S(1)}, bf16[4,128,128]{2,1,0:T(8,128)(2,1)S(1)}, bf16[4,128,128]{2...) custom-call(s32[1]{0:T(128)} %bitcast.me_ref, ...), custom_call_target="tpu_custom_call" | custom-call | tf_op jit(solution)/shard_map/pallas_call | solution.py:147
  7.6 0.8 collective-permute-start.12
  8.4 2.7 %collective-permute-start.13 = (bf16[4,128,128]{2,1,0:T(8,128)(2,1)S(1)}, bf16[4,128,128]{2,1,0:T(8,128)(2,1)S(1)}, u32[]{:S(2)}, u32[]{:S(2)}) collective-permute-start(bf16[4,128,128]{2,1,0:T(8,128)(2,1)S(1)} %get-tuple-element.60), channel_id=1, source_target_pairs={{0,12},{4,8},{8,4},{12,0},{1,13},{5,9},{9,5},{13,1},{2,14},{6,10},... | collective-permute-start | bytes 393224 | tf_op jit(solution)/shard_map/ppermute | solution.py:158
  11.2 0.7 copy-done
  11.8 0.1 copy.17
  11.9 0.6 gather_fusion
  12.5 0.7 copy-done.1
  13.2 0.1 compare_reduce_fusion.1
  13.3 0.1 copy.16
  13.4 0.1 compare_reduce_fusion
  13.4 0.5 collective-permute-done.7.refs_2_
  14.0 0.5 collective-permute-start.14
  14.4 6.7 %collective-permute-done.8.refs_3_ = bf16[4,128,128]{2,1,0:T(8,128)(2,1)S(1)} collective-permute-done((bf16[4,128,128]{2,1,0:T(8,128)(2,1)S(1)}, bf16[4,128,128]{2,1,0:T(8,128)(2,1)S(1)}, u32[]{:S(2)}, u32[]{:S(2)}) %collective-permute-start.8) | collective-permute-done | bytes 131104 | tf_op jit(solution)/shard_map/ppermute | solution.py:158
  21.1 3.6 %collective-permute-start.18 = (bf16[4,128,128]{2,1,0:T(8,128)(2,1)S(1)}, bf16[4,128,128]{2,1,0:T(8,128)(2,1)S(1)}, u32[]{:S(2)}, u32[]{:S(2)}) collective-permute-start(bf16[4,128,128]{2,1,0:T(8,128)(2,1)S(1)} %get-tuple-element.67), channel_id=1, source_target_pairs={{0,8},{4,12},{8,0},{12,4},{1,9},{5,13},{9,1},{13,5},{2,10},{6,14},... | collective-permute-start | bytes 393224 | tf_op jit(solution)/shard_map/ppermute | solution.py:158
  24.7 0.7 collective-permute-start.19
  25.4 1.1 %collective-permute-done.12.refs_0_ = bf16[4,128,128]{2,1,0:T(8,128)(2,1)S(1)} collective-permute-done((bf16[4,128,128]{2,1,0:T(8,128)(2,1)S(1)}, bf16[4,128,128]{2,1,0:T(8,128)(2,1)S(1)}, u32[]{:S(2)}, u32[]{:S(2)}) %collective-permute-start.12) | collective-permute-done | bytes 131104 | tf_op jit(solution)/shard_map/ppermute | solution.py:158
  26.4 5.6 %collective-permute-start.20 = (bf16[4,128,128]{2,1,0:T(8,128)(2,1)S(1)}, bf16[4,128,128]{2,1,0:T(8,128)(2,1)S(1)}, u32[]{:S(2)}, u32[]{:S(2)}) collective-permute-start(bf16[4,128,128]{2,1,0:T(8,128)(2,1)S(1)} %get-tuple-element.69), channel_id=1, source_target_pairs={{0,4},{4,0},{8,12},{12,8},{1,5},{5,1},{9,13},{13,9},{2,6},{6,2},{1... | collective-permute-start | bytes 393224 | tf_op jit(solution)/shard_map/ppermute | solution.py:158
  32.0 0.1 or_select_fusion
  32.2 0.1 reshape.148.bias_ref
  32.3 1.4 %shard_map.96 = (bf16[4,128,128]{2,1,0:T(8,128)(2,1)S(1)}, bf16[4,128,128]{2,1,0:T(8,128)(2,1)S(1)}, bf16[4,128,128]{2,1,0:T(8,128)(2,1)S(1)}, bf16[4,128,128]{2,1,0:T(8,128)(2,1)S(1)}) custom-call(f32[8,512]{1,0:T(8,128)S(1)} %reshape.148.bias_ref, bf16[4,128,128]{2,1,0:T(8,128)(2,1)S(1)} %get-tuple-element.51.refs_0_, ...), custom_call_target="tpu_custom_call" | custom-call | tf_op jit(solution)/shard_map/pallas_call | solution.py:161
  33.7 1.4 %collective-permute-start.1 = (bf16[4,128,128]{2,1,0:T(8,128)(2,1)S(1)}, bf16[4,128,128]{2,1,0:T(8,128)(2,1)S(1)}, u32[]{:S(2)}, u32[]{:S(2)}) collective-permute-start(bf16[4,128,128]{2,1,0:T(8,128)(2,1)S(1)} %get-tuple-element.45), channel_id=1, source_target_pairs={{0,12},{4,8},{8,4},{12,0},{1,13},{5,9},{9,5},{13,1},{2,14},{6,10},... | collective-permute-start | bytes 393224 | tf_op jit(solution)/shard_map/ppermute | solution.py:158
  35.2 6.0 %collective-permute-start.2 = (bf16[4,128,128]{2,1,0:T(8,128)(2,1)S(1)}, bf16[4,128,128]{2,1,0:T(8,128)(2,1)S(1)}, u32[]{:S(2)}, u32[]{:S(2)}) collective-permute-start(bf16[4,128,128]{2,1,0:T(8,128)(2,1)S(1)} %get-tuple-element.46), channel_id=1, source_target_pairs={{0,4},{4,0},{8,12},{12,8},{1,5},{5,1},{9,13},{13,9},{2,6},{6,2},{1... | collective-permute-start | bytes 393224 | tf_op jit(solution)/shard_map/ppermute | solution.py:158
  41.2 3.4 %collective-permute-done.19.refs_1_ = bf16[4,128,128]{2,1,0:T(8,128)(2,1)S(1)} collective-permute-done((bf16[4,128,128]{2,1,0:T(8,128)(2,1)S(1)}, bf16[4,128,128]{2,1,0:T(8,128)(2,1)S(1)}, u32[]{:S(2)}, u32[]{:S(2)}) %collective-permute-start.19) | collective-permute-done | bytes 131104 | tf_op jit(solution)/shard_map/ppermute | solution.py:158
  44.6 0.2 collective-permute-start.10
  44.8 1.3 %shard_map.97 = (bf16[4,128,128]{2,1,0:T(8,128)(2,1)S(1)}, bf16[4,128,128]{2,1,0:T(8,128)(2,1)S(1)}, bf16[4,128,128]{2,1,0:T(8,128)(2,1)S(1)}, bf16[4,128,128]{2,1,0:T(8,128)(2,1)S(1)}) custom-call(f32[8,512]{1,0:T(8,128)S(1)} %reshape.148.bias_ref, bf16[4,128,128]{2,1,0:T(8,128)(2,1)S(1)} %collective-permute-done.12.refs_0_, ...), custom_call_target="tpu_custom_call" | custom-call | tf_op jit(solution)/shard_map/pallas_call | solution.py:161
  46.2 1.4 %shard_map.98 = (bf16[4,128,128]{2,1,0:T(8,128)(2,1)S(1)}, bf16[4,128,128]{2,1,0:T(8,128)(2,1)S(1)}, bf16[4,128,128]{2,1,0:T(8,128)(2,1)S(1)}, bf16[4,128,128]{2,1,0:T(8,128)(2,1)S(1)}) custom-call(f32[8,512]{1,0:T(8,128)S(1)} %reshape.148.bias_ref, bf16[4,128,128]{2,1,0:T(8,128)(2,1)S(1)} %collective-permute-done.18.refs_0_, ...), custom_call_target="tpu_custom_call" | custom-call | tf_op jit(solution)/shard_map/pallas_call | solution.py:161
  47.5 1.7 %collective-permute-done.refs_0_ = bf16[4,128,128]{2,1,0:T(8,128)(2,1)S(1)} collective-permute-done((bf16[4,128,128]{2,1,0:T(8,128)(2,1)S(1)}, bf16[4,128,128]{2,1,0:T(8,128)(2,1)S(1)}, u32[]{:S(2)}, u32[]{:S(2)}) %collective-permute-start) | collective-permute-done | bytes 131104 | tf_op jit(solution)/shard_map/ppermute | solution.py:158
  49.2 3.6 %collective-permute-start.11 = (bf16[4,128,128]{2,1,0:T(8,128)(2,1)S(1)}, bf16[4,128,128]{2,1,0:T(8,128)(2,1)S(1)}, u32[]{:S(2)}, u32[]{:S(2)}) collective-permute-start(bf16[4,128,128]{2,1,0:T(8,128)(2,1)S(1)} %get-tuple-element.57), channel_id=1, source_target_pairs={{0,4},{4,0},{8,12},{12,8},{1,5},{5,1},{9,13},{13,9},{2,6},{6,2},{1... | collective-permute-start | bytes 393224 | tf_op jit(solution)/shard_map/ppermute | solution.py:158
  52.8 3.0 %collective-permute-done.1.refs_1_ = bf16[4,128,128]{2,1,0:T(8,128)(2,1)S(1)} collective-permute-done((bf16[4,128,128]{2,1,0:T(8,128)(2,1)S(1)}, bf16[4,128,128]{2,1,0:T(8,128)(2,1)S(1)}, u32[]{:S(2)}, u32[]{:S(2)}) %collective-permute-start.1) | collective-permute-done | bytes 131104 | tf_op jit(solution)/shard_map/ppermute | solution.py:158
  55.8 0.2 collective-permute-start.16
  56.1 3.8 %collective-permute-done.9.refs_0_ = bf16[4,128,128]{2,1,0:T(8,128)(2,1)S(1)} collective-permute-done((bf16[4,128,128]{2,1,0:T(8,128)(2,1)S(1)}, bf16[4,128,128]{2,1,0:T(8,128)(2,1)S(1)}, u32[]{:S(2)}, u32[]{:S(2)}) %collective-permute-start.9) | collective-permute-done | bytes 131104 | tf_op jit(solution)/shard_map/ppermute | solution.py:158
  59.8 5.9 %collective-permute-start.17 = (bf16[4,128,128]{2,1,0:T(8,128)(2,1)S(1)}, bf16[4,128,128]{2,1,0:T(8,128)(2,1)S(1)}, u32[]{:S(2)}, u32[]{:S(2)}) collective-permute-start(bf16[4,128,128]{2,1,0:T(8,128)(2,1)S(1)} %get-tuple-element.65), channel_id=1, source_target_pairs={{0,4},{4,0},{8,12},{12,8},{1,5},{5,1},{9,13},{13,9},{2,6},{6,2},{1... | collective-permute-start | bytes 393224 | tf_op jit(solution)/shard_map/ppermute | solution.py:158
  65.7 1.3 %collective-permute-done.10.refs_1_ = bf16[4,128,128]{2,1,0:T(8,128)(2,1)S(1)} collective-permute-done((bf16[4,128,128]{2,1,0:T(8,128)(2,1)S(1)}, bf16[4,128,128]{2,1,0:T(8,128)(2,1)S(1)}, u32[]{:S(2)}, u32[]{:S(2)}) %collective-permute-start.10) | collective-permute-done | bytes 131104 | tf_op jit(solution)/shard_map/ppermute | solution.py:158
  67.1 1.4 %shard_map.94 = (bf16[4,128,128]{2,1,0:T(8,128)(2,1)S(1)}, bf16[4,128,128]{2,1,0:T(8,128)(2,1)S(1)}, bf16[4,128,128]{2,1,0:T(8,128)(2,1)S(1)}, bf16[4,128,128]{2,1,0:T(8,128)(2,1)S(1)}) custom-call(f32[8,512]{1,0:T(8,128)S(1)} %reshape.148.bias_ref, bf16[4,128,128]{2,1,0:T(8,128)(2,1)S(1)} %collective-permute-done.refs_0_, ...), custom_call_target="tpu_custom_call" | custom-call | tf_op jit(solution)/shard_map/pallas_call | solution.py:161
  68.4 0.3 collective-permute-start.22
  68.7 0.3 collective-permute-done.15.refs_4_
  69.0 6.2 %collective-permute-start.23 = (bf16[4,128,128]{2,1,0:T(8,128)(2,1)S(1)}, bf16[4,128,128]{2,1,0:T(8,128)(2,1)S(1)}, u32[]{:S(2)}, u32[]{:S(2)}) collective-permute-start(bf16[4,128,128]{2,1,0:T(8,128)(2,1)S(1)} %get-tuple-element.73), channel_id=1, source_target_pairs={{0,4},{4,0},{8,12},{12,8},{1,5},{5,1},{9,13},{13,9},{2,6},{6,2},{1... | collective-permute-start | bytes 393224 | tf_op jit(solution)/shard_map/ppermute | solution.py:158
  75.3 3.0 %collective-permute-done.16.refs_5_ = bf16[4,128,128]{2,1,0:T(8,128)(2,1)S(1)} collective-permute-done((bf16[4,128,128]{2,1,0:T(8,128)(2,1)S(1)}, bf16[4,128,128]{2,1,0:T(8,128)(2,1)S(1)}, u32[]{:S(2)}, u32[]{:S(2)}) %collective-permute-start.16) | collective-permute-done | bytes 131104 | tf_op jit(solution)/shard_map/ppermute | solution.py:158
  78.3 0.2 collective-permute-start.4
  78.5 3.8 %collective-permute-done.21.refs_8_ = bf16[4,128,128]{2,1,0:T(8,128)(2,1)S(1)} collective-permute-done((bf16[4,128,128]{2,1,0:T(8,128)(2,1)S(1)}, bf16[4,128,128]{2,1,0:T(8,128)(2,1)S(1)}, u32[]{:S(2)}, u32[]{:S(2)}) %collective-permute-start.21) | collective-permute-done | bytes 131104 | tf_op jit(solution)/shard_map/ppermute | solution.py:158
  82.3 5.9 %collective-permute-start.5 = (bf16[4,128,128]{2,1,0:T(8,128)(2,1)S(1)}, bf16[4,128,128]{2,1,0:T(8,128)(2,1)S(1)}, u32[]{:S(2)}, u32[]{:S(2)}) collective-permute-start(bf16[4,128,128]{2,1,0:T(8,128)(2,1)S(1)} %get-tuple-element.50), channel_id=1, source_target_pairs={{0,4},{4,0},{8,12},{12,8},{1,5},{5,1},{9,13},{13,9},{2,6},{6,2},{1... | collective-permute-start | bytes 393224 | tf_op jit(solution)/shard_map/ppermute | solution.py:158
  88.2 1.3 %collective-permute-done.22.refs_9_ = bf16[4,128,128]{2,1,0:T(8,128)(2,1)S(1)} collective-permute-done((bf16[4,128,128]{2,1,0:T(8,128)(2,1)S(1)}, bf16[4,128,128]{2,1,0:T(8,128)(2,1)S(1)}, u32[]{:S(2)}, u32[]{:S(2)}) %collective-permute-start.22) | collective-permute-done | bytes 131104 | tf_op jit(solution)/shard_map/ppermute | solution.py:158
  89.5 1.5 %shard_map.99 = (bf16[128,2048]{1,0:T(8,128)(2,1)}, bf16[128,2048]{1,0:T(8,128)(2,1)}, bf16[128,2048]{1,0:T(8,128)(2,1)}, bf16[128,2048]{1,0:T(8,128)(2,1)}) custom-call(s32[1]{0:T(128)} %bitcast.me_ref, bf16[4,128,128]{2,1,0:T(8,128)(2,1)S(1)} %collective-permute-done.9.refs_0_, bf16[4,128,128]{2,1,0:T(8,128)(2,1)S(1)} %collective-permute-done.10.refs_1_, ...), custom_call_target="tpu_custom_call" | custom-call | tf_op jit(solution)/shard_map/pallas_call | solution.py:189
  91.0 3.0 %collective-permute-done.4.refs_1_ = bf16[4,128,128]{2,1,0:T(8,128)(2,1)S(1)} collective-permute-done((bf16[4,128,128]{2,1,0:T(8,128)(2,1)S(1)}, bf16[4,128,128]{2,1,0:T(8,128)(2,1)S(1)}, u32[]{:S(2)}, u32[]{:S(2)}) %collective-permute-start.4) | collective-permute-done | bytes 131104 | tf_op jit(solution)/shard_map/ppermute | solution.py:158
  94.0 0.8 shard_map.100
  (25 shorter events, 0.4 us)
Async XLA Ops:
  1.6 12.4 %collective-permute-start.7 = (bf16[4,128,128]{2,1,0:T(8,128)(2,1)S(1)}, bf16[4,128,128]{2,1,0:T(8,128)(2,1)S(1)}, u32[]{:S(2)}, u32[]{:S(2)}) collective-permute-start(bf16[4,128,128]{2,1,0:T(8,128)(2,1)S(1)} %get-tuple-element.53), channel_id=1, source_target_pairs={{0,12},{4,8},{8,4},{12,0},{1,13},{5,9},{9,5},{13,1},{2,14},{6,10},... | collective-permute-start | bytes 393224 | tf_op jit(solution)/shard_map/ppermute | solution.py:158
  2.1 19.0 %collective-permute-start.8 = (bf16[4,128,128]{2,1,0:T(8,128)(2,1)S(1)}, bf16[4,128,128]{2,1,0:T(8,128)(2,1)S(1)}, u32[]{:S(2)}, u32[]{:S(2)}) collective-permute-start(bf16[4,128,128]{2,1,0:T(8,128)(2,1)S(1)} %get-tuple-element.54), channel_id=1, source_target_pairs={{0,8},{4,12},{8,0},{12,4},{1,9},{5,13},{9,1},{13,5},{2,10},{6,14},... | collective-permute-start | bytes 393224 | tf_op jit(solution)/shard_map/ppermute | solution.py:158
  7.5 17.1 %collective-permute-start.6 = (bf16[4,128,128]{2,1,0:T(8,128)(2,1)S(1)}, bf16[4,128,128]{2,1,0:T(8,128)(2,1)S(1)}, u32[]{:S(2)}, u32[]{:S(2)}) collective-permute-start(bf16[4,128,128]{2,1,0:T(8,128)(2,1)S(1)} %get-tuple-element.52), channel_id=1, source_target_pairs={{0,4},{4,0},{8,12},{12,8},{1,5},{5,1},{9,13},{13,9},{2,6},{6,2},{1... | collective-permute-start | bytes 393224 | tf_op jit(solution)/shard_map/ppermute | solution.py:158
  7.6 18.8 %collective-permute-start.12 = (bf16[4,128,128]{2,1,0:T(8,128)(2,1)S(1)}, bf16[4,128,128]{2,1,0:T(8,128)(2,1)S(1)}, u32[]{:S(2)}, u32[]{:S(2)}) collective-permute-start(bf16[4,128,128]{2,1,0:T(8,128)(2,1)S(1)} %get-tuple-element.59), channel_id=1, source_target_pairs={{0,8},{4,12},{8,0},{12,4},{1,9},{5,13},{9,1},{13,5},{2,10},{6,14},... | collective-permute-start | bytes 393224 | tf_op jit(solution)/shard_map/ppermute | solution.py:158
  8.4 25.2 %collective-permute-start.13 = (bf16[4,128,128]{2,1,0:T(8,128)(2,1)S(1)}, bf16[4,128,128]{2,1,0:T(8,128)(2,1)S(1)}, u32[]{:S(2)}, u32[]{:S(2)}) collective-permute-start(bf16[4,128,128]{2,1,0:T(8,128)(2,1)S(1)} %get-tuple-element.60), channel_id=1, source_target_pairs={{0,12},{4,8},{8,4},{12,0},{1,13},{5,9},{9,5},{13,1},{2,14},{6,10},... | collective-permute-start | bytes 393224 | tf_op jit(solution)/shard_map/ppermute | solution.py:158
  11.1 0.7 copy-start
  12.5 0.7 copy-start.1
  14.0 19.7 %collective-permute-start.14 = (bf16[4,128,128]{2,1,0:T(8,128)(2,1)S(1)}, bf16[4,128,128]{2,1,0:T(8,128)(2,1)S(1)}, u32[]{:S(2)}, u32[]{:S(2)}) collective-permute-start(bf16[4,128,128]{2,1,0:T(8,128)(2,1)S(1)} %get-tuple-element.61), channel_id=1, source_target_pairs={{0,4},{4,0},{8,12},{12,8},{1,5},{5,1},{9,13},{13,9},{2,6},{6,2},{1... | collective-permute-start | bytes 393224 | tf_op jit(solution)/shard_map/ppermute | solution.py:158
  21.1 14.1 %collective-permute-start.18 = (bf16[4,128,128]{2,1,0:T(8,128)(2,1)S(1)}, bf16[4,128,128]{2,1,0:T(8,128)(2,1)S(1)}, u32[]{:S(2)}, u32[]{:S(2)}) collective-permute-start(bf16[4,128,128]{2,1,0:T(8,128)(2,1)S(1)} %get-tuple-element.67), channel_id=1, source_target_pairs={{0,8},{4,12},{8,0},{12,4},{1,9},{5,13},{9,1},{13,5},{2,10},{6,14},... | collective-permute-start | bytes 393224 | tf_op jit(solution)/shard_map/ppermute | solution.py:158
  24.7 19.9 %collective-permute-start.19 = (bf16[4,128,128]{2,1,0:T(8,128)(2,1)S(1)}, bf16[4,128,128]{2,1,0:T(8,128)(2,1)S(1)}, u32[]{:S(2)}, u32[]{:S(2)}) collective-permute-start(bf16[4,128,128]{2,1,0:T(8,128)(2,1)S(1)} %get-tuple-element.68), channel_id=1, source_target_pairs={{0,12},{4,8},{8,4},{12,0},{1,13},{5,9},{9,5},{13,1},{2,14},{6,10},... | collective-permute-start | bytes 393224 | tf_op jit(solution)/shard_map/ppermute | solution.py:158
  26.4 18.2 %collective-permute-start.20 = (bf16[4,128,128]{2,1,0:T(8,128)(2,1)S(1)}, bf16[4,128,128]{2,1,0:T(8,128)(2,1)S(1)}, u32[]{:S(2)}, u32[]{:S(2)}) collective-permute-start(bf16[4,128,128]{2,1,0:T(8,128)(2,1)S(1)} %get-tuple-element.69), channel_id=1, source_target_pairs={{0,4},{4,0},{8,12},{12,8},{1,5},{5,1},{9,13},{13,9},{2,6},{6,2},{1... | collective-permute-start | bytes 393224 | tf_op jit(solution)/shard_map/ppermute | solution.py:158
  33.6 15.6 %collective-permute-start = (bf16[4,128,128]{2,1,0:T(8,128)(2,1)S(1)}, bf16[4,128,128]{2,1,0:T(8,128)(2,1)S(1)}, u32[]{:S(2)}, u32[]{:S(2)}) collective-permute-start(bf16[4,128,128]{2,1,0:T(8,128)(2,1)S(1)} %get-tuple-element.44), channel_id=1, source_target_pairs={{0,8},{4,12},{8,0},{12,4},{1,9},{5,13},{9,1},{13,5},{2,10},{6,14},... | collective-permute-start | bytes 393224 | tf_op jit(solution)/shard_map/ppermute | solution.py:158
  33.7 22.1 %collective-permute-start.1 = (bf16[4,128,128]{2,1,0:T(8,128)(2,1)S(1)}, bf16[4,128,128]{2,1,0:T(8,128)(2,1)S(1)}, u32[]{:S(2)}, u32[]{:S(2)}) collective-permute-start(bf16[4,128,128]{2,1,0:T(8,128)(2,1)S(1)} %get-tuple-element.45), channel_id=1, source_target_pairs={{0,12},{4,8},{8,4},{12,0},{1,13},{5,9},{9,5},{13,1},{2,14},{6,10},... | collective-permute-start | bytes 393224 | tf_op jit(solution)/shard_map/ppermute | solution.py:158
  35.2 20.7 %collective-permute-start.2 = (bf16[4,128,128]{2,1,0:T(8,128)(2,1)S(1)}, bf16[4,128,128]{2,1,0:T(8,128)(2,1)S(1)}, u32[]{:S(2)}, u32[]{:S(2)}) collective-permute-start(bf16[4,128,128]{2,1,0:T(8,128)(2,1)S(1)} %get-tuple-element.46), channel_id=1, source_target_pairs={{0,4},{4,0},{8,12},{12,8},{1,5},{5,1},{9,13},{13,9},{2,6},{6,2},{1... | collective-permute-start | bytes 393224 | tf_op jit(solution)/shard_map/ppermute | solution.py:158
  44.6 15.2 %collective-permute-start.9 = (bf16[4,128,128]{2,1,0:T(8,128)(2,1)S(1)}, bf16[4,128,128]{2,1,0:T(8,128)(2,1)S(1)}, u32[]{:S(2)}, u32[]{:S(2)}) collective-permute-start(bf16[4,128,128]{2,1,0:T(8,128)(2,1)S(1)} %get-tuple-element.55), channel_id=1, source_target_pairs={{0,8},{4,12},{8,0},{12,4},{1,9},{5,13},{9,1},{13,5},{2,10},{6,14},... | collective-permute-start | bytes 393224 | tf_op jit(solution)/shard_map/ppermute | solution.py:158
  44.6 22.5 %collective-permute-start.10 = (bf16[4,128,128]{2,1,0:T(8,128)(2,1)S(1)}, bf16[4,128,128]{2,1,0:T(8,128)(2,1)S(1)}, u32[]{:S(2)}, u32[]{:S(2)}) collective-permute-start(bf16[4,128,128]{2,1,0:T(8,128)(2,1)S(1)} %get-tuple-element.56), channel_id=1, source_target_pairs={{0,12},{4,8},{8,4},{12,0},{1,13},{5,9},{9,5},{13,1},{2,14},{6,10},... | collective-permute-start | bytes 393224 | tf_op jit(solution)/shard_map/ppermute | solution.py:158
  49.2 19.2 %collective-permute-start.11 = (bf16[4,128,128]{2,1,0:T(8,128)(2,1)S(1)}, bf16[4,128,128]{2,1,0:T(8,128)(2,1)S(1)}, u32[]{:S(2)}, u32[]{:S(2)}) collective-permute-start(bf16[4,128,128]{2,1,0:T(8,128)(2,1)S(1)} %get-tuple-element.57), channel_id=1, source_target_pairs={{0,4},{4,0},{8,12},{12,8},{1,5},{5,1},{9,13},{13,9},{2,6},{6,2},{1... | collective-permute-start | bytes 393224 | tf_op jit(solution)/shard_map/ppermute | solution.py:158
  55.8 13.2 %collective-permute-start.15 = (bf16[4,128,128]{2,1,0:T(8,128)(2,1)S(1)}, bf16[4,128,128]{2,1,0:T(8,128)(2,1)S(1)}, u32[]{:S(2)}, u32[]{:S(2)}) collective-permute-start(bf16[4,128,128]{2,1,0:T(8,128)(2,1)S(1)} %get-tuple-element.63), channel_id=1, source_target_pairs={{0,8},{4,12},{8,0},{12,4},{1,9},{5,13},{9,1},{13,5},{2,10},{6,14},... | collective-permute-start | bytes 393224 | tf_op jit(solution)/shard_map/ppermute | solution.py:158
  55.8 22.5 %collective-permute-start.16 = (bf16[4,128,128]{2,1,0:T(8,128)(2,1)S(1)}, bf16[4,128,128]{2,1,0:T(8,128)(2,1)S(1)}, u32[]{:S(2)}, u32[]{:S(2)}) collective-permute-start(bf16[4,128,128]{2,1,0:T(8,128)(2,1)S(1)} %get-tuple-element.64), channel_id=1, source_target_pairs={{0,12},{4,8},{8,4},{12,0},{1,13},{5,9},{9,5},{13,1},{2,14},{6,10},... | collective-permute-start | bytes 393224 | tf_op jit(solution)/shard_map/ppermute | solution.py:158
  59.8 18.5 %collective-permute-start.17 = (bf16[4,128,128]{2,1,0:T(8,128)(2,1)S(1)}, bf16[4,128,128]{2,1,0:T(8,128)(2,1)S(1)}, u32[]{:S(2)}, u32[]{:S(2)}) collective-permute-start(bf16[4,128,128]{2,1,0:T(8,128)(2,1)S(1)} %get-tuple-element.65), channel_id=1, source_target_pairs={{0,4},{4,0},{8,12},{12,8},{1,5},{5,1},{9,13},{13,9},{2,6},{6,2},{1... | collective-permute-start | bytes 393224 | tf_op jit(solution)/shard_map/ppermute | solution.py:158
  67.1 15.2 %collective-permute-start.21 = (bf16[4,128,128]{2,1,0:T(8,128)(2,1)S(1)}, bf16[4,128,128]{2,1,0:T(8,128)(2,1)S(1)}, u32[]{:S(2)}, u32[]{:S(2)}) collective-permute-start(bf16[4,128,128]{2,1,0:T(8,128)(2,1)S(1)} %get-tuple-element.71), channel_id=1, source_target_pairs={{0,8},{4,12},{8,0},{12,4},{1,9},{5,13},{9,1},{13,5},{2,10},{6,14},... | collective-permute-start | bytes 393224 | tf_op jit(solution)/shard_map/ppermute | solution.py:158
  68.4 21.1 %collective-permute-start.22 = (bf16[4,128,128]{2,1,0:T(8,128)(2,1)S(1)}, bf16[4,128,128]{2,1,0:T(8,128)(2,1)S(1)}, u32[]{:S(2)}, u32[]{:S(2)}) collective-permute-start(bf16[4,128,128]{2,1,0:T(8,128)(2,1)S(1)} %get-tuple-element.72), channel_id=1, source_target_pairs={{0,12},{4,8},{8,4},{12,0},{1,13},{5,9},{9,5},{13,1},{2,14},{6,10},... | collective-permute-start | bytes 393224 | tf_op jit(solution)/shard_map/ppermute | solution.py:158
  69.0 20.5 %collective-permute-start.23 = (bf16[4,128,128]{2,1,0:T(8,128)(2,1)S(1)}, bf16[4,128,128]{2,1,0:T(8,128)(2,1)S(1)}, u32[]{:S(2)}, u32[]{:S(2)}) collective-permute-start(bf16[4,128,128]{2,1,0:T(8,128)(2,1)S(1)} %get-tuple-element.73), channel_id=1, source_target_pairs={{0,4},{4,0},{8,12},{12,8},{1,5},{5,1},{9,13},{13,9},{2,6},{6,2},{1... | collective-permute-start | bytes 393224 | tf_op jit(solution)/shard_map/ppermute | solution.py:158
  78.3 12.7 %collective-permute-start.3 = (bf16[4,128,128]{2,1,0:T(8,128)(2,1)S(1)}, bf16[4,128,128]{2,1,0:T(8,128)(2,1)S(1)}, u32[]{:S(2)}, u32[]{:S(2)}) collective-permute-start(bf16[4,128,128]{2,1,0:T(8,128)(2,1)S(1)} %get-tuple-element.48), channel_id=1, source_target_pairs={{0,8},{4,12},{8,0},{12,4},{1,9},{5,13},{9,1},{13,5},{2,10},{6,14},... | collective-permute-start | bytes 393224 | tf_op jit(solution)/shard_map/ppermute | solution.py:158
  78.3 15.7 %collective-permute-start.4 = (bf16[4,128,128]{2,1,0:T(8,128)(2,1)S(1)}, bf16[4,128,128]{2,1,0:T(8,128)(2,1)S(1)}, u32[]{:S(2)}, u32[]{:S(2)}) collective-permute-start(bf16[4,128,128]{2,1,0:T(8,128)(2,1)S(1)} %get-tuple-element.49), channel_id=1, source_target_pairs={{0,12},{4,8},{8,4},{12,0},{1,13},{5,9},{9,5},{13,1},{2,14},{6,10},... | collective-permute-start | bytes 393224 | tf_op jit(solution)/shard_map/ppermute | solution.py:158
  82.3 11.7 %collective-permute-start.5 = (bf16[4,128,128]{2,1,0:T(8,128)(2,1)S(1)}, bf16[4,128,128]{2,1,0:T(8,128)(2,1)S(1)}, u32[]{:S(2)}, u32[]{:S(2)}) collective-permute-start(bf16[4,128,128]{2,1,0:T(8,128)(2,1)S(1)} %get-tuple-element.50), channel_id=1, source_target_pairs={{0,4},{4,0},{8,12},{12,8},{1,5},{5,1},{9,13},{13,9},{2,6},{6,2},{1... | collective-permute-start | bytes 393224 | tf_op jit(solution)/shard_map/ppermute | solution.py:158

commit v6 on v5

--- a/solution.py
+++ b/solution.py
@@ -173,8 +173,10 @@
     order_out = [*range(2, ranks), 1, 0]
     slots = [(head, step) for head in range(heads) for step in steps]
     early = [(0, step) for step in steps if step > 1]
-    pieces = pack(early)
-    pieces.update(pack([slot for slot in slots if slot not in early]))
+    pieces = {}
+    for wanted in (early[:1], early[1:], [slot for slot in slots if slot not in early]):
+        if wanted:
+            pieces.update(pack(wanted))
     got = {
         slot: permute(pieces[slot], slot[1]) if slot[1] else pieces[slot] for slot in slots
     }
@@ -201,7 +203,7 @@
         pltpu.SemaphoreType.DMA((4,)),
     ]
     done = [(head, step) for head in range(heads) for step in order_out]
-    last = [slot for slot in done if slot[0] == heads - 1 and slot[1]]
+    last = [slot for slot in done if slot[0] == heads - 1 and slot[1] >= min(2, ranks - 1)]
     outs = []
     if len(last) < len(done):
         outs = unpack(rows_kernel, [slot for slot in done if slot not in last], rows, outs)

time: 95.8 us -> 95.3 us (level)
  starting transfers between devices: 48 us -> 29.7 us
  waiting for transfers between devices: 33 us -> 50.4 us
    ppermute x24, starting transfers between devices: 48 us -> 29.7 us  [permute(): return lax.ppermute(x, 'ctx', [(j, j ^ step) for j in range(ranks)])]
    ppermute x24, waiting for transfers between devices: 33 us -> 50.4 us  [permute(): return lax.ppermute(x, 'ctx', [(j, j ^ step) for j in range(ranks)])]
    pallas_call x2 -> x3, Pallas kernels: 2.9 us -> 3.63 us  [pack(): pl.pallas_call(functools.partial(pack_kernel, ranks=ranks, wanted=wanted)...]
  transfers between devices with their start and end apart: 24 -> 24, of which waited for: 13 -> 11; matrix products, arithmetic and copies ran while one was open for 1% -> 1% of each run, Pallas kernels for 9% -> 10%
where the time goes in v6:
time: 95.3 us; the launch traced here: 94.7 us
  waiting for transfers between devices  50.4 us (53%)
  starting transfers between devices  29.7 us (31%)
  Pallas kernels  11.3 us (12%)
  local copies, waits for them, and re-layouts  2.18 us (2%)
    ppermute x24, waiting for transfers between devices, permute(): return lax.ppermute(x, 'ctx', [(j, j ^ step) for j in range(ranks)])  50.4 us
    ppermute x24, starting transfers between devices, permute(): return lax.ppermute(x, 'ctx', [(j, j ^ step) for j in range(ranks)])  29.7 us
    pallas_call x4, Pallas kernels, attend(): pl.pallas_call(functools.partial(attention_kernel, ranks=ranks, tokens=to...  5.41 us
    pallas_call x3, Pallas kernels, pack(): pl.pallas_call(functools.partial(pack_kernel, ranks=ranks, wanted=wanted)...  3.63 us
    pallas_call x2, Pallas kernels, unpack(): pl.pallas_call(functools.partial(kernel, ranks=ranks, wanted=wanted), out...  2.23 us
  transfers between devices with their start and end apart: 24, of which 11 were waited for; matrix products, arithmetic and copies ran while one was open for 1% of the time, Pallas kernels for 10%

profile of v6, /device:TPU:18, one launch (start us, length us, event | category | flops | bytes accessed | tf_op | source)
XLA Modules:
  0.0 94.7 jit_solution(3744726936904112988)
XLA Ops:
  0.6 0.8 shard_map.95
  1.5 0.5 collective-permute-start.6
  2.0 0.8 shard_map.96
  2.9 3.6 %collective-permute-start.7 = (bf16[4,128,128]{2,1,0:T(8,128)(2,1)S(1)}, bf16[4,128,128]{2,1,0:T(8,128)(2,1)S(1)}, u32[]{:S(2)}, u32[]{:S(2)}) collective-permute-start(bf16[4,128,128]{2,1,0:T(8,128)(2,1)S(1)} %shard_map.96), channel_id=1, source_target_pairs={{0,8},{4,12},{8,0},{12,4},{1,9},{5,13},{9,1},{13,5},{2,10},{6,14},... | collective-permute-start | bytes 393224 | tf_op jit(solution)/shard_map/ppermute | solution.py:158
  6.4 1.9 %shard_map.93 = (bf16[4,128,128]{2,1,0:T(8,128)(2,1)S(1)}, bf16[4,128,128]{2,1,0:T(8,128)(2,1)S(1)}, bf16[4,128,128]{2,1,0:T(8,128)(2,1)S(1)}, bf16[4,128,128]{2...) custom-call(s32[1]{0:T(128)} %bitcast.me_ref, ...), custom_call_target="tpu_custom_call" | custom-call | tf_op jit(solution)/shard_map/pallas_call | solution.py:147
  8.4 0.1 collective-permute-start
  8.5 1.0 %collective-permute-start.1 = (bf16[4,128,128]{2,1,0:T(8,128)(2,1)S(1)}, bf16[4,128,128]{2,1,0:T(8,128)(2,1)S(1)}, u32[]{:S(2)}, u32[]{:S(2)}) collective-permute-start(bf16[4,128,128]{2,1,0:T(8,128)(2,1)S(1)} %get-tuple-element.43), channel_id=1, source_target_pairs={{0,12},{4,8},{8,4},{12,0},{1,13},{5,9},{9,5},{13,1},{2,14},{6,10},... | collective-permute-start | bytes 393224 | tf_op jit(solution)/shard_map/ppermute | solution.py:158
  9.4 3.4 %collective-permute-start.2 = (bf16[4,128,128]{2,1,0:T(8,128)(2,1)S(1)}, bf16[4,128,128]{2,1,0:T(8,128)(2,1)S(1)}, u32[]{:S(2)}, u32[]{:S(2)}) collective-permute-start(bf16[4,128,128]{2,1,0:T(8,128)(2,1)S(1)} %get-tuple-element.44), channel_id=1, source_target_pairs={{0,4},{4,0},{8,12},{12,8},{1,5},{5,1},{9,13},{13,9},{2,6},{6,2},{1... | collective-permute-start | bytes 393224 | tf_op jit(solution)/shard_map/ppermute | solution.py:158
  12.8 0.0 copy-start
  12.9 0.7 copy-done
  13.5 0.1 copy.17
  13.6 0.6 gather_fusion
  14.2 0.1 broadcast_select_fusion
  14.2 0.7 copy-done.1
  14.9 0.1 compare_reduce_fusion.1
  15.0 0.1 copy.16
  15.1 0.1 compare_reduce_fusion
  15.1 3.8 %collective-permute-done.6.refs_2_ = bf16[4,128,128]{2,1,0:T(8,128)(2,1)S(1)} collective-permute-done((bf16[4,128,128]{2,1,0:T(8,128)(2,1)S(1)}, bf16[4,128,128]{2,1,0:T(8,128)(2,1)S(1)}, u32[]{:S(2)}, u32[]{:S(2)}) %collective-permute-start.6) | collective-permute-done | bytes 131104 | tf_op jit(solution)/shard_map/ppermute | solution.py:158
  18.9 0.0 collective-permute-start.5
  18.9 3.6 %collective-permute-done.refs_0_ = bf16[4,128,128]{2,1,0:T(8,128)(2,1)S(1)} collective-permute-done((bf16[4,128,128]{2,1,0:T(8,128)(2,1)S(1)}, bf16[4,128,128]{2,1,0:T(8,128)(2,1)S(1)}, u32[]{:S(2)}, u32[]{:S(2)}) %collective-permute-start) | collective-permute-done | bytes 131104 | tf_op jit(solution)/shard_map/ppermute | solution.py:158
  22.6 3.4 %collective-permute-start.11 = (bf16[4,128,128]{2,1,0:T(8,128)(2,1)S(1)}, bf16[4,128,128]{2,1,0:T(8,128)(2,1)S(1)}, u32[]{:S(2)}, u32[]{:S(2)}) collective-permute-start(bf16[4,128,128]{2,1,0:T(8,128)(2,1)S(1)} %get-tuple-element.54), channel_id=1, source_target_pairs={{0,8},{4,12},{8,0},{12,4},{1,9},{5,13},{9,1},{13,5},{2,10},{6,14},... | collective-permute-start | bytes 393224 | tf_op jit(solution)/shard_map/ppermute | solution.py:158
  26.0 7.0 %collective-permute-done.1.refs_1_ = bf16[4,128,128]{2,1,0:T(8,128)(2,1)S(1)} collective-permute-done((bf16[4,128,128]{2,1,0:T(8,128)(2,1)S(1)}, bf16[4,128,128]{2,1,0:T(8,128)(2,1)S(1)}, u32[]{:S(2)}, u32[]{:S(2)}) %collective-permute-start.1) | collective-permute-done | bytes 131104 | tf_op jit(solution)/shard_map/ppermute | solution.py:158
  33.0 0.1 or_select_fusion
  33.1 0.1 broadcast_in_dim.38
  33.2 0.1 reshape.148.bias_ref
  33.2 1.4 %shard_map.94 = (bf16[4,128,128]{2,1,0:T(8,128)(2,1)S(1)}, bf16[4,128,128]{2,1,0:T(8,128)(2,1)S(1)}, bf16[4,128,128]{2,1,0:T(8,128)(2,1)S(1)}, bf16[4,128,128]{2,1,0:T(8,128)(2,1)S(1)}) custom-call(f32[8,512]{1,0:T(8,128)S(1)} %reshape.148.bias_ref, bf16[4,128,128]{2,1,0:T(8,128)(2,1)S(1)} %collective-permute-done.refs_0_, ...), custom_call_target="tpu_custom_call" | custom-call | tf_op jit(solution)/shard_map/pallas_call | solution.py:161
  34.6 3.5 %collective-permute-start.17 = (bf16[4,128,128]{2,1,0:T(8,128)(2,1)S(1)}, bf16[4,128,128]{2,1,0:T(8,128)(2,1)S(1)}, u32[]{:S(2)}, u32[]{:S(2)}) collective-permute-start(bf16[4,128,128]{2,1,0:T(8,128)(2,1)S(1)} %get-tuple-element.62), channel_id=1, source_target_pairs={{0,8},{4,12},{8,0},{12,4},{1,9},{5,13},{9,1},{13,5},{2,10},{6,14},... | collective-permute-start | bytes 393224 | tf_op jit(solution)/shard_map/ppermute | solution.py:158
  38.1 0.0 collective-permute-start.18
  38.2 1.9 %collective-permute-start.19 = (bf16[4,128,128]{2,1,0:T(8,128)(2,1)S(1)}, bf16[4,128,128]{2,1,0:T(8,128)(2,1)S(1)}, u32[]{:S(2)}, u32[]{:S(2)}) collective-permute-start(bf16[4,128,128]{2,1,0:T(8,128)(2,1)S(1)} %get-tuple-element.64), channel_id=1, source_target_pairs={{0,4},{4,0},{8,12},{12,8},{1,5},{5,1},{9,13},{13,9},{2,6},{6,2},{1... | collective-permute-start | bytes 393224 | tf_op jit(solution)/shard_map/ppermute | solution.py:158
  40.1 1.4 %shard_map.97 = (bf16[4,128,128]{2,1,0:T(8,128)(2,1)S(1)}, bf16[4,128,128]{2,1,0:T(8,128)(2,1)S(1)}, bf16[4,128,128]{2,1,0:T(8,128)(2,1)S(1)}, bf16[4,128,128]{2,1,0:T(8,128)(2,1)S(1)}) custom-call(f32[8,512]{1,0:T(8,128)S(1)} %reshape.148.bias_ref, bf16[4,128,128]{2,1,0:T(8,128)(2,1)S(1)} %get-tuple-element.48.refs_0_, ...), custom_call_target="tpu_custom_call" | custom-call | tf_op jit(solution)/shard_map/pallas_call | solution.py:161
  41.4 2.3 %collective-permute-done.12.refs_1_ = bf16[4,128,128]{2,1,0:T(8,128)(2,1)S(1)} collective-permute-done((bf16[4,128,128]{2,1,0:T(8,128)(2,1)S(1)}, bf16[4,128,128]{2,1,0:T(8,128)(2,1)S(1)}, u32[]{:S(2)}, u32[]{:S(2)}) %collective-permute-start.12) | collective-permute-done | bytes 131104 | tf_op jit(solution)/shard_map/ppermute | solution.py:158
  43.7 0.3 collective-permute-start.8
  44.0 1.4 %shard_map.98 = (bf16[4,128,128]{2,1,0:T(8,128)(2,1)S(1)}, bf16[4,128,128]{2,1,0:T(8,128)(2,1)S(1)}, bf16[4,128,128]{2,1,0:T(8,128)(2,1)S(1)}, bf16[4,128,128]{2,1,0:T(8,128)(2,1)S(1)}) custom-call(f32[8,512]{1,0:T(8,128)S(1)} %reshape.148.bias_ref, bf16[4,128,128]{2,1,0:T(8,128)(2,1)S(1)} %collective-permute-done.11.refs_0_, ...), custom_call_target="tpu_custom_call" | custom-call | tf_op jit(solution)/shard_map/pallas_call | solution.py:161
  45.3 3.3 %collective-permute-start.9 = (bf16[4,128,128]{2,1,0:T(8,128)(2,1)S(1)}, bf16[4,128,128]{2,1,0:T(8,128)(2,1)S(1)}, u32[]{:S(2)}, u32[]{:S(2)}) collective-permute-start(bf16[4,128,128]{2,1,0:T(8,128)(2,1)S(1)} %get-tuple-element.51), channel_id=1, source_target_pairs={{0,12},{4,8},{8,4},{12,0},{1,13},{5,9},{9,5},{13,1},{2,14},{6,10},... | collective-permute-start | bytes 393224 | tf_op jit(solution)/shard_map/ppermute | solution.py:158
  48.6 9.7 %collective-permute-done.18.refs_1_ = bf16[4,128,128]{2,1,0:T(8,128)(2,1)S(1)} collective-permute-done((bf16[4,128,128]{2,1,0:T(8,128)(2,1)S(1)}, bf16[4,128,128]{2,1,0:T(8,128)(2,1)S(1)}, u32[]{:S(2)}, u32[]{:S(2)}) %collective-permute-start.18) | collective-permute-done | bytes 131104 | tf_op jit(solution)/shard_map/ppermute | solution.py:158
  58.3 3.5 %collective-permute-start.15 = (bf16[4,128,128]{2,1,0:T(8,128)(2,1)S(1)}, bf16[4,128,128]{2,1,0:T(8,128)(2,1)S(1)}, u32[]{:S(2)}, u32[]{:S(2)}) collective-permute-start(bf16[4,128,128]{2,1,0:T(8,128)(2,1)S(1)} %get-tuple-element.59), channel_id=1, source_target_pairs={{0,12},{4,8},{8,4},{12,0},{1,13},{5,9},{9,5},{13,1},{2,14},{6,10},... | collective-permute-start | bytes 393224 | tf_op jit(solution)/shard_map/ppermute | solution.py:158
  61.8 0.9 collective-permute-start.16
  62.7 1.4 %shard_map.99 = (bf16[4,128,128]{2,1,0:T(8,128)(2,1)S(1)}, bf16[4,128,128]{2,1,0:T(8,128)(2,1)S(1)}, bf16[4,128,128]{2,1,0:T(8,128)(2,1)S(1)}, bf16[4,128,128]{2,1,0:T(8,128)(2,1)S(1)}) custom-call(f32[8,512]{1,0:T(8,128)S(1)} %reshape.148.bias_ref, bf16[4,128,128]{2,1,0:T(8,128)(2,1)S(1)} %collective-permute-done.17.refs_0_, ...), custom_call_target="tpu_custom_call" | custom-call | tf_op jit(solution)/shard_map/pallas_call | solution.py:161
  64.0 3.6 %collective-permute-done.9.refs_1_ = bf16[4,128,128]{2,1,0:T(8,128)(2,1)S(1)} collective-permute-done((bf16[4,128,128]{2,1,0:T(8,128)(2,1)S(1)}, bf16[4,128,128]{2,1,0:T(8,128)(2,1)S(1)}, u32[]{:S(2)}, u32[]{:S(2)}) %collective-permute-start.9) | collective-permute-done | bytes 131104 | tf_op jit(solution)/shard_map/ppermute | solution.py:158
  67.7 1.9 %collective-permute-done.14.refs_4_ = bf16[4,128,128]{2,1,0:T(8,128)(2,1)S(1)} collective-permute-done((bf16[4,128,128]{2,1,0:T(8,128)(2,1)S(1)}, bf16[4,128,128]{2,1,0:T(8,128)(2,1)S(1)}, u32[]{:S(2)}, u32[]{:S(2)}) %collective-permute-start.14) | collective-permute-done | bytes 131104 | tf_op jit(solution)/shard_map/ppermute | solution.py:158
  69.6 4.3 %collective-permute-start.22 = (bf16[4,128,128]{2,1,0:T(8,128)(2,1)S(1)}, bf16[4,128,128]{2,1,0:T(8,128)(2,1)S(1)}, u32[]{:S(2)}, u32[]{:S(2)}) collective-permute-start(bf16[4,128,128]{2,1,0:T(8,128)(2,1)S(1)} %get-tuple-element.68), channel_id=1, source_target_pairs={{0,4},{4,0},{8,12},{12,8},{1,5},{5,1},{9,13},{13,9},{2,6},{6,2},{1... | collective-permute-start | bytes 393224 | tf_op jit(solution)/shard_map/ppermute | solution.py:158
  73.9 4.0 %collective-permute-done.15.refs_5_ = bf16[4,128,128]{2,1,0:T(8,128)(2,1)S(1)} collective-permute-done((bf16[4,128,128]{2,1,0:T(8,128)(2,1)S(1)}, bf16[4,128,128]{2,1,0:T(8,128)(2,1)S(1)}, u32[]{:S(2)}, u32[]{:S(2)}) %collective-permute-start.15) | collective-permute-done | bytes 131104 | tf_op jit(solution)/shard_map/ppermute | solution.py:158
  78.0 0.1 collective-permute-start.4
  78.1 1.7 %collective-permute-done.20.refs_8_ = bf16[4,128,128]{2,1,0:T(8,128)(2,1)S(1)} collective-permute-done((bf16[4,128,128]{2,1,0:T(8,128)(2,1)S(1)}, bf16[4,128,128]{2,1,0:T(8,128)(2,1)S(1)}, u32[]{:S(2)}, u32[]{:S(2)}) %collective-permute-start.20) | collective-permute-done | bytes 131104 | tf_op jit(solution)/shard_map/ppermute | solution.py:158
  79.8 9.4 %collective-permute-done.21.refs_9_ = bf16[4,128,128]{2,1,0:T(8,128)(2,1)S(1)} collective-permute-done((bf16[4,128,128]{2,1,0:T(8,128)(2,1)S(1)}, bf16[4,128,128]{2,1,0:T(8,128)(2,1)S(1)}, u32[]{:S(2)}, u32[]{:S(2)}) %collective-permute-start.21) | collective-permute-done | bytes 131104 | tf_op jit(solution)/shard_map/ppermute | solution.py:158
  89.2 1.5 %shard_map.100 = (bf16[128,2048]{1,0:T(8,128)(2,1)}, bf16[128,2048]{1,0:T(8,128)(2,1)}, bf16[128,2048]{1,0:T(8,128)(2,1)}, bf16[128,2048]{1,0:T(8,128)(2,1)}) custom-call(s32[1]{0:T(128)} %bitcast.me_ref, bf16[4,128,128]{2,1,0:T(8,128)(2,1)S(1)} %collective-permute-done.8.refs_0_, bf16[4,128,128]{2,1,0:T(8,128)(2,1)S(1)} %collective-permute-done.9.refs_1_, ...), custom_call_target="tpu_custom_call" | custom-call | tf_op jit(solution)/shard_map/pallas_call | solution.py:191
  90.7 3.2 %collective-permute-done.4.refs_1_ = bf16[4,128,128]{2,1,0:T(8,128)(2,1)S(1)} collective-permute-done((bf16[4,128,128]{2,1,0:T(8,128)(2,1)S(1)}, bf16[4,128,128]{2,1,0:T(8,128)(2,1)S(1)}, u32[]{:S(2)}, u32[]{:S(2)}) %collective-permute-start.4) | collective-permute-done | bytes 131104 | tf_op jit(solution)/shard_map/ppermute | solution.py:158
  94.0 0.8 shard_map.101
  (26 shorter events, 0.1 us)
Async XLA Ops:
  1.5 17.4 %collective-permute-start.6 = (bf16[4,128,128]{2,1,0:T(8,128)(2,1)S(1)}, bf16[4,128,128]{2,1,0:T(8,128)(2,1)S(1)}, u32[]{:S(2)}, u32[]{:S(2)}) collective-permute-start(bf16[4,128,128]{2,1,0:T(8,128)(2,1)S(1)} %shard_map.95), channel_id=1, source_target_pairs={{0,12},{4,8},{8,4},{12,0},{1,13},{5,9},{9,5},{13,1},{2,14},{6,10},... | collective-permute-start | bytes 393224 | tf_op jit(solution)/shard_map/ppermute | solution.py:158
  2.9 31.7 %collective-permute-start.7 = (bf16[4,128,128]{2,1,0:T(8,128)(2,1)S(1)}, bf16[4,128,128]{2,1,0:T(8,128)(2,1)S(1)}, u32[]{:S(2)}, u32[]{:S(2)}) collective-permute-start(bf16[4,128,128]{2,1,0:T(8,128)(2,1)S(1)} %shard_map.96), channel_id=1, source_target_pairs={{0,8},{4,12},{8,0},{12,4},{1,9},{5,13},{9,1},{13,5},{2,10},{6,14},... | collective-permute-start | bytes 393224 | tf_op jit(solution)/shard_map/ppermute | solution.py:158
  8.4 14.2 %collective-permute-start = (bf16[4,128,128]{2,1,0:T(8,128)(2,1)S(1)}, bf16[4,128,128]{2,1,0:T(8,128)(2,1)S(1)}, u32[]{:S(2)}, u32[]{:S(2)}) collective-permute-start(bf16[4,128,128]{2,1,0:T(8,128)(2,1)S(1)} %get-tuple-element.42), channel_id=1, source_target_pairs={{0,8},{4,12},{8,0},{12,4},{1,9},{5,13},{9,1},{13,5},{2,10},{6,14},... | collective-permute-start | bytes 393224 | tf_op jit(solution)/shard_map/ppermute | solution.py:158
  8.5 24.5 %collective-permute-start.1 = (bf16[4,128,128]{2,1,0:T(8,128)(2,1)S(1)}, bf16[4,128,128]{2,1,0:T(8,128)(2,1)S(1)}, u32[]{:S(2)}, u32[]{:S(2)}) collective-permute-start(bf16[4,128,128]{2,1,0:T(8,128)(2,1)S(1)} %get-tuple-element.43), channel_id=1, source_target_pairs={{0,12},{4,8},{8,4},{12,0},{1,13},{5,9},{9,5},{13,1},{2,14},{6,10},... | collective-permute-start | bytes 393224 | tf_op jit(solution)/shard_map/ppermute | solution.py:158
  9.4 23.5 %collective-permute-start.2 = (bf16[4,128,128]{2,1,0:T(8,128)(2,1)S(1)}, bf16[4,128,128]{2,1,0:T(8,128)(2,1)S(1)}, u32[]{:S(2)}, u32[]{:S(2)}) collective-permute-start(bf16[4,128,128]{2,1,0:T(8,128)(2,1)S(1)} %get-tuple-element.44), channel_id=1, source_target_pairs={{0,4},{4,0},{8,12},{12,8},{1,5},{5,1},{9,13},{13,9},{2,6},{6,2},{1... | collective-permute-start | bytes 393224 | tf_op jit(solution)/shard_map/ppermute | solution.py:158
  12.8 0.7 copy-start
  14.2 0.7 copy-start.1
  18.9 19.2 %collective-permute-start.5 = (bf16[4,128,128]{2,1,0:T(8,128)(2,1)S(1)}, bf16[4,128,128]{2,1,0:T(8,128)(2,1)S(1)}, u32[]{:S(2)}, u32[]{:S(2)}) collective-permute-start(bf16[4,128,128]{2,1,0:T(8,128)(2,1)S(1)} %get-tuple-element.49), channel_id=1, source_target_pairs={{0,4},{4,0},{8,12},{12,8},{1,5},{5,1},{9,13},{13,9},{2,6},{6,2},{1... | collective-permute-start | bytes 393224 | tf_op jit(solution)/shard_map/ppermute | solution.py:158
  22.6 15.6 %collective-permute-start.11 = (bf16[4,128,128]{2,1,0:T(8,128)(2,1)S(1)}, bf16[4,128,128]{2,1,0:T(8,128)(2,1)S(1)}, u32[]{:S(2)}, u32[]{:S(2)}) collective-permute-start(bf16[4,128,128]{2,1,0:T(8,128)(2,1)S(1)} %get-tuple-element.54), channel_id=1, source_target_pairs={{0,8},{4,12},{8,0},{12,4},{1,9},{5,13},{9,1},{13,5},{2,10},{6,14},... | collective-permute-start | bytes 393224 | tf_op jit(solution)/shard_map/ppermute | solution.py:158
  33.0 10.7 %collective-permute-start.12 = (bf16[4,128,128]{2,1,0:T(8,128)(2,1)S(1)}, bf16[4,128,128]{2,1,0:T(8,128)(2,1)S(1)}, u32[]{:S(2)}, u32[]{:S(2)}) collective-permute-start(bf16[4,128,128]{2,1,0:T(8,128)(2,1)S(1)} %get-tuple-element.55), channel_id=1, source_target_pairs={{0,12},{4,8},{8,4},{12,0},{1,13},{5,9},{9,5},{13,1},{2,14},{6,10},... | collective-permute-start | bytes 393224 | tf_op jit(solution)/shard_map/ppermute | solution.py:158
  33.0 10.7 %collective-permute-start.13 = (bf16[4,128,128]{2,1,0:T(8,128)(2,1)S(1)}, bf16[4,128,128]{2,1,0:T(8,128)(2,1)S(1)}, u32[]{:S(2)}, u32[]{:S(2)}) collective-permute-start(bf16[4,128,128]{2,1,0:T(8,128)(2,1)S(1)} %get-tuple-element.56), channel_id=1, source_target_pairs={{0,4},{4,0},{8,12},{12,8},{1,5},{5,1},{9,13},{13,9},{2,6},{6,2},{1... | collective-permute-start | bytes 393224 | tf_op jit(solution)/shard_map/ppermute | solution.py:158
  34.6 10.7 %collective-permute-start.17 = (bf16[4,128,128]{2,1,0:T(8,128)(2,1)S(1)}, bf16[4,128,128]{2,1,0:T(8,128)(2,1)S(1)}, u32[]{:S(2)}, u32[]{:S(2)}) collective-permute-start(bf16[4,128,128]{2,1,0:T(8,128)(2,1)S(1)} %get-tuple-element.62), channel_id=1, source_target_pairs={{0,8},{4,12},{8,0},{12,4},{1,9},{5,13},{9,1},{13,5},{2,10},{6,14},... | collective-permute-start | bytes 393224 | tf_op jit(solution)/shard_map/ppermute | solution.py:158
  38.1 20.1 %collective-permute-start.18 = (bf16[4,128,128]{2,1,0:T(8,128)(2,1)S(1)}, bf16[4,128,128]{2,1,0:T(8,128)(2,1)S(1)}, u32[]{:S(2)}, u32[]{:S(2)}) collective-permute-start(bf16[4,128,128]{2,1,0:T(8,128)(2,1)S(1)} %get-tuple-element.63), channel_id=1, source_target_pairs={{0,12},{4,8},{8,4},{12,0},{1,13},{5,9},{9,5},{13,1},{2,14},{6,10},... | collective-permute-start | bytes 393224 | tf_op jit(solution)/shard_map/ppermute | solution.py:158
  38.2 20.1 %collective-permute-start.19 = (bf16[4,128,128]{2,1,0:T(8,128)(2,1)S(1)}, bf16[4,128,128]{2,1,0:T(8,128)(2,1)S(1)}, u32[]{:S(2)}, u32[]{:S(2)}) collective-permute-start(bf16[4,128,128]{2,1,0:T(8,128)(2,1)S(1)} %get-tuple-element.64), channel_id=1, source_target_pairs={{0,4},{4,0},{8,12},{12,8},{1,5},{5,1},{9,13},{13,9},{2,6},{6,2},{1... | collective-permute-start | bytes 393224 | tf_op jit(solution)/shard_map/ppermute | solution.py:158
  43.7 14.6 %collective-permute-start.23 = (bf16[4,128,128]{2,1,0:T(8,128)(2,1)S(1)}, bf16[4,128,128]{2,1,0:T(8,128)(2,1)S(1)}, u32[]{:S(2)}, u32[]{:S(2)}) collective-permute-start(bf16[4,128,128]{2,1,0:T(8,128)(2,1)S(1)} %get-tuple-element.70), channel_id=1, source_target_pairs={{0,4},{4,0},{8,12},{12,8},{1,5},{5,1},{9,13},{13,9},{2,6},{6,2},{1... | collective-permute-start | bytes 393224 | tf_op jit(solution)/shard_map/ppermute | solution.py:158
  43.7 18.1 %collective-permute-start.8 = (bf16[4,128,128]{2,1,0:T(8,128)(2,1)S(1)}, bf16[4,128,128]{2,1,0:T(8,128)(2,1)S(1)}, u32[]{:S(2)}, u32[]{:S(2)}) collective-permute-start(bf16[4,128,128]{2,1,0:T(8,128)(2,1)S(1)} %get-tuple-element.50), channel_id=1, source_target_pairs={{0,8},{4,12},{8,0},{12,4},{1,9},{5,13},{9,1},{13,5},{2,10},{6,14},... | collective-permute-start | bytes 393224 | tf_op jit(solution)/shard_map/ppermute | solution.py:158
  45.3 22.3 %collective-permute-start.9 = (bf16[4,128,128]{2,1,0:T(8,128)(2,1)S(1)}, bf16[4,128,128]{2,1,0:T(8,128)(2,1)S(1)}, u32[]{:S(2)}, u32[]{:S(2)}) collective-permute-start(bf16[4,128,128]{2,1,0:T(8,128)(2,1)S(1)} %get-tuple-element.51), channel_id=1, source_target_pairs={{0,12},{4,8},{8,4},{12,0},{1,13},{5,9},{9,5},{13,1},{2,14},{6,10},... | collective-permute-start | bytes 393224 | tf_op jit(solution)/shard_map/ppermute | solution.py:158
  58.3 9.4 %collective-permute-start.10 = (bf16[4,128,128]{2,1,0:T(8,128)(2,1)S(1)}, bf16[4,128,128]{2,1,0:T(8,128)(2,1)S(1)}, u32[]{:S(2)}, u32[]{:S(2)}) collective-permute-start(bf16[4,128,128]{2,1,0:T(8,128)(2,1)S(1)} %get-tuple-element.52), channel_id=1, source_target_pairs={{0,4},{4,0},{8,12},{12,8},{1,5},{5,1},{9,13},{13,9},{2,6},{6,2},{1... | collective-permute-start | bytes 393224 | tf_op jit(solution)/shard_map/ppermute | solution.py:158
  58.3 11.3 %collective-permute-start.14 = (bf16[4,128,128]{2,1,0:T(8,128)(2,1)S(1)}, bf16[4,128,128]{2,1,0:T(8,128)(2,1)S(1)}, u32[]{:S(2)}, u32[]{:S(2)}) collective-permute-start(bf16[4,128,128]{2,1,0:T(8,128)(2,1)S(1)} %get-tuple-element.58), channel_id=1, source_target_pairs={{0,8},{4,12},{8,0},{12,4},{1,9},{5,13},{9,1},{13,5},{2,10},{6,14},... | collective-permute-start | bytes 393224 | tf_op jit(solution)/shard_map/ppermute | solution.py:158
  58.3 19.7 %collective-permute-start.15 = (bf16[4,128,128]{2,1,0:T(8,128)(2,1)S(1)}, bf16[4,128,128]{2,1,0:T(8,128)(2,1)S(1)}, u32[]{:S(2)}, u32[]{:S(2)}) collective-permute-start(bf16[4,128,128]{2,1,0:T(8,128)(2,1)S(1)} %get-tuple-element.59), channel_id=1, source_target_pairs={{0,12},{4,8},{8,4},{12,0},{1,13},{5,9},{9,5},{13,1},{2,14},{6,10},... | collective-permute-start | bytes 393224 | tf_op jit(solution)/shard_map/ppermute | solution.py:158
  61.8 16.2 %collective-permute-start.16 = (bf16[4,128,128]{2,1,0:T(8,128)(2,1)S(1)}, bf16[4,128,128]{2,1,0:T(8,128)(2,1)S(1)}, u32[]{:S(2)}, u32[]{:S(2)}) collective-permute-start(bf16[4,128,128]{2,1,0:T(8,128)(2,1)S(1)} %get-tuple-element.60), channel_id=1, source_target_pairs={{0,4},{4,0},{8,12},{12,8},{1,5},{5,1},{9,13},{13,9},{2,6},{6,2},{1... | collective-permute-start | bytes 393224 | tf_op jit(solution)/shard_map/ppermute | solution.py:158
  67.7 12.1 %collective-permute-start.20 = (bf16[4,128,128]{2,1,0:T(8,128)(2,1)S(1)}, bf16[4,128,128]{2,1,0:T(8,128)(2,1)S(1)}, u32[]{:S(2)}, u32[]{:S(2)}) collective-permute-start(bf16[4,128,128]{2,1,0:T(8,128)(2,1)S(1)} %get-tuple-element.66), channel_id=1, source_target_pairs={{0,8},{4,12},{8,0},{12,4},{1,9},{5,13},{9,1},{13,5},{2,10},{6,14},... | collective-permute-start | bytes 393224 | tf_op jit(solution)/shard_map/ppermute | solution.py:158
  67.7 21.6 %collective-permute-start.21 = (bf16[4,128,128]{2,1,0:T(8,128)(2,1)S(1)}, bf16[4,128,128]{2,1,0:T(8,128)(2,1)S(1)}, u32[]{:S(2)}, u32[]{:S(2)}) collective-permute-start(bf16[4,128,128]{2,1,0:T(8,128)(2,1)S(1)} %get-tuple-element.67), channel_id=1, source_target_pairs={{0,12},{4,8},{8,4},{12,0},{1,13},{5,9},{9,5},{13,1},{2,14},{6,10},... | collective-permute-start | bytes 393224 | tf_op jit(solution)/shard_map/ppermute | solution.py:158
  69.6 19.6 %collective-permute-start.22 = (bf16[4,128,128]{2,1,0:T(8,128)(2,1)S(1)}, bf16[4,128,128]{2,1,0:T(8,128)(2,1)S(1)}, u32[]{:S(2)}, u32[]{:S(2)}) collective-permute-start(bf16[4,128,128]{2,1,0:T(8,128)(2,1)S(1)} %get-tuple-element.68), channel_id=1, source_target_pairs={{0,4},{4,0},{8,12},{12,8},{1,5},{5,1},{9,13},{13,9},{2,6},{6,2},{1... | collective-permute-start | bytes 393224 | tf_op jit(solution)/shard_map/ppermute | solution.py:158
  78.0 12.8 %collective-permute-start.3 = (bf16[4,128,128]{2,1,0:T(8,128)(2,1)S(1)}, bf16[4,128,128]{2,1,0:T(8,128)(2,1)S(1)}, u32[]{:S(2)}, u32[]{:S(2)}) collective-permute-start(bf16[4,128,128]{2,1,0:T(8,128)(2,1)S(1)} %get-tuple-element.46), channel_id=1, source_target_pairs={{0,8},{4,12},{8,0},{12,4},{1,9},{5,13},{9,1},{13,5},{2,10},{6,14},... | collective-permute-start | bytes 393224 | tf_op jit(solution)/shard_map/ppermute | solution.py:158
  78.0 16.0 %collective-permute-start.4 = (bf16[4,128,128]{2,1,0:T(8,128)(2,1)S(1)}, bf16[4,128,128]{2,1,0:T(8,128)(2,1)S(1)}, u32[]{:S(2)}, u32[]{:S(2)}) collective-permute-start(bf16[4,128,128]{2,1,0:T(8,128)(2,1)S(1)} %get-tuple-element.47), channel_id=1, source_target_pairs={{0,12},{4,8},{8,4},{12,0},{1,13},{5,9},{9,5},{13,1},{2,14},{6,10},... | collective-permute-start | bytes 393224 | tf_op jit(solution)/shard_map/ppermute | solution.py:158
